TPU v7x, 256 devices: a whole 4x4x8 slice. The times are simulated.
256 devices in a mesh: dp: 8 (over z), expert: 8 (over x, core), tensor: 4 (over y).
Axes of the slice: x: 4, y: 4, z: 8, core: 2. Of those that a mesh axis runs over, the one named last changes fastest.
Arguments:
- skip_stream_entry: bfloat16 [4096, 4096], P(('dp', 'expert', 'tensor')), may hold values from -6 to 6
- question_vectors: bfloat16 [4096, 2048], P(('dp', 'expert'), 'tensor'), may hold values from -5 to 5
- fresh_lookup_vectors: bfloat16 [4096, 512], P(('dp', 'expert'), 'tensor'), may hold values from -5 to 5
- fresh_content_vectors: bfloat16 [4096, 512], P(('dp', 'expert'), 'tensor'), may hold values from -10 to 10
- stored_lookup_sheets: bfloat16 [2560, 4, 128, 128], P(('dp', 'expert'), 'tensor'), may hold values from -5 to 5
- stored_content_sheets: bfloat16 [2560, 4, 128, 128], P(('dp', 'expert'), 'tensor'), may hold values from -10 to 10
- sequence_sheet_map: int32 [1088, 8], P(('dp', 'expert')), may hold values from 0 to 39
- stored_position_counts: int32 [1088], P(('dp', 'expert')), may hold values from 2 to 1024
- attention_merge_matrix: bfloat16 [2048, 4096], P('tensor'), may hold values from -0.59765625 to 0.59765625
- premix_scale_factor: bfloat16 [4096], replicated, may hold values from 0.5 to 1.5
- chosen_specialists: int32 [4096, 2], P(('dp', 'expert', 'tensor')), may hold values from 0 to 7, all different within a row; in each aligned block of 16 rows (0 to 15, 16 to 31, ...) at most 6 rows name the same one
- selection_shares: float32 [4096, 2], P(('dp', 'expert', 'tensor')), may hold values from 0.2 to 1
- allowed_placements: int32 [8], replicated, may hold values from 2 to 3
- favored_specialist: int32 [1], replicated, may hold values from 0 to 7
- gating_matrices: bfloat16 [8, 7168, 4096], P('expert', ('dp', 'tensor')), may hold values from -0.09375 to 0.09375
- expand_matrices: bfloat16 [8, 7168, 4096], P('expert', ('dp', 'tensor')), may hold values from -0.09375 to 0.09375
- contract_matrices: bfloat16 [8, 7168, 4096], P('expert', ('dp', 'tensor')), may hold values from -0.0625 to 0.0625
Outputs:
- layer_out: bfloat16 [4096, 4096], P(('dp', 'expert', 'tensor'))
Inputs may be any that keep to these rules, and one draw needn't show every extreme that they name: `chosen_specialists`: in the 16 rows of one device no expert is named by more than 6 rows; a token names two different experts.
All inputs are finite; a program needn't handle non-finite values.
Results may differ from a plain program's by a relative error of at most 0.018.
Values may be sent and summed in bfloat16 or wider, within the bound.
A program may use at most 128 MiB of HBM per device.

v0:
```python
from functools import reduce
import math

import jax
import jax.numpy as jnp
from jax import lax
from jax.sharding import PartitionSpec as P

HD = 128
PLACEMENT_MOST = 6


def normalize(parts):
    highest = reduce(
        jnp.maximum,
        [
            jnp.max(jnp.where(visible, scores, -jnp.inf), axis=-1, keepdims=True)
            for scores, visible in parts
        ],
    )
    portions = [jnp.where(visible, jnp.exp(scores - highest), 0.0) for scores, visible in parts]
    denominator = reduce(
        jnp.add, [jnp.sum(portion, axis=-1, keepdims=True) for portion in portions]
    )
    return [(portion / denominator).astype(jnp.bfloat16) for portion in portions]


def attend(question_vectors, new_keys, new_values, key_pages, value_pages, table, spans):
    rows_all, head_count, head_width = question_vectors.shape
    kv_heads = new_keys.shape[1]
    group_size = head_count // kv_heads
    single_count = spans.shape[0] - 1
    page_count = table.shape[1]
    page_width = key_pages.shape[2]
    context = page_count * page_width
    inverse_root = 1.0 / math.sqrt(head_width)
    page_keys = key_pages[table]
    page_values = value_pages[table]
    grouped = question_vectors.reshape(rows_all, kv_heads, group_size, head_width)
    positions = jnp.arange(context, dtype=jnp.int32)
    single_q = grouped[:single_count]
    cache_dec = (
        jnp.einsum(
            "rkgh,rmkph->rkgmp",
            single_q,
            page_keys[:single_count],
            preferred_element_type=jnp.float32,
        ).reshape(single_count, kv_heads, group_size, context)
        * inverse_root
    )
    seen_dec = (positions[None, :] < spans[:single_count, None])[:, None, None, :]
    own_dec = (
        jnp.einsum(
            "rkgh,rkh->rkg", single_q, new_keys[:single_count], preferred_element_type=jnp.float32
        )[..., None]
        * inverse_root
    )
    weight_cache, weight_own = normalize(
        [(cache_dec, seen_dec), (own_dec, jnp.full(own_dec.shape, True))]
    )
    out_dec = jnp.einsum(
        "rkgmp,rmkph->rkgh",
        weight_cache.reshape(single_count, kv_heads, group_size, page_count, page_width),
        page_values[:single_count],
        preferred_element_type=jnp.float32,
    )
    out_dec = (
        out_dec
        + weight_own.astype(jnp.float32)
        * new_values[:single_count].astype(jnp.float32)[:, :, None, :]
    )
    prompt_q = grouped[single_count:]
    prompt_rows = rows_all - single_count
    cache_pro = (
        jnp.einsum(
            "rkgh,mkph->rkgmp",
            prompt_q,
            page_keys[single_count],
            preferred_element_type=jnp.float32,
        ).reshape(prompt_rows, kv_heads, group_size, context)
        * inverse_root
    )
    seen_pro = (positions < spans[single_count])[None, None, None, :]
    new_pro = (
        jnp.einsum(
            "rkgh,mkh->rkgm", prompt_q, new_keys[single_count:], preferred_element_type=jnp.float32
        )
        * inverse_root
    )
    prompt_index = jnp.arange(prompt_rows, dtype=jnp.int32)
    causal = (prompt_index[:, None] >= prompt_index[None, :])[:, None, None, :]
    weight_cpro, weight_npro = normalize([(cache_pro, seen_pro), (new_pro, causal)])
    out_pro = jnp.einsum(
        "rkgmp,mkph->rkgh",
        weight_cpro.reshape(prompt_rows, kv_heads, group_size, page_count, page_width),
        page_values[single_count],
        preferred_element_type=jnp.float32,
    )
    out_pro = out_pro + jnp.einsum(
        "rkgm,mkh->rkgh", weight_npro, new_values[single_count:], preferred_element_type=jnp.float32
    )
    joined = jnp.concatenate([out_dec, out_pro], axis=0).astype(jnp.bfloat16)
    return joined.reshape(rows_all, head_count * head_width)


def slot_table(member, ranking, keeping, slot_count):
    slot_hit = (
        ranking[:, :, None, None] == jnp.arange(slot_count, dtype=jnp.int32)[None, None, None, :]
    )
    return ((member[..., None] > 0) & keeping[:, :, None, None] & slot_hit).astype(jnp.bfloat16)


def expert_pass(send, gating_matrices, expand_matrices, contract_matrices):
    specialist_index, slot_count, model_width = send.shape
    holders = lax.axis_size("expert")
    local_count = gating_matrices.shape[0]
    arrived = lax.all_to_all(
        send.reshape(holders, local_count, slot_count, model_width),
        "expert",
        split_axis=0,
        concat_axis=0,
        tiled=True,
    )
    row_piece = lax.all_gather(arrived, ("dp", "tensor"), axis=0, tiled=True)
    gate_part = jnp.einsum(
        "qesd,efd->qesf", row_piece, gating_matrices, preferred_element_type=jnp.float32
    )
    up_part = jnp.einsum(
        "qesd,efd->qesf", row_piece, expand_matrices, preferred_element_type=jnp.float32
    )
    hidden = (jax.nn.silu(gate_part) * up_part).astype(jnp.bfloat16)
    summed = lax.psum_scatter(
        jnp.einsum(
            "qesf,efd->qesd", hidden, contract_matrices, preferred_element_type=jnp.float32
        ).astype(jnp.bfloat16),
        ("dp", "tensor"),
        scatter_dimension=0,
        tiled=True,
    )
    arrived_back = lax.all_to_all(summed, "expert", split_axis=0, concat_axis=0, tiled=True)
    return arrived_back.reshape(specialist_index, slot_count, model_width)


def local(
    skip_stream_entry,
    question_vectors,
    fresh_lookup_vectors,
    fresh_content_vectors,
    stored_lookup_sheets,
    stored_content_sheets,
    sequence_sheet_map,
    stored_position_counts,
    attention_merge_matrix,
    premix_scale_factor,
    chosen_specialists,
    selection_shares,
    allowed_placements,
    favored_specialist,
    gating_matrices,
    expand_matrices,
    contract_matrices,
):
    token_count = chosen_specialists.shape[0]
    specialist_index = allowed_placements.shape[0]
    picked = (
        chosen_specialists[:, :, None]
        == jnp.arange(specialist_index, dtype=jnp.int32)[None, None, :]
    ).astype(jnp.int32)
    flat_routes = picked.reshape(token_count * 2, specialist_index)
    busiest_specialist = favored_specialist[0]
    before = (jnp.cumsum(flat_routes, axis=0) - flat_routes).reshape(
        token_count, 2, specialist_index
    )
    ranking = jnp.sum(before * picked, axis=2)
    placement_ceiling = jnp.where(
        jnp.arange(specialist_index, dtype=jnp.int32) == busiest_specialist,
        PLACEMENT_MOST,
        allowed_placements,
    )
    keeping = ranking < jnp.sum(picked * placement_ceiling[None, None, :], axis=2)
    row_total = question_vectors.shape[0]
    heads_out = attend(
        question_vectors.reshape(row_total, -1, HD),
        fresh_lookup_vectors.reshape(row_total, -1, HD),
        fresh_content_vectors.reshape(row_total, -1, HD),
        stored_lookup_sheets,
        stored_content_sheets,
        sequence_sheet_map,
        stored_position_counts,
    )
    total_attn = lax.psum(
        jnp.dot(heads_out, attention_merge_matrix, preferred_element_type=jnp.float32).astype(
            jnp.bfloat16
        ),
        "tensor",
    ).astype(jnp.float32)
    own_attn = lax.dynamic_slice_in_dim(
        total_attn, lax.axis_index("tensor") * token_count, token_count, 0
    )
    stream = (skip_stream_entry.astype(jnp.float32) + own_attn).astype(jnp.bfloat16)
    wide = stream.astype(jnp.float32)
    squares = jnp.mean(wide * wide, axis=1, keepdims=True)
    normed = (wide * lax.rsqrt(squares + 1e-05) * premix_scale_factor.astype(jnp.float32)).astype(
        jnp.bfloat16
    )
    main_slots = PLACEMENT_MOST
    table_main = slot_table(picked, ranking, keeping, main_slots)
    send = jnp.einsum(
        "nkes,nd->esd", table_main, normed, preferred_element_type=jnp.float32
    ).astype(jnp.bfloat16)
    expert_out = expert_pass(send, gating_matrices, expand_matrices, contract_matrices)
    chosen = jnp.einsum("nkes,esd->nkd", table_main, expert_out, preferred_element_type=jnp.float32)
    mixed = jnp.sum(selection_shares[:, :, None] * chosen, axis=1)
    return (wide + mixed).astype(jnp.bfloat16)


def solution(mesh):
    placed = (
        P(("dp", "expert", "tensor"), None),
        P(("dp", "expert"), "tensor"),
        P(("dp", "expert"), "tensor"),
        P(("dp", "expert"), "tensor"),
        P(("dp", "expert"), "tensor", None, None),
        P(("dp", "expert"), "tensor", None, None),
        P(("dp", "expert"), None),
        P(("dp", "expert")),
        P("tensor", None),
        P(),
        P(("dp", "expert", "tensor"), None),
        P(("dp", "expert", "tensor"), None),
        P(),
        P(),
        P("expert", ("dp", "tensor"), None),
        P("expert", ("dp", "tensor"), None),
        P("expert", ("dp", "tensor"), None),
    )
    return jax.shard_map(
        local,
        mesh=mesh,
        in_specs=placed,
        out_specs=P(("dp", "expert", "tensor"), None),
        check_vma=False,
    )
```

profile of v0, /device:TPU:1, one launch (start us, length us, event | category | flops | bytes accessed | tf_op | source)
XLA Modules:
  0.0 524.3 jit_solution(17643247825610489916)
XLA Ops:
  6.6 0.9 slice.44
  7.4 1.2 slice.49
  8.7 1.2 broadcast_compare_fusion.1
  9.8 0.7 compare_select_fusion
  10.5 1.3 slice_bitcast_fusion.5
  11.8 0.1 copy.32
  11.9 0.1 reshape.332
  12.0 1.3 slice_convert_fusion
  13.3 1.6 select_reduce_fusion.2
  14.8 8.8 %gather_fusion.1 = bf16[136,128,128]{2,1,0:T(8,128)(2,1)} fusion(bf16[40,128,128]{2,1,0:T(8,128)(2,1)} %bitcast.233, s32[1024]{0:T(1024)S(1)} %pad_clamp_fusion), kind=kCustom, calls=%fused_computation.1 | custom fusion | bytes 8913440 | tf_op jit(solution)/shard_map/gather | solution.py:38
  23.7 0.0 copy-start.2
  23.7 1.3 copy-done.2
  25.0 7.5 %gather_fusion = bf16[136,128,128]{2,1,0:T(8,128)(2,1)} fusion(bf16[40,128,128]{2,1,0:T(8,128)(2,1)S(1)} %bitcast.234, s32[1024]{0:T(1024)S(1)} %pad_clamp_fusion), kind=kCustom, calls=%fused_computation | custom fusion | bytes 8913440 | tf_op jit(solution)/shard_map/gather | solution.py:37
  32.5 0.0 copy-start.8
  32.6 0.0 copy-start.13
  32.6 0.0 slice-start.1
  32.6 0.8 copy-done.8
  33.4 1.7 select_reduce_fusion
  35.2 0.3 bitcast_reduce_fusion
  35.5 0.2 convolution_bitcast_fusion.2
  35.7 0.0 slice-start.2
  35.7 0.0 copy-start.7
  35.8 0.3 fusion.43
  36.1 0.1 broadcast_compare_fusion
  36.2 0.0 copy-done.9
  36.2 0.1 fusion.88
  36.4 0.0 copy-start.3
  36.4 1.3 select_reduce_fusion.1
  37.7 0.3 bitcast_reduce_fusion.1
  38.0 1.4 slice-done.2
  39.4 0.0 copy-start.4
  39.4 0.8 fusion.45
  40.2 1.7 convolution_convert_fusion
  41.8 0.0 all-reduce.2.cloned.1.call-update
  41.8 0.0 all-gather.2.cloned.1.call-start
  42.6 0.1 copy.38
  42.6 0.0 copy-done.15
  42.6 0.1 select_reduce_fusion.4
  42.7 0.1 eq.56
  42.8 0.1 fusion.82
  42.9 0.1 reduce_window_sum.11
  42.9 0.2 select_reduce_fusion.3
  43.1 0.1 reduce_sum.82
  43.2 0.1 copy.39
  43.3 0.0 copy-done.6
  43.4 48.7 %all-reduce.2.cloned.1.call-done = bf16[64,4096]{1,0:T(8,128)(2,1)} async-done(((bf16[64,4096]{1,0:T(8,128)(2,1)}), bf16[64,4096]{1,0:T(8,128)(2,1)}) %all-reduce.2.cloned.1.call-update) | async-done | bytes 524304 | tf_op jit(solution)/shard_map/psum | solution.py:191
  92.1 1.1 fusion.53
  93.2 0.3 fusion.5
  93.5 0.2 copy.41
  93.7 15.9 %all_to_all.10 = bf16[8,1,6,4096]{3,2,1,0:T(8,128)(2,1)S(1)} all-to-all(bf16[8,1,6,4096]{3,2,1,0:T(8,128)(2,1)S(1)} %copy.41), channel_id=1, replica_groups=mesh['dp'=8,'expert'=8,'tensor'=4] {'expert'}, dimensions={0} | all-to-all | bytes 786432 | tf_op jit(solution)/shard_map/all_to_all | solution.py:117
  109.6 1.0 copy.42
  110.6 0.0 all-gather.2.cloned.1.call-update
  110.6 0.2 reduce-scatter.4.cloned.1.call-start
  110.9 118.4 %all-gather.2.cloned.1.call-done = bf16[256,1,6,4096]{3,0,2,1:T(8,128)(2,1)} async-done(((bf16[8,1,6,4096]{3,0,2,1:T(8,128)(2,1)}), bf16[256,1,6,4096]{3,0,2,1:T(8,128)(2,1)}) %all-gather.2.cloned.1.call-update) | async-done | bytes 12582928 | tf_op jit(solution)/shard_map/all_gather | solution.py:124
  229.3 7.5 %fusion.9 = f32[256,1,6,224]{0,3,2,1:T(8,128)S(1)} fusion(bf16[1,224,4096]{2,1,0:T(8,128)(2,1)} %param.31, bf16[256,1,6,4096]{3,0,2,1:T(8,128)(2,1)} %all-gather.2.cloned.1.call-done), kind=kOutput, calls=%fused_computation.15 | convolution fusion | flops 2818572288 | bytes 15794176 | tf_op jit(solution)/shard_map/qesd,efd->qesf/dot_general | solution.py:125
  236.8 19.2 %fusion.97 = bf16[32,8,6,4096]{3,1,0,2:T(8,128)(2,1)} fusion(bf16[1,224,4096]{2,1,0:T(8,128)(2,1)S(1)} %copy-done, bf16[1,224,4096]{2,1,0:T(8,128)(2,1)} %param.32, bf16[256,1,6,4096]{3,0,2,1:T(8,128)(2,1)} %all-gather.2.cloned.1.call-done, f32[256,1,6,224]{0,3,2,1:T(8,128)S(1)} %fusion.9), kind=kOutput, calls=%fused_computation.124 | convolution fusion | flops 5645500416 | bytes 30212096 | tf_op jit(solution)/shard_map/qesf,efd->qesd/dot_general | solution.py:133
  256.0 10.6 %copy.58 = bf16[32,8,6,4096]{3,1,2,0:T(8,128)(2,1)} copy(bf16[32,8,6,4096]{3,1,0,2:T(8,128)(2,1)} %fusion.97) | data formatting | bytes 25165824
  266.7 0.0 reduce-scatter.4.cloned.1.call-update
  266.7 0.0 copy-start.1
  266.7 230.6 %reduce-scatter.4.cloned.1.call-done = bf16[8,24576]{1,0:T(8,128)(2,1)} async-done(((bf16[256,24576]{1,0:T(8,128)(2,1)}), bf16[8,24576]{1,0:T(8,128)(2,1)}) %reduce-scatter.4.cloned.1.call-update) | async-done | bytes 393232
  497.3 1.2 copy.43
  498.5 18.2 %all_to_all.11 = bf16[8,1,6,4096]{3,2,1,0:T(8,128)(2,1)S(1)} all-to-all(bf16[8,1,6,4096]{3,2,1,0:T(8,128)(2,1)S(1)} %copy.43), channel_id=1, replica_groups=mesh['dp'=8,'expert'=8,'tensor'=4] {'expert'}, dimensions={0} | all-to-all | bytes 786432 | tf_op jit(solution)/shard_map/all_to_all | solution.py:140
  516.8 0.3 fusion.39
  517.1 0.7 fusion.56
  (47 shorter events, 0.3 us)
Async XLA Ops:
  6.5 230.2 %copy-start = (bf16[1,224,4096]{2,1,0:T(8,128)(2,1)S(1)}, bf16[1,224,4096]{2,1,0:T(8,128)(2,1)}, u32[]{:S(2)}) copy-start(bf16[1,224,4096]{2,1,0:T(8,128)(2,1)} %param.33) | copy-start | bytes 5505028
  6.5 85.6 %all-reduce.2.cloned.1.call-start = ((), (), s32[]{:S(2)}) async-start(), calls=%async_computation.3 | async-start | bytes 1048576 | tf_op jit(solution)/shard_map/psum | solution.py:191
  23.7 1.3 copy-start.2
  25.0 10.7 %slice-start = ((s8[4456448]{0:T(1024)(128)(4,1)}), s8[262144]{0:T(1024)(128)(4,1)S(1)}, s32[]{:S(2)}) async-start(s8[4456448]{0:T(1024)(128)(4,1)} %bitcast.229), calls=%async_computation.6 | async-start | bytes 524288
  32.5 0.8 copy-start.8
  32.6 0.8 copy-start.12
  32.6 2.6 copy-start.10
  32.6 2.9 copy-start.13
  32.6 3.1 slice-start.1
  33.4 2.7 copy-start.14
  33.4 2.8 copy-start.9
  33.4 3.0 slice-start.3
  35.7 3.6 slice-start.2
  35.7 3.6 copy-start.7
  36.4 3.8 copy-start.3
  39.4 3.2 copy-start.5
  39.4 3.3 copy-start.15
  39.4 4.0 copy-start.6
  39.4 52.7 %copy-start.4 = (bf16[16,4096]{1,0:T(8,128)(2,1)S(1)}, bf16[16,4096]{1,0:T(8,128)(2,1)}, u32[]{:S(2)}) copy-start(bf16[16,4096]{1,0:T(8,128)(2,1)} %param.17) | copy-start | bytes 393220
  41.8 187.5 %all-gather.2.cloned.1.call-start = ((), (), s32[]{:S(2)}) async-start(), calls=%async_computation.4 | async-start | bytes 12976128 | tf_op jit(solution)/shard_map/all_gather | solution.py:124
  110.6 386.6 %reduce-scatter.4.cloned.1.call-start = ((), (), s32[]{:S(2)}) async-start(), calls=%async_computation.5 | async-start | bytes 12976128
  266.7 250.1 %copy-start.11 = (f32[16,2]{0,1:T(2,128)S(1)}, f32[16,2]{0,1:T(2,128)}, u32[]{:S(2)}) copy-start(f32[16,2]{0,1:T(2,128)} %param.28) | copy-start | bytes 388
  266.7 251.1 %copy-start.1 = (bf16[1,224,4096]{2,1,0:T(8,128)(2,1)S(1)}, bf16[1,224,4096]{2,1,0:T(8,128)(2,1)}, u32[]{:S(2)}) copy-start(bf16[1,224,4096]{2,1,0:T(8,128)(2,1)} %param.33) | copy-start | bytes 5505028
Sparse Core Ops, SparseCore 0:
  42.0 50.0 all-reduce.1
  110.8 118.4 all-gather.1
  266.8 230.4 reduce-scatter.3
where the time goes:
time: 525 us; the launch traced here: 524 us
  waiting for transfers between devices  398 us (76%)
  local copies, waits for them, and re-layouts  36.9 us (7%)
  matrix products  35 us (7%)
  blocking collectives  34.1 us (6%)
  between operations  14.1 us (3%)
  other arithmetic  6.11 us (1%)
    unnamed x4, waiting for transfers between devices  231 us
    all_gather x1, waiting for transfers between devices, expert_pass(): row_piece = lax.all_gather(arrived, ('dp', 'tensor'), axis=0, tiled=True)  118 us
    psum x1, waiting for transfers between devices, local(): lax.psum(jnp.dot(heads_out, attention_merge_matrix, preferred_element_typ...  48.7 us
    dot_general x1, matrix products, expert_pass(): jnp.einsum('qesf,efd->qesd', hidden, contract_matrices, preferred_element...  19.2 us
    all_to_all x1, blocking collectives, expert_pass(): lax.all_to_all(summed, 'expert', split_axis=0, concat_axis=0, tiled=True)  18.2 us
    all_to_all x1, blocking collectives, expert_pass(): lax.all_to_all(send.reshape(holders, local_count, slot_count, model_width...  15.9 us
    unnamed x40, local copies, waits for them, and re-layouts  12.9 us
  transfers between devices with their start and end apart: 3, of which 3 were waited for; matrix products, arithmetic and copies ran while one was open for 0% of the time, Pallas kernels for 0%

commit v1 on v0

--- a/solution.py
+++ b/solution.py
@@ -188,15 +188,14 @@
         sequence_sheet_map,
         stored_position_counts,
     )
-    total_attn = lax.psum(
+    own_attn = lax.psum_scatter(
         jnp.dot(heads_out, attention_merge_matrix, preferred_element_type=jnp.float32).astype(
             jnp.bfloat16
         ),
         "tensor",
+        scatter_dimension=0,
+        tiled=True,
     ).astype(jnp.float32)
-    own_attn = lax.dynamic_slice_in_dim(
-        total_attn, lax.axis_index("tensor") * token_count, token_count, 0
-    )
     stream = (skip_stream_entry.astype(jnp.float32) + own_attn).astype(jnp.bfloat16)
     wide = stream.astype(jnp.float32)
     squares = jnp.mean(wide * wide, axis=1, keepdims=True)

time: 525 us -> 501 us (0.954)
  waiting for transfers between devices: 398 us -> 373 us
    psum x1 -> x0, waiting for transfers between devices: 48.7 us -> none  [local(): lax.psum(jnp.dot(heads_out, attention_merge_matrix, preferred_element_typ...]
    reduce_scatter x0 -> x1, waiting for transfers between devices: none -> 24.7 us  [local(): lax.psum_scatter(jnp.dot(heads_out, attention_merge_matrix, preferred_ele...]
    unnamed x40 -> x42, local copies, waits for them, and re-layouts: 12.9 us -> 12.9 us
where the time goes in v1:
time: 501 us; the launch traced here: 500 us
  waiting for transfers between devices  373 us (74%)
  local copies, waits for them, and re-layouts  36.9 us (7%)
  matrix products  35.9 us (7%)
  blocking collectives  34.1 us (7%)
  between operations  14.1 us (3%)
  other arithmetic  6.11 us (1%)
    unnamed x4, waiting for transfers between devices  231 us
    all_gather x1, waiting for transfers between devices, expert_pass(): row_piece = lax.all_gather(arrived, ('dp', 'tensor'), axis=0, tiled=True)  118 us
    reduce_scatter x1, waiting for transfers between devices, local(): lax.psum_scatter(jnp.dot(heads_out, attention_merge_matrix, preferred_ele...  24.7 us
    dot_general x1, matrix products, expert_pass(): jnp.einsum('qesf,efd->qesd', hidden, contract_matrices, preferred_element...  19.3 us
    all_to_all x1, blocking collectives, expert_pass(): lax.all_to_all(summed, 'expert', split_axis=0, concat_axis=0, tiled=True)  18.3 us
    all_to_all x1, blocking collectives, expert_pass(): lax.all_to_all(send.reshape(holders, local_count, slot_count, model_width...  15.7 us
    unnamed x42, local copies, waits for them, and re-layouts  12.9 us
  transfers between devices with their start and end apart: 3, of which 3 were waited for; matrix products, arithmetic and copies ran while one was open for 0% of the time, Pallas kernels for 0%

profile of v1, /device:TPU:1, one launch (start us, length us, event | category | flops | bytes accessed | tf_op | source)
XLA Modules:
  0.0 500.2 jit_solution(16697747358621664481)
XLA Ops:
  6.6 0.9 slice.44
  7.4 1.2 slice.49
  8.7 1.2 broadcast_compare_fusion.1
  9.8 0.7 compare_select_fusion
  10.5 1.3 slice_bitcast_fusion.5
  11.8 0.1 copy.32
  11.9 0.1 reshape.332
  12.0 1.3 slice_convert_fusion
  13.3 1.6 select_reduce_fusion.2
  14.8 8.8 %gather_fusion.1 = bf16[136,128,128]{2,1,0:T(8,128)(2,1)} fusion(bf16[40,128,128]{2,1,0:T(8,128)(2,1)} %bitcast.233, s32[1024]{0:T(1024)S(1)} %pad_clamp_fusion), kind=kCustom, calls=%fused_computation.1 | custom fusion | bytes 8913440 | tf_op jit(solution)/shard_map/gather | solution.py:38
  23.7 0.0 copy-start.2
  23.7 1.3 copy-done.2
  25.0 7.5 %gather_fusion = bf16[136,128,128]{2,1,0:T(8,128)(2,1)} fusion(bf16[40,128,128]{2,1,0:T(8,128)(2,1)S(1)} %bitcast.234, s32[1024]{0:T(1024)S(1)} %pad_clamp_fusion), kind=kCustom, calls=%fused_computation | custom fusion | bytes 8913440 | tf_op jit(solution)/shard_map/gather | solution.py:37
  32.5 0.0 copy-start.9
  32.6 0.0 copy-start.14
  32.6 0.0 slice-start.1
  32.6 0.8 copy-done.9
  33.4 0.0 copy-done.13
  33.4 1.7 select_reduce_fusion
  35.2 0.3 bitcast_reduce_fusion
  35.5 0.2 convolution_bitcast_fusion.2
  35.7 0.0 slice-start.2
  35.7 0.0 copy-start.8
  35.7 0.3 fusion.43
  36.1 0.1 broadcast_compare_fusion
  36.2 0.1 fusion.88
  36.4 0.0 copy-start.3
  36.4 1.3 select_reduce_fusion.1
  37.7 0.3 bitcast_reduce_fusion.1
  38.0 1.4 slice-done.2
  39.3 0.0 copy-done.8
  39.4 0.0 copy-start.4
  39.4 0.8 fusion.45
  40.2 1.6 convolution_convert_fusion
  41.8 0.0 reduce-scatter.5.cloned.1.call-update
  41.8 0.0 all-gather.2.cloned.1.call-start
  41.9 0.1 copy.38
  42.0 0.1 eq.56
  42.0 0.1 fusion.82
  42.8 0.1 reduce_window_sum.11
  42.8 0.2 select_reduce_fusion.3
  43.0 0.1 reduce_sum.82
  43.1 0.1 copy.39
  43.2 0.0 copy-done.16
  43.2 0.1 select_reduce_fusion.4
  43.4 24.7 %reduce-scatter.5.cloned.1.call-done = bf16[16,4096]{1,0:T(8,128)(2,1)} async-done(((bf16[64,4096]{1,0:T(8,128)(2,1)}), bf16[16,4096]{1,0:T(8,128)(2,1)}) %reduce-scatter.5.cloned.1.call-update) | async-done | bytes 131088 | tf_op jit(solution)/shard_map/reduce_scatter | solution.py:191
  68.1 1.1 fusion.53
  69.2 1.2 fusion.5
  70.4 0.2 copy.41
  70.6 15.7 %all_to_all.10 = bf16[8,1,6,4096]{3,2,1,0:T(8,128)(2,1)S(1)} all-to-all(bf16[8,1,6,4096]{3,2,1,0:T(8,128)(2,1)S(1)} %copy.41), channel_id=1, replica_groups=mesh['dp'=8,'expert'=8,'tensor'=4] {'expert'}, dimensions={0} | all-to-all | bytes 786432 | tf_op jit(solution)/shard_map/all_to_all | solution.py:117
  86.4 1.0 copy.42
  87.4 0.0 all-gather.2.cloned.1.call-update
  87.4 0.2 reduce-scatter.7.cloned.1.call-start
  87.6 117.5 %all-gather.2.cloned.1.call-done = bf16[256,1,6,4096]{3,0,2,1:T(8,128)(2,1)} async-done(((bf16[8,1,6,4096]{3,0,2,1:T(8,128)(2,1)}), bf16[256,1,6,4096]{3,0,2,1:T(8,128)(2,1)}) %all-gather.2.cloned.1.call-update) | async-done | bytes 12582928 | tf_op jit(solution)/shard_map/all_gather | solution.py:124
  205.1 7.4 %fusion.9 = f32[256,1,6,224]{0,3,2,1:T(8,128)S(1)} fusion(bf16[1,224,4096]{2,1,0:T(8,128)(2,1)} %param.31, bf16[256,1,6,4096]{3,0,2,1:T(8,128)(2,1)} %all-gather.2.cloned.1.call-done), kind=kOutput, calls=%fused_computation.15 | convolution fusion | flops 2818572288 | bytes 15794176 | tf_op jit(solution)/shard_map/qesd,efd->qesf/dot_general | solution.py:125
  212.6 19.3 %fusion.97 = bf16[32,8,6,4096]{3,1,0,2:T(8,128)(2,1)} fusion(bf16[1,224,4096]{2,1,0:T(8,128)(2,1)S(1)} %copy-done, bf16[1,224,4096]{2,1,0:T(8,128)(2,1)} %param.32, bf16[256,1,6,4096]{3,0,2,1:T(8,128)(2,1)} %all-gather.2.cloned.1.call-done, f32[256,1,6,224]{0,3,2,1:T(8,128)S(1)} %fusion.9), kind=kOutput, calls=%fused_computation.124 | convolution fusion | flops 5645500416 | bytes 30212096 | tf_op jit(solution)/shard_map/qesf,efd->qesd/dot_general | solution.py:133
  231.9 10.6 %copy.58 = bf16[32,8,6,4096]{3,1,2,0:T(8,128)(2,1)} copy(bf16[32,8,6,4096]{3,1,0,2:T(8,128)(2,1)} %fusion.97) | data formatting | bytes 25165824
  242.5 0.0 reduce-scatter.7.cloned.1.call-update
  242.5 0.0 copy-start.1
  242.6 230.5 %reduce-scatter.7.cloned.1.call-done = bf16[8,24576]{1,0:T(8,128)(2,1)} async-done(((bf16[256,24576]{1,0:T(8,128)(2,1)}), bf16[8,24576]{1,0:T(8,128)(2,1)}) %reduce-scatter.7.cloned.1.call-update) | async-done | bytes 393232
  473.1 1.2 copy.43
  474.3 18.3 %all_to_all.11 = bf16[8,1,6,4096]{3,2,1,0:T(8,128)(2,1)S(1)} all-to-all(bf16[8,1,6,4096]{3,2,1,0:T(8,128)(2,1)S(1)} %copy.43), channel_id=1, replica_groups=mesh['dp'=8,'expert'=8,'tensor'=4] {'expert'}, dimensions={0} | all-to-all | bytes 786432 | tf_op jit(solution)/shard_map/all_to_all | solution.py:140
  492.6 0.3 fusion.39
  493.0 0.7 fusion.56
  (49 shorter events, 0.3 us)
Async XLA Ops:
  6.5 206.1 %copy-start = (bf16[1,224,4096]{2,1,0:T(8,128)(2,1)S(1)}, bf16[1,224,4096]{2,1,0:T(8,128)(2,1)}, u32[]{:S(2)}) copy-start(bf16[1,224,4096]{2,1,0:T(8,128)(2,1)} %param.33) | copy-start | bytes 5505028
  6.5 61.6 %reduce-scatter.5.cloned.1.call-start = ((), (), s32[]{:S(2)}) async-start(), calls=%async_computation.4 | async-start | bytes 655360 | tf_op jit(solution)/shard_map/reduce_scatter | solution.py:191
  23.7 1.3 copy-start.2
  25.0 10.7 %slice-start = ((s8[4456448]{0:T(1024)(128)(4,1)}), s8[262144]{0:T(1024)(128)(4,1)S(1)}, s32[]{:S(2)}) async-start(s8[4456448]{0:T(1024)(128)(4,1)} %bitcast.229), calls=%async_computation.7 | async-start | bytes 524288
  32.5 0.8 copy-start.9
  32.6 0.8 copy-start.13
  32.6 2.6 copy-start.11
  32.6 2.9 copy-start.14
  32.6 3.1 slice-start.1
  33.4 2.7 copy-start.15
  33.4 2.8 copy-start.10
  33.4 3.0 slice-start.3
  35.7 3.6 slice-start.2
  35.7 3.6 copy-start.8
  36.4 3.8 copy-start.3
  39.3 2.5 copy-start.6
  39.4 3.8 copy-start.7
  39.4 3.8 copy-start.16
  39.4 28.7 %copy-start.4 = (bf16[16,4096]{1,0:T(8,128)(2,1)S(1)}, bf16[16,4096]{1,0:T(8,128)(2,1)}, u32[]{:S(2)}) copy-start(bf16[16,4096]{1,0:T(8,128)(2,1)} %param.17) | copy-start | bytes 393220
  41.8 163.3 %all-gather.2.cloned.1.call-start = ((), (), s32[]{:S(2)}) async-start(), calls=%async_computation.5 | async-start | bytes 12976128 | tf_op jit(solution)/shard_map/all_gather | solution.py:124
  87.4 385.7 %reduce-scatter.7.cloned.1.call-start = ((), (), s32[]{:S(2)}) async-start(), calls=%async_computation.6 | async-start | bytes 12976128
  242.5 250.1 %copy-start.12 = (f32[16,2]{0,1:T(2,128)S(1)}, f32[16,2]{0,1:T(2,128)}, u32[]{:S(2)}) copy-start(f32[16,2]{0,1:T(2,128)} %param.28) | copy-start | bytes 388
  242.5 250.5 %copy-start.5 = (bf16[16,4096]{1,0:T(8,128)(2,1)S(1)}, bf16[16,4096]{1,0:T(8,128)(2,1)}, u32[]{:S(2)}) copy-start(bf16[16,4096]{1,0:T(8,128)(2,1)} %reduce-scatter.5.cloned.1.call-done) | copy-start | bytes 393220
  242.5 251.2 %copy-start.1 = (bf16[1,224,4096]{2,1,0:T(8,128)(2,1)S(1)}, bf16[1,224,4096]{2,1,0:T(8,128)(2,1)}, u32[]{:S(2)}) copy-start(bf16[1,224,4096]{2,1,0:T(8,128)(2,1)} %param.33) | copy-start | bytes 5505028
Sparse Core Ops, SparseCore 0:
  41.9 26.1 reduce-scatter.4
  87.5 117.5 all-gather.1
  242.7 230.3 reduce-scatter.6

commit v2 on v1

--- a/solution.py
+++ b/solution.py
@@ -129,11 +129,12 @@
         "qesd,efd->qesf", row_piece, expand_matrices, preferred_element_type=jnp.float32
     )
     hidden = (jax.nn.silu(gate_part) * up_part).astype(jnp.bfloat16)
+    partial_out = jnp.einsum(
+        "qesf,efd->qesd", hidden, contract_matrices, preferred_element_type=jnp.float32
+    ).astype(jnp.bfloat16)
     summed = lax.psum_scatter(
-        jnp.einsum(
-            "qesf,efd->qesd", hidden, contract_matrices, preferred_element_type=jnp.float32
-        ).astype(jnp.bfloat16),
-        ("dp", "tensor"),
+        lax.psum_scatter(partial_out, "dp", scatter_dimension=0, tiled=True),
+        "tensor",
         scatter_dimension=0,
         tiled=True,
     )

time: 501 us -> 417 us (0.83)
  waiting for transfers between devices: 373 us -> 301 us
  local copies, waits for them, and re-layouts: 36.9 us -> 29 us
    unnamed x4 -> x5, waiting for transfers between devices: 231 us -> 26.2 us
    reduce_scatter x0 -> x1, waiting for transfers between devices: none -> 132 us  [expert_pass(): lax.psum_scatter(partial_out, 'dp', scatter_dimension=0, tiled=True)]
    unnamed x42 -> x40, local copies, waits for them, and re-layouts: 12.9 us -> 4.99 us
  transfers between devices with their start and end apart: 3 -> 4, of which waited for: 3 -> 4; matrix products, arithmetic and copies ran while one was open for 0% -> 0% of each run, Pallas kernels for 0% -> 0%
where the time goes in v2:
time: 417 us
  waiting for transfers between devices  301 us (72%)
  matrix products  35.9 us (9%)
  blocking collectives  30.8 us (7%)
  local copies, waits for them, and re-layouts  29 us (7%)
  between operations  14.2 us (3%)
  other arithmetic  6.11 us (1%)
    reduce_scatter x1, waiting for transfers between devices, expert_pass(): lax.psum_scatter(partial_out, 'dp', scatter_dimension=0, tiled=True)  132 us
    all_gather x1, waiting for transfers between devices, expert_pass(): row_piece = lax.all_gather(arrived, ('dp', 'tensor'), axis=0, tiled=True)  118 us
    unnamed x5, waiting for transfers between devices  26.2 us
    reduce_scatter x1, waiting for transfers between devices, local(): lax.psum_scatter(jnp.dot(heads_out, attention_merge_matrix, preferred_ele...  24.8 us
    dot_general x1, matrix products, expert_pass(): jnp.einsum('qesf,efd->qesd', hidden, contract_matrices, preferred_element...  19.3 us
    all_to_all x1, blocking collectives, expert_pass(): lax.all_to_all(send.reshape(holders, local_count, slot_count, model_width...  15.8 us
    all_to_all x1, blocking collectives, expert_pass(): lax.all_to_all(summed, 'expert', split_axis=0, concat_axis=0, tiled=True)  15.1 us
    gather x1, local copies, waits for them, and re-layouts, attend(): page_values = value_pages[table]  8.83 us
  transfers between devices with their start and end apart: 4, of which 4 were waited for; matrix products, arithmetic and copies ran while one was open for 0% of the time, Pallas kernels for 0%

profile of v2, /device:TPU:1, one launch (start us, length us, event | category | flops | bytes accessed | tf_op | source)
XLA Modules:
  0.0 416.9 jit_solution(13904441723688626765)
XLA Ops:
  6.6 0.9 slice.44
  7.4 1.2 slice.49
  8.7 1.2 broadcast_compare_fusion.1
  9.8 0.7 compare_select_fusion
  10.5 1.3 slice_bitcast_fusion.5
  11.8 0.1 copy.32
  11.9 0.1 reshape.332
  12.0 1.3 slice_convert_fusion
  13.3 1.6 select_reduce_fusion.2
  14.8 8.8 %gather_fusion.1 = bf16[136,128,128]{2,1,0:T(8,128)(2,1)} fusion(bf16[40,128,128]{2,1,0:T(8,128)(2,1)} %bitcast.219, s32[1024]{0:T(1024)S(1)} %pad_clamp_fusion), kind=kCustom, calls=%fused_computation.1 | custom fusion | bytes 8913440 | tf_op jit(solution)/shard_map/gather | solution.py:38
  23.7 0.0 copy-start.1
  23.7 1.3 copy-done.1
  25.0 7.5 %gather_fusion = bf16[136,128,128]{2,1,0:T(8,128)(2,1)} fusion(bf16[40,128,128]{2,1,0:T(8,128)(2,1)S(1)} %bitcast.220, s32[1024]{0:T(1024)S(1)} %pad_clamp_fusion), kind=kCustom, calls=%fused_computation | custom fusion | bytes 8913440 | tf_op jit(solution)/shard_map/gather | solution.py:37
  32.5 0.0 copy-start.8
  32.6 0.0 copy-start.13
  32.6 0.0 slice-start.1
  32.6 0.8 copy-done.8
  33.4 1.7 select_reduce_fusion
  35.2 0.3 bitcast_reduce_fusion
  35.5 0.2 convolution_bitcast_fusion.2
  35.7 0.0 copy-start.7
  35.7 0.3 fusion.43
  36.1 0.1 broadcast_compare_fusion
  36.2 0.1 fusion.88
  36.4 0.0 copy-start.2
  36.4 1.3 select_reduce_fusion.1
  37.7 0.3 bitcast_reduce_fusion.1
  38.0 1.4 slice-done.2
  39.3 0.0 copy-start.3
  39.4 0.8 fusion.45
  40.1 1.6 convolution_convert_fusion
  41.8 0.0 reduce-scatter.6.cloned.1.call-update
  41.8 0.0 all-gather.2.cloned.1.call-start
  41.9 0.1 copy.38
  41.9 0.1 eq.56
  42.0 0.1 fusion.82
  42.8 0.1 reduce_window_sum.11
  42.8 0.2 select_reduce_fusion.3
  43.0 0.1 reduce_sum.82
  43.1 0.1 copy.39
  43.2 0.0 copy-done.15
  43.2 0.1 select_reduce_fusion.4
  43.3 24.8 %reduce-scatter.6.cloned.1.call-done = bf16[16,4096]{1,0:T(8,128)(2,1)} async-done(((bf16[64,4096]{1,0:T(8,128)(2,1)}), bf16[16,4096]{1,0:T(8,128)(2,1)}) %reduce-scatter.6.cloned.1.call-update) | async-done | bytes 131088 | tf_op jit(solution)/shard_map/reduce_scatter | solution.py:192
  68.1 1.1 fusion.53
  69.2 1.2 fusion.5
  70.4 0.2 copy.41
  70.6 15.8 %all_to_all.10 = bf16[8,1,6,4096]{3,2,1,0:T(8,128)(2,1)S(1)} all-to-all(bf16[8,1,6,4096]{3,2,1,0:T(8,128)(2,1)S(1)} %copy.41), channel_id=1, replica_groups=mesh['dp'=8,'expert'=8,'tensor'=4] {'expert'}, dimensions={0} | all-to-all | bytes 786432 | tf_op jit(solution)/shard_map/all_to_all | solution.py:117
  86.4 1.0 copy.42
  87.4 0.0 all-gather.2.cloned.1.call-update
  87.4 0.2 reduce-scatter.8.cloned.1.call-start
  87.6 117.5 %all-gather.2.cloned.1.call-done = bf16[256,1,6,4096]{3,0,2,1:T(8,128)(2,1)} async-done(((bf16[8,1,6,4096]{3,0,2,1:T(8,128)(2,1)}), bf16[256,1,6,4096]{3,0,2,1:T(8,128)(2,1)}) %all-gather.2.cloned.1.call-update) | async-done | bytes 12582928 | tf_op jit(solution)/shard_map/all_gather | solution.py:124
  205.1 7.5 %fusion.9 = f32[256,1,6,224]{0,3,2,1:T(8,128)S(1)} fusion(bf16[1,224,4096]{2,1,0:T(8,128)(2,1)} %param.31, bf16[256,1,6,4096]{3,0,2,1:T(8,128)(2,1)} %all-gather.2.cloned.1.call-done), kind=kOutput, calls=%fused_computation.15 | convolution fusion | flops 2818572288 | bytes 15794176 | tf_op jit(solution)/shard_map/qesd,efd->qesf/dot_general | solution.py:125
  212.6 19.3 %convert_bitcast_fusion = bf16[256,1,6,4096]{3,0,2,1:T(8,128)(2,1)} fusion(bf16[1,224,4096]{2,1,0:T(8,128)(2,1)S(1)} %copy-done, bf16[1,224,4096]{2,1,0:T(8,128)(2,1)} %param.32, bf16[256,1,6,4096]{3,0,2,1:T(8,128)(2,1)} %all-gather.2.cloned.1.call-done, f32[256,1,6,224]{0,3,2,1:T(8,128)S(1)} %fusion.9), kind=kOutput, calls=%fused_computation.6 | convolution fusion | flops 5645500416 | bytes 30212096 | tf_op jit(solution)/shard_map/qesf,efd->qesd/dot_general | solution.py:132
  231.9 0.0 reduce-scatter.8.cloned.1.call-update
  231.9 0.0 copy-start.11
  231.9 0.0 reduce-scatter.10.cloned.1.call-start
  232.0 132.1 %reduce-scatter.8.cloned.1.call-done = bf16[32,1,6,4096]{3,0,2,1:T(8,128)(2,1)} async-done(((bf16[256,1,6,4096]{3,0,2,1:T(8,128)(2,1)}), bf16[32,1,6,4096]{3,0,2,1:T(8,128)(2,1)}) %reduce-scatter.8.cloned.1.call-update) | async-done | bytes 1572880 | tf_op jit(solution)/shard_map/reduce_scatter | solution.py:136
  364.1 2.7 copy.58
  366.8 0.0 reduce-scatter.10.cloned.1.call-update
  366.8 26.2 %reduce-scatter.10.cloned.1.call-done = bf16[8,24576]{1,0:T(8,128)(2,1)} async-done(((bf16[32,24576]{1,0:T(8,128)(2,1)}), bf16[8,24576]{1,0:T(8,128)(2,1)}) %reduce-scatter.10.cloned.1.call-update) | async-done | bytes 393232
  393.0 1.2 copy.43
  394.2 15.1 %all_to_all.11 = bf16[8,1,6,4096]{3,2,1,0:T(8,128)(2,1)S(1)} all-to-all(bf16[8,1,6,4096]{3,2,1,0:T(8,128)(2,1)S(1)} %copy.43), channel_id=1, replica_groups=mesh['dp'=8,'expert'=8,'tensor'=4] {'expert'}, dimensions={0} | all-to-all | bytes 786432 | tf_op jit(solution)/shard_map/all_to_all | solution.py:141
  409.3 0.3 fusion.39
  409.6 0.7 fusion.56
  (50 shorter events, 0.3 us)
Async XLA Ops:
  6.5 206.1 %copy-start = (bf16[1,224,4096]{2,1,0:T(8,128)(2,1)S(1)}, bf16[1,224,4096]{2,1,0:T(8,128)(2,1)}, u32[]{:S(2)}) copy-start(bf16[1,224,4096]{2,1,0:T(8,128)(2,1)} %param.33) | copy-start | bytes 5505028
  6.5 61.6 %reduce-scatter.6.cloned.1.call-start = ((), (), s32[]{:S(2)}) async-start(), calls=%async_computation.5 | async-start | bytes 655360 | tf_op jit(solution)/shard_map/reduce_scatter | solution.py:192
  23.7 1.3 copy-start.1
  25.0 10.7 %slice-start = ((s8[4456448]{0:T(1024)(128)(4,1)}), s8[262144]{0:T(1024)(128)(4,1)S(1)}, s32[]{:S(2)}) async-start(s8[4456448]{0:T(1024)(128)(4,1)} %bitcast.215), calls=%async_computation.9 | async-start | bytes 524288
  32.5 0.8 copy-start.8
  32.5 0.8 copy-start.12
  32.5 2.6 copy-start.10
  32.6 2.9 copy-start.13
  32.6 3.1 slice-start.1
  33.4 2.7 copy-start.14
  33.4 2.8 copy-start.9
  33.4 3.0 slice-start.3
  35.7 3.6 slice-start.2
  35.7 3.6 copy-start.7
  36.4 3.8 copy-start.2
  39.3 2.5 copy-start.5
  39.3 3.8 copy-start.6
  39.3 3.8 copy-start.15
  39.3 28.8 %copy-start.3 = (bf16[16,4096]{1,0:T(8,128)(2,1)S(1)}, bf16[16,4096]{1,0:T(8,128)(2,1)}, u32[]{:S(2)}) copy-start(bf16[16,4096]{1,0:T(8,128)(2,1)} %param.17) | copy-start | bytes 393220
  41.8 163.3 %all-gather.2.cloned.1.call-start = ((), (), s32[]{:S(2)}) async-start(), calls=%async_computation.6 | async-start | bytes 12976128 | tf_op jit(solution)/shard_map/all_gather | solution.py:124
  87.4 276.7 %reduce-scatter.8.cloned.1.call-start = ((), (), s32[]{:S(2)}) async-start(), calls=%async_computation.7 | async-start | bytes 14155776 | tf_op jit(solution)/shard_map/reduce_scatter | solution.py:136
  231.9 177.3 %copy-start.11 = (f32[16,2]{0,1:T(2,128)S(1)}, f32[16,2]{0,1:T(2,128)}, u32[]{:S(2)}) copy-start(f32[16,2]{0,1:T(2,128)} %param.28) | copy-start | bytes 388
  231.9 177.7 %copy-start.4 = (bf16[16,4096]{1,0:T(8,128)(2,1)S(1)}, bf16[16,4096]{1,0:T(8,128)(2,1)}, u32[]{:S(2)}) copy-start(bf16[16,4096]{1,0:T(8,128)(2,1)} %reduce-scatter.6.cloned.1.call-done) | copy-start | bytes 393220
  231.9 161.0 %reduce-scatter.10.cloned.1.call-start = ((), (), s32[]{:S(2)}) async-start(), calls=%async_computation.8 | async-start | bytes 1966080
Sparse Core Ops, SparseCore 0:
  41.9 26.1 reduce-scatter.5
  87.5 117.5 all-gather.1
  232.0 131.9 reduce-scatter.7
  366.9 26.0 reduce-scatter.9

commit v3 on v2

--- a/solution.py
+++ b/solution.py
@@ -1,13 +1,150 @@
 from functools import reduce
+import functools
 import math
 
 import jax
 import jax.numpy as jnp
 from jax import lax
+from jax.experimental import pallas as pl
+from jax.experimental.pallas import tpu as pltpu
 from jax.sharding import PartitionSpec as P
 
 HD = 128
 PLACEMENT_MOST = 6
+
+
+MESH_ID = pl.DeviceIdType.MESH
+
+
+def ring_phase(n, me, step_to, own, chunk_lead, recv, send0, send_sems, recv_sems, first_sem, finish):
+    copies = []
+    for s in range(n - 1):
+        c = lax.rem(me + n * 2 - step_to[1] * (s + 1), n)
+        if s == 0:
+            for i in range(chunk_lead):
+                send0[i] = own(c, i).astype(send0.dtype)
+            src = send0
+        else:
+            copies[-1].wait_recv()
+            for i in range(chunk_lead):
+                recv[s - 1, i] = (own(c, i) + recv[s - 1, i].astype(jnp.float32)).astype(recv.dtype)
+            src = recv.at[s - 1]
+        copy = pltpu.make_async_remote_copy(
+            src_ref=src,
+            dst_ref=recv.at[s],
+            send_sem=send_sems.at[first_sem + s],
+            recv_sem=recv_sems.at[first_sem + s],
+            device_id=step_to[0],
+            device_id_type=MESH_ID,
+        )
+        copy.start()
+        copies.append(copy)
+        yield copies
+    copies[-1].wait_recv()
+    for i in range(chunk_lead):
+        finish(i, own(me, i) + recv[n - 2, i].astype(jnp.float32))
+    yield copies
+
+
+def moe_sum_kernel(n_dp, n_t, p_ref, o_ref, *scratch):
+    recv_sems, send_sems = scratch[-2], scratch[-1]
+    bufs = scratch[:-2]
+    me_dp = lax.axis_index("dp")
+    me_t = lax.axis_index("tensor")
+    me_e = lax.axis_index("expert")
+    width = o_ref.shape[1] // 4
+
+    def dp_dev(d):
+        return (lax.rem(me_dp + n_dp + d, n_dp), me_e, me_t)
+
+    def t_dev(d):
+        return (me_dp, me_e, lax.rem(me_t + n_t + d, n_t))
+
+    barrier = pltpu.get_barrier_semaphore()
+    for dev in (dp_dev(1), dp_dev(-1), t_dev(1), t_dev(-1)):
+        pl.semaphore_signal(barrier, 1, device_id=dev, device_id_type=MESH_ID)
+    pl.semaphore_wait(barrier, 4)
+
+    streams = []
+    sem_at = 0
+    for block in range(4):
+        cols = pl.ds(block * width, width)
+        direction = 1 if block % 2 == 0 else -1
+        r1, s1, acc, r2, s2 = bufs[block * 5: block * 5 + 5]
+        if block < 2:
+            first = (n_dp, me_dp, (dp_dev(direction), direction), n_t)
+            own1 = lambda c, i, cols=cols: p_ref[c, i, :, cols].astype(jnp.float32)
+            second = (n_t, me_t, (t_dev(direction), direction))
+        else:
+            first = (n_t, me_t, (t_dev(direction), direction), n_dp)
+            own1 = lambda c, i, cols=cols: p_ref[i, c, :, cols].astype(jnp.float32)
+            second = (n_dp, me_dp, (dp_dev(direction), direction))
+
+        def fin1(i, v, acc=acc):
+            acc[i] = v
+
+        def fin2(i, v, cols=cols):
+            o_ref[:, cols] = v.astype(o_ref.dtype)
+
+        own2 = lambda c, i, acc=acc: acc[c]
+
+        def stream(first=first, second=second, own1=own1, own2=own2, r1=r1, s1=s1, r2=r2, s2=s2,
+                   fin1=fin1, fin2=fin2, base=sem_at):
+            n1, me1, to1, lead = first
+            copies = []
+            for copies in ring_phase(n1, me1, to1, own1, lead, r1, s1, send_sems, recv_sems, base, fin1):
+                yield
+            done1 = copies
+            n2, me2, to2 = second
+            for copies in ring_phase(n2, me2, to2, own2, 1, r2, s2, send_sems, recv_sems, base + n1 - 1,
+                                     lambda i, v: fin2(i, v)):
+                yield
+            for copy in done1 + copies:
+                copy.wait_send()
+
+        streams.append(stream())
+        sem_at += n_dp + n_t - 2
+
+    live = list(streams)
+    while live:
+        nxt = []
+        for st in live:
+            try:
+                next(st)
+                nxt.append(st)
+            except StopIteration:
+                pass
+        live = nxt
+
+
+def moe_sum(partial, n_dp, n_t):
+    rows, model_width = partial.shape[2], partial.shape[3]
+    width = model_width // 4
+    scratch = []
+    for block in range(4):
+        if block < 2:
+            n1, lead, n2 = n_dp, n_t, n_t
+        else:
+            n1, lead, n2 = n_t, n_dp, n_dp
+        scratch += [
+            pltpu.VMEM((n1 - 1, lead, rows, width), jnp.bfloat16),
+            pltpu.VMEM((lead, rows, width), jnp.bfloat16),
+            pltpu.VMEM((lead, rows, width), jnp.float32),
+            pltpu.VMEM((n2 - 1, 1, rows, width), jnp.bfloat16),
+            pltpu.VMEM((1, rows, width), jnp.bfloat16),
+        ]
+    copies = 4 * (n_dp + n_t - 2)
+    scratch += [pltpu.SemaphoreType.DMA((copies,)), pltpu.SemaphoreType.DMA((copies,))]
+    return pl.pallas_call(
+        functools.partial(moe_sum_kernel, n_dp, n_t),
+        out_shape=jax.ShapeDtypeStruct((rows, model_width), jnp.bfloat16),
+        in_specs=[pl.BlockSpec(memory_space=pltpu.VMEM)],
+        out_specs=pl.BlockSpec(memory_space=pltpu.VMEM),
+        scratch_shapes=scratch,
+        compiler_params=pltpu.CompilerParams(
+            collective_id=0, has_side_effects=True, vmem_limit_bytes=60 * 1024 * 1024
+        ),
+    )(partial)
 
 
 def normalize(parts):
@@ -132,12 +269,10 @@
     partial_out = jnp.einsum(
         "qesf,efd->qesd", hidden, contract_matrices, preferred_element_type=jnp.float32
     ).astype(jnp.bfloat16)
-    summed = lax.psum_scatter(
-        lax.psum_scatter(partial_out, "dp", scatter_dimension=0, tiled=True),
-        "tensor",
-        scatter_dimension=0,
-        tiled=True,
-    )
+    n_dp, n_t = lax.axis_size("dp"), lax.axis_size("tensor")
+    summed = moe_sum(
+        partial_out.reshape(n_dp, n_t, -1, model_width), n_dp, n_t
+    ).reshape(holders, local_count, slot_count, model_width)
     arrived_back = lax.all_to_all(summed, "expert", split_axis=0, concat_axis=0, tiled=True)
     return arrived_back.reshape(specialist_index, slot_count, model_width)
 

time: 417 us -> 403 us (0.966)
  waiting for transfers between devices: 301 us -> 143 us
  Pallas kernels: 0 us -> 104 us
  local copies, waits for them, and re-layouts: 29 us -> 58.8 us
  blocking collectives: 30.8 us -> 37.1 us
    reduce_scatter x1 -> x0, waiting for transfers between devices: 132 us -> none  [expert_pass(): lax.psum_scatter(partial_out, 'dp', scatter_dimension=0, tiled=True)]
    pallas_call x0 -> x1, Pallas kernels: none -> 104 us  [moe_sum(): pl.pallas_call(functools.partial(moe_sum_kernel, n_dp, n_t), out_shape=ja...]
    unnamed x5 -> x2, waiting for transfers between devices: 26.2 us -> 0.03 us
    reshape x0 -> x2, local copies, waits for them, and re-layouts: none -> 19.9 us  [the longest x1 18.8 us: expert_pass(): partial_out.reshape(n_dp, n_t, -1, model_width)]
    convert_element_type x0 -> x1, local copies, waits for them, and re-layouts: none -> 13.8 us  [expert_pass(): partial_out = jnp.einsum('qesf,efd->qesd', hidden, contract_matrices, pre...]
    all_to_all x1, blocking collectives: 15.1 us -> 21.3 us  [expert_pass(): lax.all_to_all(summed, 'expert', split_axis=0, concat_axis=0, tiled=True)]
  transfers between devices with their start and end apart: 4 -> 2, of which waited for: 4 -> 2; matrix products, arithmetic and copies ran while one was open for 0% -> 0% of each run, Pallas kernels for 0% -> 0%
where the time goes in v3:
time: 403 us; the launch traced here: 402 us
  waiting for transfers between devices  143 us (35%)
  Pallas kernels  104 us (26%)
  local copies, waits for them, and re-layouts  58.8 us (15%)
  matrix products  39.1 us (10%)
  blocking collectives  37.1 us (9%)
  between operations  14.4 us (4%)
  other arithmetic  6.11 us (2%)
    all_gather x1, waiting for transfers between devices, expert_pass(): row_piece = lax.all_gather(arrived, ('dp', 'tensor'), axis=0, tiled=True)  118 us
    pallas_call x1, Pallas kernels, moe_sum(): pl.pallas_call(functools.partial(moe_sum_kernel, n_dp, n_t), out_shape=ja...  104 us
    reduce_scatter x1, waiting for transfers between devices, local(): lax.psum_scatter(jnp.dot(heads_out, attention_merge_matrix, preferred_ele...  24.7 us
    all_to_all x1, blocking collectives, expert_pass(): lax.all_to_all(summed, 'expert', split_axis=0, concat_axis=0, tiled=True)  21.3 us
    dot_general x1, matrix products, expert_pass(): jnp.einsum('qesf,efd->qesd', hidden, contract_matrices, preferred_element...  19.8 us
    reshape x1, local copies, waits for them, and re-layouts, expert_pass(): partial_out.reshape(n_dp, n_t, -1, model_width)  18.8 us
    all_to_all x1, blocking collectives, expert_pass(): lax.all_to_all(send.reshape(holders, local_count, slot_count, model_width...  15.8 us
    convert_element_type x1, local copies, waits for them, and re-layouts, expert_pass(): partial_out = jnp.einsum('qesf,efd->qesd', hidden, contract_matrices, pre...  13.8 us
  transfers between devices with their start and end apart: 2, of which 2 were waited for; matrix products, arithmetic and copies ran while one was open for 0% of the time, Pallas kernels for 0%

profile of v3, /device:TPU:1, one launch (start us, length us, event | category | flops | bytes accessed | tf_op | source)
XLA Modules:
  0.0 402.0 jit_solution(15826873496802579094)
XLA Ops:
  6.6 0.9 slice.44
  7.4 1.2 slice.49
  8.7 1.2 broadcast_compare_fusion.1
  9.8 0.7 compare_select_fusion
  10.5 1.3 slice_bitcast_fusion.5
  11.8 0.1 copy.36
  11.9 0.1 reshape.340
  12.0 1.3 slice_convert_fusion
  13.3 1.6 select_reduce_fusion.2
  14.8 8.8 %gather_fusion.1 = bf16[136,128,128]{2,1,0:T(8,128)(2,1)} fusion(bf16[40,128,128]{2,1,0:T(8,128)(2,1)} %bitcast.216, s32[1024]{0:T(1024)S(1)} %pad_clamp_fusion), kind=kCustom, calls=%fused_computation.1 | custom fusion | bytes 8913440 | tf_op jit(solution)/shard_map/gather | solution.py:175
  23.7 0.0 copy-start.2
  23.7 1.3 copy-done.2
  25.0 7.5 %gather_fusion = bf16[136,128,128]{2,1,0:T(8,128)(2,1)} fusion(bf16[40,128,128]{2,1,0:T(8,128)(2,1)S(1)} %bitcast.217, s32[1024]{0:T(1024)S(1)} %pad_clamp_fusion), kind=kCustom, calls=%fused_computation | custom fusion | bytes 8913440 | tf_op jit(solution)/shard_map/gather | solution.py:174
  32.5 0.0 copy-start.9
  32.6 0.0 copy-start.14
  32.6 0.0 slice-start.1
  32.6 0.8 copy-done.9
  33.4 1.7 select_reduce_fusion
  35.2 0.3 bitcast_reduce_fusion
  35.5 0.2 convolution_bitcast_fusion.2
  35.7 0.0 slice-done
  35.7 0.0 slice-done.1
  35.7 0.0 slice-start.2
  35.7 0.0 copy-start.8
  35.7 0.3 fusion.43
  36.1 0.1 broadcast_compare_fusion
  36.2 0.1 fusion.88
  36.4 0.0 copy-start.3
  36.4 1.3 select_reduce_fusion.1
  37.7 0.3 bitcast_reduce_fusion.1
  38.0 1.4 slice-done.2
  39.3 0.0 copy-start.4
  39.4 0.8 fusion.45
  40.1 1.6 convolution_convert_fusion
  41.8 0.0 reduce-scatter.2.cloned.1.call-update
  41.8 0.0 all-gather.2.cloned.1.call-start
  41.8 0.0 copy-done.6
  41.9 0.1 copy.42
  41.9 0.1 eq.56
  42.0 0.1 fusion.82
  42.8 0.1 reduce_window_sum.11
  42.8 0.2 select_reduce_fusion.3
  43.0 0.1 reduce_sum.82
  43.1 0.1 copy.43
  43.2 0.0 copy-done.16
  43.2 0.1 select_reduce_fusion.4
  43.3 24.7 %reduce-scatter.2.cloned.1.call-done = bf16[16,4096]{1,0:T(8,128)(2,1)} async-done(((bf16[64,4096]{1,0:T(8,128)(2,1)}), bf16[16,4096]{1,0:T(8,128)(2,1)}) %reduce-scatter.2.cloned.1.call-update) | async-done | bytes 131088 | tf_op jit(solution)/shard_map/reduce_scatter | solution.py:327
  68.1 1.1 fusion.53
  69.2 1.2 fusion.5
  70.4 0.2 copy.45
  70.6 15.8 %all_to_all.10 = bf16[8,1,6,4096]{3,2,1,0:T(8,128)(2,1)S(1)} all-to-all(bf16[8,1,6,4096]{3,2,1,0:T(8,128)(2,1)S(1)} %copy.45), channel_id=1, replica_groups=mesh['dp'=8,'expert'=8,'tensor'=4] {'expert'}, dimensions={0} | all-to-all | bytes 786432 | tf_op jit(solution)/shard_map/all_to_all | solution.py:254
  86.4 1.0 copy.46
  87.4 0.0 all-gather.2.cloned.1.call-update
  87.4 117.7 %all-gather.2.cloned.1.call-done = bf16[256,1,6,4096]{3,0,2,1:T(8,128)(2,1)} async-done(((bf16[8,1,6,4096]{3,0,2,1:T(8,128)(2,1)}), bf16[256,1,6,4096]{3,0,2,1:T(8,128)(2,1)}) %all-gather.2.cloned.1.call-update) | async-done | bytes 12582928 | tf_op jit(solution)/shard_map/all_gather | solution.py:261
  205.1 10.1 %fusion.9 = f32[256,1,6,224]{0,3,2,1:T(8,128)} fusion(bf16[1,224,4096]{2,1,0:T(8,128)(2,1)} %param.31, bf16[256,1,6,4096]{3,0,2,1:T(8,128)(2,1)} %all-gather.2.cloned.1.call-done), kind=kOutput, calls=%fused_computation.15 | convolution fusion | flops 2818572288 | bytes 15794176 | tf_op jit(solution)/shard_map/qesd,efd->qesf/dot_general | solution.py:262
  215.3 19.8 %convert_bitcast_fusion = bf16[256,1,6,4096]{3,0,2,1:T(8,128)(2,1)} fusion(bf16[1,224,4096]{2,1,0:T(8,128)(2,1)S(1)} %copy-done, bf16[1,224,4096]{2,1,0:T(8,128)(2,1)} %param.32, bf16[256,1,6,4096]{3,0,2,1:T(8,128)(2,1)} %all-gather.2.cloned.1.call-done, f32[256,1,6,224]{0,3,2,1:T(8,128)} %fusion.9), kind=kOutput, calls=%fused_computation.6 | convolution fusion | flops 5645500416 | bytes 30212096 | tf_op jit(solution)/shard_map/qesf,efd->qesd/dot_general | solution.py:269
  235.0 13.8 %copy.47 = bf16[256,1,6,4096]{3,2,0,1:T(8,128)(2,1)} copy(bf16[256,1,6,4096]{3,0,2,1:T(8,128)(2,1)} %convert_bitcast_fusion) | data formatting | bytes 25165824 | tf_op jit(solution)/shard_map/convert_element_type | solution.py:271
  248.8 18.8 %reshape.333.p_ref = bf16[8,4,48,4096]{3,2,1,0:T(8,128)(2,1)} reshape(bf16[256,1,6,4096]{3,2,0,1:T(8,128)(2,1)} %copy.47) | data formatting | bytes 25165824 | tf_op jit(solution)/shard_map/reshape | solution.py:274
  267.6 104.1 %shard_map.163 = bf16[48,4096]{1,0:T(8,128)(2,1)} custom-call(bf16[8,4,48,4096]{3,2,1,0:T(8,128)(2,1)} %reshape.333.p_ref), custom_call_target="tpu_custom_call" | custom-call | tf_op jit(solution)/shard_map/pallas_call | solution.py:138
  371.7 1.1 reshape.334
  372.8 21.3 %all_to_all.11 = bf16[8,1,6,4096]{3,2,1,0:T(8,128)(2,1)S(1)} all-to-all(bf16[8,1,6,4096]{3,2,1,0:T(8,128)(2,1)S(1)} %bitcast.218), channel_id=1, replica_groups=mesh['dp'=8,'expert'=8,'tensor'=4] {'expert'}, dimensions={0} | all-to-all | bytes 786432 | tf_op jit(solution)/shard_map/all_to_all | solution.py:276
  394.1 0.0 copy-done.12
  394.1 0.3 fusion.39
  394.5 0.7 fusion.56
  (48 shorter events, 0.3 us)
Async XLA Ops:
  6.5 208.7 %copy-start = (bf16[1,224,4096]{2,1,0:T(8,128)(2,1)S(1)}, bf16[1,224,4096]{2,1,0:T(8,128)(2,1)}, u32[]{:S(2)}) copy-start(bf16[1,224,4096]{2,1,0:T(8,128)(2,1)} %param.33) | copy-start | bytes 5505028
  6.5 61.5 %reduce-scatter.2.cloned.1.call-start = ((), (), s32[]{:S(2)}) async-start(), calls=%async_computation.3 | async-start | bytes 655360 | tf_op jit(solution)/shard_map/reduce_scatter | solution.py:327
  23.7 1.3 copy-start.2
  25.0 10.7 %slice-start = ((s8[4456448]{0:T(1024)(128)(4,1)}), s8[262144]{0:T(1024)(128)(4,1)S(1)}, s32[]{:S(2)}) async-start(s8[4456448]{0:T(1024)(128)(4,1)} %bitcast.212), calls=%async_computation.5 | async-start | bytes 524288
  32.5 0.8 copy-start.9
  32.5 0.8 copy-start.13
  32.5 2.6 copy-start.11
  32.6 2.9 copy-start.14
  32.6 3.1 slice-start.1
  33.4 2.7 copy-start.15
  33.4 2.8 copy-start.10
  33.4 3.0 slice-start.3
  35.7 3.6 slice-start.2
  35.7 3.6 copy-start.8
  36.4 3.8 copy-start.3
  39.3 2.5 copy-start.6
  39.3 3.8 copy-start.7
  39.3 3.8 copy-start.16
  39.3 28.7 %copy-start.4 = (bf16[16,4096]{1,0:T(8,128)(2,1)S(1)}, bf16[16,4096]{1,0:T(8,128)(2,1)}, u32[]{:S(2)}) copy-start(bf16[16,4096]{1,0:T(8,128)(2,1)} %param.17) | copy-start | bytes 393220
  41.8 163.3 %all-gather.2.cloned.1.call-start = ((), (), s32[]{:S(2)}) async-start(), calls=%async_computation.4 | async-start | bytes 12976128 | tf_op jit(solution)/shard_map/all_gather | solution.py:261
  267.6 126.5 %copy-start.12 = (f32[16,2]{0,1:T(2,128)S(1)}, f32[16,2]{0,1:T(2,128)}, u32[]{:S(2)}) copy-start(f32[16,2]{0,1:T(2,128)} %param.28) | copy-start | bytes 388
  267.6 126.9 %copy-start.5 = (bf16[16,4096]{1,0:T(8,128)(2,1)S(1)}, bf16[16,4096]{1,0:T(8,128)(2,1)}, u32[]{:S(2)}) copy-start(bf16[16,4096]{1,0:T(8,128)(2,1)} %reduce-scatter.2.cloned.1.call-done) | copy-start | bytes 393220
  267.6 127.6 %copy-start.1 = (bf16[1,224,4096]{2,1,0:T(8,128)(2,1)S(1)}, bf16[1,224,4096]{2,1,0:T(8,128)(2,1)}, u32[]{:S(2)}) copy-start(bf16[1,224,4096]{2,1,0:T(8,128)(2,1)} %param.33) | copy-start | bytes 5505028
Sparse Core Ops, SparseCore 0:
  41.9 26.1 reduce-scatter.1
  87.5 117.5 all-gather.1

commit v4 on v3

--- a/solution.py
+++ b/solution.py
@@ -249,30 +249,23 @@
 
 def expert_pass(send, gating_matrices, expand_matrices, contract_matrices):
     specialist_index, slot_count, model_width = send.shape
-    holders = lax.axis_size("expert")
     local_count = gating_matrices.shape[0]
-    arrived = lax.all_to_all(
-        send.reshape(holders, local_count, slot_count, model_width),
-        "expert",
-        split_axis=0,
-        concat_axis=0,
-        tiled=True,
-    )
+    flat = send.reshape(specialist_index * slot_count, model_width)
+    arrived = lax.all_to_all(flat, "expert", split_axis=0, concat_axis=0, tiled=True)
     row_piece = lax.all_gather(arrived, ("dp", "tensor"), axis=0, tiled=True)
-    gate_part = jnp.einsum(
-        "qesd,efd->qesf", row_piece, gating_matrices, preferred_element_type=jnp.float32
-    )
-    up_part = jnp.einsum(
-        "qesd,efd->qesf", row_piece, expand_matrices, preferred_element_type=jnp.float32
+    assert local_count == 1
+    gate_part = lax.dot_general(
+        row_piece, gating_matrices[0], (((1,), (1,)), ((), ())), preferred_element_type=jnp.float32
+    )
+    up_part = lax.dot_general(
+        row_piece, expand_matrices[0], (((1,), (1,)), ((), ())), preferred_element_type=jnp.float32
     )
     hidden = (jax.nn.silu(gate_part) * up_part).astype(jnp.bfloat16)
-    partial_out = jnp.einsum(
-        "qesf,efd->qesd", hidden, contract_matrices, preferred_element_type=jnp.float32
+    partial_out = jnp.dot(
+        hidden, contract_matrices[0], preferred_element_type=jnp.float32
     ).astype(jnp.bfloat16)
     n_dp, n_t = lax.axis_size("dp"), lax.axis_size("tensor")
-    summed = moe_sum(
-        partial_out.reshape(n_dp, n_t, -1, model_width), n_dp, n_t
-    ).reshape(holders, local_count, slot_count, model_width)
+    summed = moe_sum(partial_out.reshape(n_dp, n_t, -1, model_width), n_dp, n_t)
     arrived_back = lax.all_to_all(summed, "expert", split_axis=0, concat_axis=0, tiled=True)
     return arrived_back.reshape(specialist_index, slot_count, model_width)
 

time: 403 us -> 369 us (0.916)
  local copies, waits for them, and re-layouts: 58.8 us -> 26.1 us
    reshape x3 -> x0, local copies, waits for them, and re-layouts: 20.1 us -> none  [the longest x1 18.8 us: expert_pass(): partial_out.reshape(n_dp, n_t, -1, model_width)]
    convert_element_type x1, local copies, waits for them, and re-layouts: 13.8 us -> 0.23 us  [local(): send = jnp.einsum('nkes,nd->esd', table_main, normed, preferred_element_t...]
where the time goes in v4:
time: 369 us
  waiting for transfers between devices  143 us (39%)
  Pallas kernels  104 us (28%)
  matrix products  38.9 us (11%)
  blocking collectives  36.8 us (10%)
  local copies, waits for them, and re-layouts  26.1 us (7%)
  between operations  14.4 us (4%)
  other arithmetic  6.11 us (2%)
    all_gather x1, waiting for transfers between devices, expert_pass(): row_piece = lax.all_gather(arrived, ('dp', 'tensor'), axis=0, tiled=True)  118 us
    pallas_call x1, Pallas kernels, moe_sum(): pl.pallas_call(functools.partial(moe_sum_kernel, n_dp, n_t), out_shape=ja...  104 us
    reduce_scatter x1, waiting for transfers between devices, local(): lax.psum_scatter(jnp.dot(heads_out, attention_merge_matrix, preferred_ele...  24.7 us
    all_to_all x1, blocking collectives, expert_pass(): lax.all_to_all(summed, 'expert', split_axis=0, concat_axis=0, tiled=True)  21 us
    dot_general x1, matrix products, expert_pass(): jnp.dot(hidden, contract_matrices[0], preferred_element_type=jnp.float32)  19.6 us
    all_to_all x1, blocking collectives, expert_pass(): lax.all_to_all(flat, 'expert', split_axis=0, concat_axis=0, tiled=True)  15.8 us
    dot_general x1, matrix products, expert_pass(): lax.dot_general(row_piece, gating_matrices[0], (((1,), (1,)), ((), ())),...  10.1 us
    gather x1, local copies, waits for them, and re-layouts, attend(): page_values = value_pages[table]  8.82 us
  transfers between devices with their start and end apart: 2, of which 2 were waited for; matrix products, arithmetic and copies ran while one was open for 0% of the time, Pallas kernels for 0%

profile of v4, /device:TPU:1, one launch (start us, length us, event | category | flops | bytes accessed | tf_op | source)
XLA Modules:
  0.0 368.9 jit_solution(9792095037523021214)
XLA Ops:
  6.5 0.0 copy-start
  6.6 0.9 slice.44
  7.4 1.2 slice.49
  8.7 1.2 broadcast_compare_fusion.1
  9.8 0.7 compare_select_fusion
  10.5 1.3 slice_bitcast_fusion.5
  11.8 0.1 copy.35
  11.9 0.1 reshape.311
  12.0 1.3 slice_convert_fusion
  13.3 1.6 select_reduce_fusion.2
  14.8 8.8 %gather_fusion.1 = bf16[136,128,128]{2,1,0:T(8,128)(2,1)} fusion(bf16[40,128,128]{2,1,0:T(8,128)(2,1)} %bitcast.152, s32[1024]{0:T(1024)S(1)} %pad_clamp_fusion), kind=kCustom, calls=%fused_computation.1 | custom fusion | bytes 8913440 | tf_op jit(solution)/shard_map/gather | solution.py:175
  23.7 0.0 copy-start.1
  23.7 1.3 copy-done.1
  25.0 7.5 %gather_fusion = bf16[136,128,128]{2,1,0:T(8,128)(2,1)} fusion(bf16[40,128,128]{2,1,0:T(8,128)(2,1)S(1)} %bitcast.153, s32[1024]{0:T(1024)S(1)} %pad_clamp_fusion), kind=kCustom, calls=%fused_computation | custom fusion | bytes 8913440 | tf_op jit(solution)/shard_map/gather | solution.py:174
  32.5 0.0 copy-start.8
  32.6 0.0 copy-start.13
  32.6 0.0 slice-start.1
  32.6 0.8 copy-done.8
  33.4 1.7 select_reduce_fusion
  35.1 0.0 copy-done.10
  35.2 0.3 bitcast_reduce_fusion
  35.5 0.0 copy-done.13
  35.5 0.2 convolution_bitcast_fusion.2
  35.7 0.0 slice-start.2
  35.7 0.0 copy-start.7
  35.7 0.3 fusion.17
  36.1 0.0 copy-done.14
  36.1 0.1 broadcast_compare_fusion
  36.2 0.1 fusion.62
  36.4 0.0 copy-start.2
  36.4 1.3 select_reduce_fusion.1
  37.6 0.3 bitcast_reduce_fusion.1
  38.0 1.4 slice-done.2
  39.3 0.0 copy-done.7
  39.3 0.0 copy-start.3
  39.3 0.8 fusion.19
  40.1 1.6 convolution_convert_fusion.1
  41.8 0.0 reduce-scatter.2.cloned.1.call-update
  41.8 0.0 all-gather.2.cloned.1.call-start
  41.8 0.1 copy.41
  41.9 0.1 eq.56
  42.0 0.1 fusion.56
  42.8 0.1 reduce_window_sum.11
  42.8 0.2 select_reduce_fusion.3
  43.0 0.1 reduce_sum.82
  43.1 0.1 copy.42
  43.2 0.0 copy-done.15
  43.2 0.1 select_reduce_fusion.4
  43.3 24.7 %reduce-scatter.2.cloned.1.call-done = bf16[16,4096]{1,0:T(8,128)(2,1)} async-done(((bf16[64,4096]{1,0:T(8,128)(2,1)}), bf16[16,4096]{1,0:T(8,128)(2,1)}) %reduce-scatter.2.cloned.1.call-update) | async-done | bytes 131088 | tf_op jit(solution)/shard_map/reduce_scatter | solution.py:320
  68.1 1.1 fusion.27
  69.1 1.2 convolution_convert_fusion.2
  70.4 0.2 copy.44
  70.6 15.8 %all_to_all.18 = bf16[8,6,4096]{2,1,0:T(8,128)(2,1)S(1)} all-to-all(bf16[8,6,4096]{2,1,0:T(8,128)(2,1)S(1)} %copy.44), channel_id=1, replica_groups=mesh['dp'=8,'expert'=8,'tensor'=4] {'expert'}, dimensions={0} | all-to-all | bytes 786432 | tf_op jit(solution)/shard_map/all_to_all | solution.py:254
  86.4 0.9 all_to_all.13
  87.3 0.0 all-gather.2.cloned.1.call-update
  87.3 117.8 %all-gather.2.cloned.1.call-done = bf16[1536,4096]{1,0:T(8,128)(2,1)} async-done(((bf16[48,4096]{1,0:T(8,128)(2,1)}), bf16[1536,4096]{1,0:T(8,128)(2,1)}) %all-gather.2.cloned.1.call-update) | async-done | bytes 12582928 | tf_op jit(solution)/shard_map/all_gather | solution.py:255
  205.1 10.1 %fusion.5 = f32[1536,224]{0,1:T(8,128)} fusion(bf16[1536,4096]{1,0:T(8,128)(2,1)} %all-gather.2.cloned.1.call-done, bf16[1,224,4096]{2,1,0:T(8,128)(2,1)} %param.31), kind=kOutput, calls=%fused_computation.11 | convolution fusion | flops 2818572288 | bytes 15794176 | tf_op jit(solution)/shard_map/dot_general | solution.py:257
  215.2 19.6 %convolution_convert_fusion = bf16[1536,4096]{1,0:T(8,128)(2,1)} fusion(bf16[1536,4096]{1,0:T(8,128)(2,1)} %all-gather.2.cloned.1.call-done, bf16[1,224,4096]{2,1,0:T(8,128)(2,1)S(1)} %copy-done, bf16[1,224,4096]{2,1,0:T(8,128)(2,1)} %param.32, f32[1536,224]{0,1:T(8,128)} %fusion.5), kind=kOutput, calls=%fused_computation.2 | convolution fusion | flops 5645500416 | bytes 30212096 | tf_op jit(solution)/shard_map/dot_general | solution.py:264
  234.8 104.0 %shard_map.163 = bf16[48,4096]{1,0:T(8,128)(2,1)} custom-call(bf16[8,4,48,4096]{3,2,1,0:T(8,128)(2,1)} %bitcast.154), custom_call_target="tpu_custom_call" | custom-call | tf_op jit(solution)/shard_map/pallas_call | solution.py:138
  338.8 1.1 all_to_all.14
  339.9 21.0 %all_to_all.19 = bf16[8,6,4096]{2,1,0:T(8,128)(2,1)S(1)} all-to-all(bf16[8,6,4096]{2,1,0:T(8,128)(2,1)S(1)} %all_to_all.14), channel_id=1, replica_groups=mesh['dp'=8,'expert'=8,'tensor'=4] {'expert'}, dimensions={0} | all-to-all | bytes 786432 | tf_op jit(solution)/shard_map/all_to_all | solution.py:269
  360.9 0.0 copy-done.11
  360.9 0.3 fusion.13
  361.3 0.7 fusion.30
  (44 shorter events, 0.3 us)
Async XLA Ops:
  6.5 208.7 %copy-start = (bf16[1,224,4096]{2,1,0:T(8,128)(2,1)S(1)}, bf16[1,224,4096]{2,1,0:T(8,128)(2,1)}, u32[]{:S(2)}) copy-start(bf16[1,224,4096]{2,1,0:T(8,128)(2,1)} %param.33) | copy-start | bytes 5505028
  6.5 61.5 %reduce-scatter.2.cloned.1.call-start = ((), (), s32[]{:S(2)}) async-start(), calls=%async_computation.3 | async-start | bytes 655360 | tf_op jit(solution)/shard_map/reduce_scatter | solution.py:320
  23.7 1.3 copy-start.1
  25.0 10.7 %slice-start = ((s8[4456448]{0:T(1024)(128)(4,1)}), s8[262144]{0:T(1024)(128)(4,1)S(1)}, s32[]{:S(2)}) async-start(s8[4456448]{0:T(1024)(128)(4,1)} %bitcast.148), calls=%async_computation.5 | async-start | bytes 524288
  32.5 0.8 copy-start.8
  32.5 0.8 copy-start.12
  32.5 2.6 copy-start.10
  32.6 2.9 copy-start.13
  32.6 3.1 slice-start.1
  33.4 2.7 copy-start.14
  33.4 2.8 copy-start.9
  33.4 3.0 slice-start.3
  35.7 3.6 slice-start.2
  35.7 3.6 copy-start.7
  36.4 3.8 %copy-start.2 = (bf16[512,4096]{1,0:T(8,128)(2,1)S(1)}, bf16[512,4096]{1,0:T(8,128)(2,1)}, u32[]{:S(2)}) copy-start(bf16[512,4096]{1,0:T(8,128)(2,1)} %param.25) | copy-start | bytes 12582916
  39.3 2.5 copy-start.5
  39.3 3.8 %copy-start.6 = (bf16[4096]{0:T(1024)(128)(2,1)S(1)}, bf16[4096]{0:T(1024)(128)(2,1)}, u32[]{:S(2)}) copy-start(bf16[4096]{0:T(1024)(128)(2,1)} %param.26) | copy-start | bytes 24580
  39.3 3.8 %copy-start.15 = (s32[8]{0:T(128)S(1)}, s32[8]{0:T(128)}, u32[]{:S(2)}) copy-start(s32[8]{0:T(128)} %param.29) | copy-start | bytes 100
  39.3 28.7 %copy-start.3 = (bf16[16,4096]{1,0:T(8,128)(2,1)S(1)}, bf16[16,4096]{1,0:T(8,128)(2,1)}, u32[]{:S(2)}) copy-start(bf16[16,4096]{1,0:T(8,128)(2,1)} %param.17) | copy-start | bytes 393220
  41.8 163.3 %all-gather.2.cloned.1.call-start = ((), (), s32[]{:S(2)}) async-start(), calls=%async_computation.4 | async-start | bytes 12976128 | tf_op jit(solution)/shard_map/all_gather | solution.py:255
  234.8 126.2 %copy-start.11 = (f32[16,2]{0,1:T(2,128)S(1)}, f32[16,2]{0,1:T(2,128)}, u32[]{:S(2)}) copy-start(f32[16,2]{0,1:T(2,128)} %param.28) | copy-start | bytes 388
  234.8 126.5 %copy-start.4 = (bf16[16,4096]{1,0:T(8,128)(2,1)S(1)}, bf16[16,4096]{1,0:T(8,128)(2,1)}, u32[]{:S(2)}) copy-start(bf16[16,4096]{1,0:T(8,128)(2,1)} %reduce-scatter.2.cloned.1.call-done) | copy-start | bytes 393220
Sparse Core Ops, SparseCore 0:
  41.9 26.1 reduce-scatter.1
  87.4 117.5 all-gather.1

commit v5 on v4

--- a/solution.py
+++ b/solution.py
@@ -117,6 +117,123 @@
         live = nxt
 
 
+def gather_phase(n, me, step_to, chunk, send_sems, recv_sems, first_sem):
+    copies = []
+    for s in range(n - 1):
+        c = lax.rem(me + n * 2 - step_to[1] * s, n)
+        if s > 0:
+            copies[-1].wait_recv()
+        copy = pltpu.make_async_remote_copy(
+            src_ref=chunk(c),
+            dst_ref=chunk(c),
+            send_sem=send_sems.at[first_sem + s],
+            recv_sem=recv_sems.at[first_sem + s],
+            device_id=step_to[0],
+            device_id_type=MESH_ID,
+        )
+        copy.start()
+        copies.append(copy)
+        yield copies
+    copies[-1].wait_recv()
+    yield copies
+
+
+def row_gather_kernel(n_dp, n_t, x_ref, o_ref, *scratch):
+    recv_sems, send_sems = scratch[-2], scratch[-1]
+    bufs = scratch[:-2]
+    me_dp = lax.axis_index("dp")
+    me_t = lax.axis_index("tensor")
+    me_e = lax.axis_index("expert")
+    rows = x_ref.shape[0]
+    width = x_ref.shape[1] // 4
+
+    def dp_dev(d):
+        return (lax.rem(me_dp + n_dp + d, n_dp), me_e, me_t)
+
+    def t_dev(d):
+        return (me_dp, me_e, lax.rem(me_t + n_t + d, n_t))
+
+    for block in range(4):
+        cols = pl.ds(block * width, width)
+        if block < 2:
+            bufs[block][me_t, me_dp] = x_ref[:, cols]
+        else:
+            bufs[block][me_dp, me_t] = x_ref[:, cols]
+
+    barrier = pltpu.get_barrier_semaphore()
+    for dev in (dp_dev(1), dp_dev(-1), t_dev(1), t_dev(-1)):
+        pl.semaphore_signal(barrier, 1, device_id=dev, device_id_type=MESH_ID)
+    pl.semaphore_wait(barrier, 4)
+
+    streams = []
+    sem_at = 0
+    for block in range(4):
+        direction = 1 if block % 2 == 0 else -1
+        g = bufs[block]
+        if block < 2:
+            first = (n_dp, me_dp, (dp_dev(direction), direction), lambda c, g=g: g.at[me_t, c])
+            second = (n_t, me_t, (t_dev(direction), direction), lambda c, g=g: g.at[c])
+        else:
+            first = (n_t, me_t, (t_dev(direction), direction), lambda c, g=g: g.at[me_dp, c])
+            second = (n_dp, me_dp, (dp_dev(direction), direction), lambda c, g=g: g.at[c])
+
+        def stream(first=first, second=second, base=sem_at):
+            n1, me1, to1, chunk1 = first
+            copies = []
+            for copies in gather_phase(n1, me1, to1, chunk1, send_sems, recv_sems, base):
+                yield
+            done1 = copies
+            n2, me2, to2, chunk2 = second
+            for copies in gather_phase(n2, me2, to2, chunk2, send_sems, recv_sems, base + n1 - 1):
+                yield
+            for copy in done1 + copies:
+                copy.wait_send()
+
+        streams.append(stream())
+        sem_at += n_dp + n_t - 2
+
+    live = list(streams)
+    while live:
+        nxt = []
+        for st in live:
+            try:
+                next(st)
+                nxt.append(st)
+            except StopIteration:
+                pass
+        live = nxt
+
+    for block in range(4):
+        cols = pl.ds(block * width, width)
+        for d in range(n_dp):
+            for t in range(n_t):
+                piece = bufs[block][t, d] if block < 2 else bufs[block][d, t]
+                o_ref[pl.ds((d * n_t + t) * rows, rows), cols] = piece
+
+
+def row_gather(x, n_dp, n_t):
+    rows, model_width = x.shape
+    width = model_width // 4
+    scratch = [
+        pltpu.VMEM((n_t, n_dp, rows, width), jnp.bfloat16),
+        pltpu.VMEM((n_t, n_dp, rows, width), jnp.bfloat16),
+        pltpu.VMEM((n_dp, n_t, rows, width), jnp.bfloat16),
+        pltpu.VMEM((n_dp, n_t, rows, width), jnp.bfloat16),
+    ]
+    copies = 4 * (n_dp + n_t - 2)
+    scratch += [pltpu.SemaphoreType.DMA((copies,)), pltpu.SemaphoreType.DMA((copies,))]
+    return pl.pallas_call(
+        functools.partial(row_gather_kernel, n_dp, n_t),
+        out_shape=jax.ShapeDtypeStruct((n_dp * n_t * rows, model_width), jnp.bfloat16),
+        in_specs=[pl.BlockSpec(memory_space=pltpu.VMEM)],
+        out_specs=pl.BlockSpec(memory_space=pltpu.VMEM),
+        scratch_shapes=scratch,
+        compiler_params=pltpu.CompilerParams(
+            collective_id=1, has_side_effects=True, vmem_limit_bytes=60 * 1024 * 1024
+        ),
+    )(x)
+
+
 def moe_sum(partial, n_dp, n_t):
     rows, model_width = partial.shape[2], partial.shape[3]
     width = model_width // 4
@@ -252,7 +369,7 @@
     local_count = gating_matrices.shape[0]
     flat = send.reshape(specialist_index * slot_count, model_width)
     arrived = lax.all_to_all(flat, "expert", split_axis=0, concat_axis=0, tiled=True)
-    row_piece = lax.all_gather(arrived, ("dp", "tensor"), axis=0, tiled=True)
+    row_piece = row_gather(arrived, lax.axis_size("dp"), lax.axis_size("tensor"))
     assert local_count == 1
     gate_part = lax.dot_general(
         row_piece, gating_matrices[0], (((1,), (1,)), ((), ())), preferred_element_type=jnp.float32

time: 369 us -> 354 us (0.959)
  waiting for transfers between devices: 143 us -> 24.8 us
  Pallas kernels: 104 us -> 203 us
    all_gather x1 -> x0, waiting for transfers between devices: 118 us -> none  [expert_pass(): row_piece = lax.all_gather(arrived, ('dp', 'tensor'), axis=0, tiled=True)]
    pallas_call x0 -> x1, Pallas kernels: none -> 101 us  [row_gather(): pl.pallas_call(functools.partial(row_gather_kernel, n_dp, n_t), out_shape...]
  transfers between devices with their start and end apart: 2 -> 1, of which waited for: 2 -> 1; matrix products, arithmetic and copies ran while one was open for 0% -> 0% of each run, Pallas kernels for 0% -> 0%
where the time goes in v5:
time: 354 us; the launch traced here: 353 us
  Pallas kernels  203 us (57%)
  blocking collectives  39.7 us (11%)
  matrix products  38.9 us (11%)
  local copies, waits for them, and re-layouts  26.1 us (7%)
  waiting for transfers between devices  24.8 us (7%)
  between operations  14.4 us (4%)
  other arithmetic  6.11 us (2%)
    pallas_call x1, Pallas kernels, moe_sum(): pl.pallas_call(functools.partial(moe_sum_kernel, n_dp, n_t), out_shape=ja...  102 us
    pallas_call x1, Pallas kernels, row_gather(): pl.pallas_call(functools.partial(row_gather_kernel, n_dp, n_t), out_shape...  101 us
    reduce_scatter x1, waiting for transfers between devices, local(): lax.psum_scatter(jnp.dot(heads_out, attention_merge_matrix, preferred_ele...  24.8 us
    all_to_all x1, blocking collectives, expert_pass(): lax.all_to_all(summed, 'expert', split_axis=0, concat_axis=0, tiled=True)  24 us
    dot_general x1, matrix products, expert_pass(): jnp.dot(hidden, contract_matrices[0], preferred_element_type=jnp.float32)  19.6 us
    all_to_all x1, blocking collectives, expert_pass(): lax.all_to_all(flat, 'expert', split_axis=0, concat_axis=0, tiled=True)  15.8 us
    dot_general x1, matrix products, expert_pass(): lax.dot_general(row_piece, gating_matrices[0], (((1,), (1,)), ((), ())),...  10.2 us
    gather x1, local copies, waits for them, and re-layouts, attend(): page_values = value_pages[table]  8.83 us
  transfers between devices with their start and end apart: 1, of which 1 were waited for; matrix products, arithmetic and copies ran while one was open for 0% of the time, Pallas kernels for 0%

profile of v5, /device:TPU:1, one launch (start us, length us, event | category | flops | bytes accessed | tf_op | source)
XLA Modules:
  0.0 353.0 jit_solution(16890281078540119117)
XLA Ops:
  6.5 0.0 copy-start
  6.5 0.0 reduce-scatter.2.cloned.1.call-start
  6.6 0.9 slice.44
  7.4 1.2 slice.49
  8.7 1.2 broadcast_compare_fusion.1
  9.8 0.7 compare_select_fusion
  10.5 1.3 slice_bitcast_fusion.5
  11.8 0.1 copy.36
  11.9 0.1 reshape.311
  12.0 1.3 slice_convert_fusion
  13.3 1.6 select_reduce_fusion.2
  14.8 8.8 %gather_fusion.1 = bf16[136,128,128]{2,1,0:T(8,128)(2,1)} fusion(bf16[40,128,128]{2,1,0:T(8,128)(2,1)} %bitcast.152, s32[1024]{0:T(1024)S(1)} %pad_clamp_fusion), kind=kCustom, calls=%fused_computation.1 | custom fusion | bytes 8913440 | tf_op jit(solution)/shard_map/gather | solution.py:292
  23.7 0.0 copy-start.1
  23.7 1.3 copy-done.1
  25.0 7.5 %gather_fusion = bf16[136,128,128]{2,1,0:T(8,128)(2,1)} fusion(bf16[40,128,128]{2,1,0:T(8,128)(2,1)S(1)} %bitcast.153, s32[1024]{0:T(1024)S(1)} %pad_clamp_fusion), kind=kCustom, calls=%fused_computation | custom fusion | bytes 8913440 | tf_op jit(solution)/shard_map/gather | solution.py:291
  32.5 0.0 copy-start.8
  32.5 0.0 copy-start.12
  32.6 0.0 copy-start.10
  32.6 0.0 copy-start.13
  32.6 0.0 slice-start.1
  32.6 0.8 copy-done.8
  33.4 0.0 copy-done.12
  33.4 1.7 select_reduce_fusion
  35.1 0.0 copy-done.10
  35.2 0.3 bitcast_reduce_fusion
  35.5 0.0 copy-done.13
  35.5 0.2 convolution_bitcast_fusion.2
  35.7 0.0 slice-done
  35.7 0.0 slice-start.2
  35.7 0.0 copy-start.7
  35.7 0.3 fusion.17
  36.1 0.1 broadcast_compare_fusion
  36.2 0.1 fusion.62
  36.4 0.0 copy-start.2
  36.4 1.3 select_reduce_fusion.1
  37.7 0.3 bitcast_reduce_fusion.1
  38.0 1.4 slice-done.2
  39.3 0.0 copy-start.3
  39.4 0.8 fusion.19
  40.1 1.6 convolution_convert_fusion.1
  41.8 0.0 reduce-scatter.2.cloned.1.call-update
  41.8 0.1 copy.42
  41.9 0.1 eq.56
  42.0 0.1 fusion.56
  42.7 0.1 reduce_window_sum.11
  42.8 0.2 select_reduce_fusion.3
  43.0 0.1 reduce_sum.82
  43.0 0.1 copy.43
  43.1 0.0 copy-done.15
  43.2 0.1 select_reduce_fusion.4
  43.3 24.8 %reduce-scatter.2.cloned.1.call-done = bf16[16,4096]{1,0:T(8,128)(2,1)} async-done(((bf16[64,4096]{1,0:T(8,128)(2,1)}), bf16[16,4096]{1,0:T(8,128)(2,1)}) %reduce-scatter.2.cloned.1.call-update) | async-done | bytes 131088 | tf_op jit(solution)/shard_map/reduce_scatter | solution.py:437
  68.1 1.1 fusion.27
  69.1 1.2 convolution_convert_fusion.2
  70.4 0.2 copy.45
  70.6 15.8 %all_to_all.17 = bf16[8,6,4096]{2,1,0:T(8,128)(2,1)S(1)} all-to-all(bf16[8,6,4096]{2,1,0:T(8,128)(2,1)S(1)} %copy.45), channel_id=1, replica_groups=mesh['dp'=8,'expert'=8,'tensor'=4] {'expert'}, dimensions={0} | all-to-all | bytes 786432 | tf_op jit(solution)/shard_map/all_to_all | solution.py:371
  86.4 0.9 all_to_all.12.x_ref
  87.3 100.7 %shard_map.163 = bf16[1536,4096]{1,0:T(8,128)(2,1)} custom-call(bf16[48,4096]{1,0:T(8,128)(2,1)} %all_to_all.12.x_ref), custom_call_target="tpu_custom_call" | custom-call | tf_op jit(solution)/shard_map/pallas_call | solution.py:225
  188.0 10.2 %fusion.5 = f32[1536,224]{0,1:T(8,128)} fusion(bf16[1536,4096]{1,0:T(8,128)(2,1)} %shard_map.163, bf16[1,224,4096]{2,1,0:T(8,128)(2,1)} %param.31), kind=kOutput, calls=%fused_computation.11 | convolution fusion | flops 2818572288 | bytes 15794176 | tf_op jit(solution)/shard_map/dot_general | solution.py:374
  198.1 19.6 %convolution_convert_fusion = bf16[1536,4096]{1,0:T(8,128)(2,1)} fusion(bf16[1536,4096]{1,0:T(8,128)(2,1)} %shard_map.163, bf16[1,224,4096]{2,1,0:T(8,128)(2,1)S(1)} %copy-done, bf16[1,224,4096]{2,1,0:T(8,128)(2,1)} %param.32, f32[1536,224]{0,1:T(8,128)} %fusion.5), kind=kOutput, calls=%fused_computation.2 | convolution fusion | flops 5645500416 | bytes 30212096 | tf_op jit(solution)/shard_map/dot_general | solution.py:381
  217.7 102.3 %shard_map.164 = bf16[48,4096]{1,0:T(8,128)(2,1)} custom-call(bf16[8,4,48,4096]{3,2,1,0:T(8,128)(2,1)} %bitcast.154), custom_call_target="tpu_custom_call" | custom-call | tf_op jit(solution)/shard_map/pallas_call | solution.py:255
  320.0 1.1 all_to_all.13
  321.1 24.0 %all_to_all.18 = bf16[8,6,4096]{2,1,0:T(8,128)(2,1)S(1)} all-to-all(bf16[8,6,4096]{2,1,0:T(8,128)(2,1)S(1)} %all_to_all.13), channel_id=1, replica_groups=mesh['dp'=8,'expert'=8,'tensor'=4] {'expert'}, dimensions={0} | all-to-all | bytes 786432 | tf_op jit(solution)/shard_map/all_to_all | solution.py:386
  345.1 0.3 fusion.13
  345.4 0.7 fusion.30
  (42 shorter events, 0.3 us)
Async XLA Ops:
  6.5 191.6 %copy-start = (bf16[1,224,4096]{2,1,0:T(8,128)(2,1)S(1)}, bf16[1,224,4096]{2,1,0:T(8,128)(2,1)}, u32[]{:S(2)}) copy-start(bf16[1,224,4096]{2,1,0:T(8,128)(2,1)} %param.33) | copy-start | bytes 5505028
  6.5 61.5 %reduce-scatter.2.cloned.1.call-start = ((), (), s32[]{:S(2)}) async-start(), calls=%async_computation.3 | async-start | bytes 655360 | tf_op jit(solution)/shard_map/reduce_scatter | solution.py:437
  23.7 1.3 copy-start.1
  25.0 10.7 %slice-start = ((s8[4456448]{0:T(1024)(128)(4,1)}), s8[262144]{0:T(1024)(128)(4,1)S(1)}, s32[]{:S(2)}) async-start(s8[4456448]{0:T(1024)(128)(4,1)} %bitcast.148), calls=%async_computation.4 | async-start | bytes 524288
  32.5 0.8 copy-start.8
  32.5 0.8 copy-start.12
  32.6 2.6 copy-start.10
  32.6 2.9 copy-start.13
  32.6 3.1 slice-start.1
  33.4 2.7 copy-start.14
  33.4 2.8 copy-start.9
  33.4 3.0 slice-start.3
  35.7 3.6 %slice-start.2 = ((bf16[136,128,128]{2,1,0:T(8,128)(2,1)}), bf16[128,128,128]{2,1,0:T(8,128)(2,1)S(1)}, s32[]{:S(2)}) async-start(bf16[136,128,128]{2,1,0:T(8,128)(2,1)} %gather_fusion.1), calls=%async_computation.6 | async-start | bytes 8388608 | tf_op jit(solution)/shard_map/slice | solution.py:318
  35.7 3.6 %copy-start.7 = (f32[16,128]{1,0:T(8,128)S(1)}, f32[16,128]{1,0:T(8,128)}, u32[]{:S(2)}) copy-start(f32[16,128]{1,0:T(8,128)} %slice_convert_fusion) | copy-start | bytes 24580
  36.4 3.8 %copy-start.2 = (bf16[512,4096]{1,0:T(8,128)(2,1)S(1)}, bf16[512,4096]{1,0:T(8,128)(2,1)}, u32[]{:S(2)}) copy-start(bf16[512,4096]{1,0:T(8,128)(2,1)} %param.25) | copy-start | bytes 12582916
  39.3 2.5 copy-start.5
  39.3 3.8 %copy-start.6 = (bf16[4096]{0:T(1024)(128)(2,1)S(1)}, bf16[4096]{0:T(1024)(128)(2,1)}, u32[]{:S(2)}) copy-start(bf16[4096]{0:T(1024)(128)(2,1)} %param.26) | copy-start | bytes 24580
  39.3 3.8 %copy-start.15 = (s32[8]{0:T(128)S(1)}, s32[8]{0:T(128)}, u32[]{:S(2)}) copy-start(s32[8]{0:T(128)} %param.29) | copy-start | bytes 100
  39.3 28.7 %copy-start.3 = (bf16[16,4096]{1,0:T(8,128)(2,1)S(1)}, bf16[16,4096]{1,0:T(8,128)(2,1)}, u32[]{:S(2)}) copy-start(bf16[16,4096]{1,0:T(8,128)(2,1)} %param.17) | copy-start | bytes 393220
  217.7 127.4 %copy-start.11 = (f32[16,2]{0,1:T(2,128)S(1)}, f32[16,2]{0,1:T(2,128)}, u32[]{:S(2)}) copy-start(f32[16,2]{0,1:T(2,128)} %param.28) | copy-start | bytes 388
  217.7 127.7 %copy-start.4 = (bf16[16,4096]{1,0:T(8,128)(2,1)S(1)}, bf16[16,4096]{1,0:T(8,128)(2,1)}, u32[]{:S(2)}) copy-start(bf16[16,4096]{1,0:T(8,128)(2,1)} %reduce-scatter.2.cloned.1.call-done) | copy-start | bytes 393220
Sparse Core Ops, SparseCore 0:
  41.9 26.0 reduce-scatter.1

commit v6 on v5

--- a/solution.py
+++ b/solution.py
@@ -14,6 +14,62 @@
 
 
 MESH_ID = pl.DeviceIdType.MESH
+
+
+def plan_order(events, rate=50000.0, latency=1.5, per_step=0.3):
+    ready = [0.0] * len(events)
+    at = [0] * len(events)
+    free = {}
+    clock = 0.0
+    order = []
+    while True:
+        live = [i for i in range(len(events)) if at[i] < len(events[i])]
+        if not live:
+            return order, clock
+        i = min(live, key=lambda k: (ready[k], k))
+        clock = max(clock, ready[i]) + per_step
+        send = events[i][at[i]]
+        if send is None:
+            ready[i] = clock
+        else:
+            link, size = send
+            start = max(clock, free.get(link, 0.0))
+            free[link] = start + size / rate
+            ready[i] = free[link] + latency
+        order.append(i)
+        at[i] += 1
+
+
+def ring_events(n1, n2, link1, link2, size1, size2):
+    return [(link1, size1)] * (n1 - 1) + [None] + [(link2, size2)] * (n2 - 1) + [None]
+
+
+def split_plan(n_dp, n_t, rows, model_width, reduce):
+    best = None
+    for first_dp in range(128, model_width // 2, 128):
+        widths = [first_dp, first_dp, model_width // 2 - first_dp, model_width // 2 - first_dp]
+        events = []
+        for block, width in enumerate(widths):
+            unit = rows * width * 2
+            sign = "+" if block % 2 == 0 else "-"
+            if block < 2:
+                big1, big2 = (n_t * unit, unit) if reduce else (unit, n_dp * unit)
+                events.append(ring_events(n_dp, n_t, "z" + sign, "y" + sign, big1, big2))
+            else:
+                big1, big2 = (n_dp * unit, unit) if reduce else (unit, n_t * unit)
+                events.append(ring_events(n_t, n_dp, "y" + sign, "z" + sign, big1, big2))
+        order, finish = plan_order(events)
+        if best is None or finish < best[0]:
+            best = (finish, widths, order)
+    return best[1], best[2]
+
+
+def run_in_order(streams, order):
+    for i in order:
+        next(streams[i])
+    for st in streams:
+        for _ in st:
+            pass
 
 
 def ring_phase(n, me, step_to, own, chunk_lead, recv, send0, send_sems, recv_sems, first_sem, finish):
@@ -46,13 +102,12 @@
     yield copies
 
 
-def moe_sum_kernel(n_dp, n_t, p_ref, o_ref, *scratch):
+def moe_sum_kernel(n_dp, n_t, widths, order, p_ref, o_ref, *scratch):
     recv_sems, send_sems = scratch[-2], scratch[-1]
     bufs = scratch[:-2]
     me_dp = lax.axis_index("dp")
     me_t = lax.axis_index("tensor")
     me_e = lax.axis_index("expert")
-    width = o_ref.shape[1] // 4
 
     def dp_dev(d):
         return (lax.rem(me_dp + n_dp + d, n_dp), me_e, me_t)
@@ -68,7 +123,7 @@
     streams = []
     sem_at = 0
     for block in range(4):
-        cols = pl.ds(block * width, width)
+        cols = pl.ds(sum(widths[:block]), widths[block])
         direction = 1 if block % 2 == 0 else -1
         r1, s1, acc, r2, s2 = bufs[block * 5: block * 5 + 5]
         if block < 2:
@@ -105,16 +160,7 @@
         streams.append(stream())
         sem_at += n_dp + n_t - 2
 
-    live = list(streams)
-    while live:
-        nxt = []
-        for st in live:
-            try:
-                next(st)
-                nxt.append(st)
-            except StopIteration:
-                pass
-        live = nxt
+    run_in_order(streams, order)
 
 
 def gather_phase(n, me, step_to, chunk, send_sems, recv_sems, first_sem):
@@ -138,14 +184,13 @@
     yield copies
 
 
-def row_gather_kernel(n_dp, n_t, x_ref, o_ref, *scratch):
+def row_gather_kernel(n_dp, n_t, widths, order, x_ref, o_ref, *scratch):
     recv_sems, send_sems = scratch[-2], scratch[-1]
     bufs = scratch[:-2]
     me_dp = lax.axis_index("dp")
     me_t = lax.axis_index("tensor")
     me_e = lax.axis_index("expert")
     rows = x_ref.shape[0]
-    width = x_ref.shape[1] // 4
 
     def dp_dev(d):
         return (lax.rem(me_dp + n_dp + d, n_dp), me_e, me_t)
@@ -154,7 +199,7 @@
         return (me_dp, me_e, lax.rem(me_t + n_t + d, n_t))
 
     for block in range(4):
-        cols = pl.ds(block * width, width)
+        cols = pl.ds(sum(widths[:block]), widths[block])
         if block < 2:
             bufs[block][me_t, me_dp] = x_ref[:, cols]
         else:
@@ -192,19 +237,10 @@
         streams.append(stream())
         sem_at += n_dp + n_t - 2
 
-    live = list(streams)
-    while live:
-        nxt = []
-        for st in live:
-            try:
-                next(st)
-                nxt.append(st)
-            except StopIteration:
-                pass
-        live = nxt
+    run_in_order(streams, order)
 
     for block in range(4):
-        cols = pl.ds(block * width, width)
+        cols = pl.ds(sum(widths[:block]), widths[block])
         for d in range(n_dp):
             for t in range(n_t):
                 piece = bufs[block][t, d] if block < 2 else bufs[block][d, t]
@@ -213,17 +249,17 @@
 
 def row_gather(x, n_dp, n_t):
     rows, model_width = x.shape
-    width = model_width // 4
+    widths, order = split_plan(n_dp, n_t, rows, model_width, False)
     scratch = [
-        pltpu.VMEM((n_t, n_dp, rows, width), jnp.bfloat16),
-        pltpu.VMEM((n_t, n_dp, rows, width), jnp.bfloat16),
-        pltpu.VMEM((n_dp, n_t, rows, width), jnp.bfloat16),
-        pltpu.VMEM((n_dp, n_t, rows, width), jnp.bfloat16),
+        pltpu.VMEM((n_t, n_dp, rows, widths[0]), jnp.bfloat16),
+        pltpu.VMEM((n_t, n_dp, rows, widths[1]), jnp.bfloat16),
+        pltpu.VMEM((n_dp, n_t, rows, widths[2]), jnp.bfloat16),
+        pltpu.VMEM((n_dp, n_t, rows, widths[3]), jnp.bfloat16),
     ]
     copies = 4 * (n_dp + n_t - 2)
     scratch += [pltpu.SemaphoreType.DMA((copies,)), pltpu.SemaphoreType.DMA((copies,))]
     return pl.pallas_call(
-        functools.partial(row_gather_kernel, n_dp, n_t),
+        functools.partial(row_gather_kernel, n_dp, n_t, tuple(widths), tuple(order)),
         out_shape=jax.ShapeDtypeStruct((n_dp * n_t * rows, model_width), jnp.bfloat16),
         in_specs=[pl.BlockSpec(memory_space=pltpu.VMEM)],
         out_specs=pl.BlockSpec(memory_space=pltpu.VMEM),
@@ -236,9 +272,10 @@
 
 def moe_sum(partial, n_dp, n_t):
     rows, model_width = partial.shape[2], partial.shape[3]
-    width = model_width // 4
+    widths, order = split_plan(n_dp, n_t, rows, model_width, True)
     scratch = []
     for block in range(4):
+        width = widths[block]
         if block < 2:
             n1, lead, n2 = n_dp, n_t, n_t
         else:
@@ -253,7 +290,7 @@
     copies = 4 * (n_dp + n_t - 2)
     scratch += [pltpu.SemaphoreType.DMA((copies,)), pltpu.SemaphoreType.DMA((copies,))]
     return pl.pallas_call(
-        functools.partial(moe_sum_kernel, n_dp, n_t),
+        functools.partial(moe_sum_kernel, n_dp, n_t, tuple(widths), tuple(order)),
         out_shape=jax.ShapeDtypeStruct((rows, model_width), jnp.bfloat16),
         in_specs=[pl.BlockSpec(memory_space=pltpu.VMEM)],
         out_specs=pl.BlockSpec(memory_space=pltpu.VMEM),

time: 354 us -> 340 us (0.960)
  Pallas kernels: 203 us -> 189 us
    pallas_call x2, Pallas kernels: 203 us -> 189 us  [the longest x1 97.2 us: row_gather(): pl.pallas_call(functools.partial(row_gather_kernel, n_dp, n_t, tuple(widt...]
where the time goes in v6:
time: 340 us
  Pallas kernels  189 us (56%)
  blocking collectives  40.7 us (12%)
  matrix products  38.9 us (11%)
  local copies, waits for them, and re-layouts  26.1 us (8%)
  waiting for transfers between devices  24.8 us (7%)
  between operations  14.4 us (4%)
  other arithmetic  6.11 us (2%)
    pallas_call x1, Pallas kernels, row_gather(): pl.pallas_call(functools.partial(row_gather_kernel, n_dp, n_t, tuple(widt...  97.2 us
    pallas_call x1, Pallas kernels, moe_sum(): pl.pallas_call(functools.partial(moe_sum_kernel, n_dp, n_t, tuple(widths)...  91.4 us
    all_to_all x1, blocking collectives, expert_pass(): lax.all_to_all(summed, 'expert', split_axis=0, concat_axis=0, tiled=True)  25 us
    reduce_scatter x1, waiting for transfers between devices, local(): lax.psum_scatter(jnp.dot(heads_out, attention_merge_matrix, preferred_ele...  24.8 us
    dot_general x1, matrix products, expert_pass(): jnp.dot(hidden, contract_matrices[0], preferred_element_type=jnp.float32)  19.6 us
    all_to_all x1, blocking collectives, expert_pass(): lax.all_to_all(flat, 'expert', split_axis=0, concat_axis=0, tiled=True)  15.8 us
    dot_general x1, matrix products, expert_pass(): lax.dot_general(row_piece, gating_matrices[0], (((1,), (1,)), ((), ())),...  10.2 us
    gather x1, local copies, waits for them, and re-layouts, attend(): page_values = value_pages[table]  8.84 us
  transfers between devices with their start and end apart: 1, of which 1 were waited for; matrix products, arithmetic and copies ran while one was open for 0% of the time, Pallas kernels for 0%

profile of v6, /device:TPU:1, one launch (start us, length us, event | category | flops | bytes accessed | tf_op | source)
XLA Modules:
  0.0 339.6 jit_solution(8352364065580144736)
XLA Ops:
  6.5 0.0 copy-start
  6.5 0.0 reduce-scatter.2.cloned.1.call-start
  6.6 0.9 slice.44
  7.4 1.2 slice.49
  8.7 1.2 broadcast_compare_fusion.1
  9.8 0.7 compare_select_fusion
  10.5 1.3 slice_bitcast_fusion.5
  11.8 0.1 copy.36
  11.9 0.1 reshape.311
  12.0 1.3 slice_convert_fusion
  13.3 1.6 select_reduce_fusion.2
  14.8 8.8 %gather_fusion.1 = bf16[136,128,128]{2,1,0:T(8,128)(2,1)} fusion(bf16[40,128,128]{2,1,0:T(8,128)(2,1)} %bitcast.152, s32[1024]{0:T(1024)S(1)} %pad_clamp_fusion), kind=kCustom, calls=%fused_computation.1 | custom fusion | bytes 8913440 | tf_op jit(solution)/shard_map/gather | solution.py:329
  23.7 0.0 copy-start.1
  23.7 1.3 copy-done.1
  25.0 7.5 %gather_fusion = bf16[136,128,128]{2,1,0:T(8,128)(2,1)} fusion(bf16[40,128,128]{2,1,0:T(8,128)(2,1)S(1)} %bitcast.153, s32[1024]{0:T(1024)S(1)} %pad_clamp_fusion), kind=kCustom, calls=%fused_computation | custom fusion | bytes 8913440 | tf_op jit(solution)/shard_map/gather | solution.py:328
  32.5 0.0 copy-start.8
  32.6 0.0 copy-start.12
  32.6 0.0 copy-start.10
  32.6 0.0 copy-start.13
  32.6 0.0 slice-start.1
  32.6 0.8 copy-done.8
  33.4 0.0 copy-done.12
  33.4 1.7 select_reduce_fusion
  35.1 0.0 copy-done.10
  35.2 0.3 bitcast_reduce_fusion
  35.5 0.2 convolution_bitcast_fusion.2
  35.7 0.0 slice-start.2
  35.7 0.0 copy-start.7
  35.8 0.3 fusion.17
  36.1 0.1 broadcast_compare_fusion
  36.2 0.0 copy-done.9
  36.2 0.1 fusion.62
  36.4 0.0 copy-start.2
  36.4 1.3 select_reduce_fusion.1
  37.7 0.3 bitcast_reduce_fusion.1
  38.0 1.4 slice-done.2
  39.4 0.0 copy-start.3
  39.4 0.8 fusion.19
  40.2 1.6 convolution_convert_fusion.1
  41.8 0.0 reduce-scatter.2.cloned.1.call-update
  41.8 0.1 copy.42
  41.9 0.1 eq.56
  42.0 0.1 fusion.56
  42.7 0.1 reduce_window_sum.11
  42.8 0.2 select_reduce_fusion.3
  43.0 0.1 reduce_sum.82
  43.1 0.1 copy.43
  43.2 0.0 copy-done.15
  43.2 0.1 select_reduce_fusion.4
  43.3 24.8 %reduce-scatter.2.cloned.1.call-done = bf16[16,4096]{1,0:T(8,128)(2,1)} async-done(((bf16[64,4096]{1,0:T(8,128)(2,1)}), bf16[16,4096]{1,0:T(8,128)(2,1)}) %reduce-scatter.2.cloned.1.call-update) | async-done | bytes 131088 | tf_op jit(solution)/shard_map/reduce_scatter | solution.py:474
  68.1 1.1 fusion.27
  69.1 1.2 convolution_convert_fusion.2
  70.4 0.2 copy.45
  70.6 15.8 %all_to_all.17 = bf16[8,6,4096]{2,1,0:T(8,128)(2,1)S(1)} all-to-all(bf16[8,6,4096]{2,1,0:T(8,128)(2,1)S(1)} %copy.45), channel_id=1, replica_groups=mesh['dp'=8,'expert'=8,'tensor'=4] {'expert'}, dimensions={0} | all-to-all | bytes 786432 | tf_op jit(solution)/shard_map/all_to_all | solution.py:408
  86.4 0.9 all_to_all.12.x_ref
  87.3 97.2 %shard_map.163 = bf16[1536,4096]{1,0:T(8,128)(2,1)} custom-call(bf16[48,4096]{1,0:T(8,128)(2,1)} %all_to_all.12.x_ref), custom_call_target="tpu_custom_call" | custom-call | tf_op jit(solution)/shard_map/pallas_call | solution.py:261
  184.5 10.2 %fusion.5 = f32[1536,224]{0,1:T(8,128)} fusion(bf16[1536,4096]{1,0:T(8,128)(2,1)} %shard_map.163, bf16[1,224,4096]{2,1,0:T(8,128)(2,1)} %param.31), kind=kOutput, calls=%fused_computation.11 | convolution fusion | flops 2818572288 | bytes 15794176 | tf_op jit(solution)/shard_map/dot_general | solution.py:411
  194.6 19.6 %convolution_convert_fusion = bf16[1536,4096]{1,0:T(8,128)(2,1)} fusion(bf16[1536,4096]{1,0:T(8,128)(2,1)} %shard_map.163, bf16[1,224,4096]{2,1,0:T(8,128)(2,1)S(1)} %copy-done, bf16[1,224,4096]{2,1,0:T(8,128)(2,1)} %param.32, f32[1536,224]{0,1:T(8,128)} %fusion.5), kind=kOutput, calls=%fused_computation.2 | convolution fusion | flops 5645500416 | bytes 30212096 | tf_op jit(solution)/shard_map/dot_general | solution.py:418
  214.2 91.4 %shard_map.164 = bf16[48,4096]{1,0:T(8,128)(2,1)} custom-call(bf16[8,4,48,4096]{3,2,1,0:T(8,128)(2,1)} %bitcast.154), custom_call_target="tpu_custom_call" | custom-call | tf_op jit(solution)/shard_map/pallas_call | solution.py:292
  305.6 1.1 all_to_all.13
  306.8 25.0 %all_to_all.18 = bf16[8,6,4096]{2,1,0:T(8,128)(2,1)S(1)} all-to-all(bf16[8,6,4096]{2,1,0:T(8,128)(2,1)S(1)} %all_to_all.13), channel_id=1, replica_groups=mesh['dp'=8,'expert'=8,'tensor'=4] {'expert'}, dimensions={0} | all-to-all | bytes 786432 | tf_op jit(solution)/shard_map/all_to_all | solution.py:423
  331.7 0.0 copy-done.11
  331.7 0.3 fusion.13
  332.1 0.7 fusion.30
  (42 shorter events, 0.3 us)
Async XLA Ops:
  6.5 188.1 %copy-start = (bf16[1,224,4096]{2,1,0:T(8,128)(2,1)S(1)}, bf16[1,224,4096]{2,1,0:T(8,128)(2,1)}, u32[]{:S(2)}) copy-start(bf16[1,224,4096]{2,1,0:T(8,128)(2,1)} %param.33) | copy-start | bytes 5505028
  6.5 61.5 %reduce-scatter.2.cloned.1.call-start = ((), (), s32[]{:S(2)}) async-start(), calls=%async_computation.3 | async-start | bytes 655360 | tf_op jit(solution)/shard_map/reduce_scatter | solution.py:474
  23.7 1.3 copy-start.1
  25.0 10.7 %slice-start = ((s8[4456448]{0:T(1024)(128)(4,1)}), s8[262144]{0:T(1024)(128)(4,1)S(1)}, s32[]{:S(2)}) async-start(s8[4456448]{0:T(1024)(128)(4,1)} %bitcast.148), calls=%async_computation.4 | async-start | bytes 524288
  32.5 0.8 copy-start.8
  32.6 0.8 copy-start.12
  32.6 2.6 copy-start.10
  32.6 2.9 copy-start.13
  32.6 3.1 slice-start.1
  33.4 2.7 copy-start.14
  33.4 2.8 copy-start.9
  33.4 3.0 slice-start.3
  35.7 3.6 %slice-start.2 = ((bf16[136,128,128]{2,1,0:T(8,128)(2,1)}), bf16[128,128,128]{2,1,0:T(8,128)(2,1)S(1)}, s32[]{:S(2)}) async-start(bf16[136,128,128]{2,1,0:T(8,128)(2,1)} %gather_fusion.1), calls=%async_computation.6 | async-start | bytes 8388608 | tf_op jit(solution)/shard_map/slice | solution.py:355
  35.7 3.6 %copy-start.7 = (f32[16,128]{1,0:T(8,128)S(1)}, f32[16,128]{1,0:T(8,128)}, u32[]{:S(2)}) copy-start(f32[16,128]{1,0:T(8,128)} %slice_convert_fusion) | copy-start | bytes 24580
  36.4 3.8 %copy-start.2 = (bf16[512,4096]{1,0:T(8,128)(2,1)S(1)}, bf16[512,4096]{1,0:T(8,128)(2,1)}, u32[]{:S(2)}) copy-start(bf16[512,4096]{1,0:T(8,128)(2,1)} %param.25) | copy-start | bytes 12582916
  39.4 2.5 copy-start.5
  39.4 3.8 %copy-start.6 = (bf16[4096]{0:T(1024)(128)(2,1)S(1)}, bf16[4096]{0:T(1024)(128)(2,1)}, u32[]{:S(2)}) copy-start(bf16[4096]{0:T(1024)(128)(2,1)} %param.26) | copy-start | bytes 24580
  39.4 3.8 %copy-start.15 = (s32[8]{0:T(128)S(1)}, s32[8]{0:T(128)}, u32[]{:S(2)}) copy-start(s32[8]{0:T(128)} %param.29) | copy-start | bytes 100
  39.4 28.7 %copy-start.3 = (bf16[16,4096]{1,0:T(8,128)(2,1)S(1)}, bf16[16,4096]{1,0:T(8,128)(2,1)}, u32[]{:S(2)}) copy-start(bf16[16,4096]{1,0:T(8,128)(2,1)} %param.17) | copy-start | bytes 393220
  214.2 117.5 %copy-start.11 = (f32[16,2]{0,1:T(2,128)S(1)}, f32[16,2]{0,1:T(2,128)}, u32[]{:S(2)}) copy-start(f32[16,2]{0,1:T(2,128)} %param.28) | copy-start | bytes 388
  214.2 117.9 %copy-start.4 = (bf16[16,4096]{1,0:T(8,128)(2,1)S(1)}, bf16[16,4096]{1,0:T(8,128)(2,1)}, u32[]{:S(2)}) copy-start(bf16[16,4096]{1,0:T(8,128)(2,1)} %reduce-scatter.2.cloned.1.call-done) | copy-start | bytes 393220
Sparse Core Ops, SparseCore 0:
  41.9 26.0 reduce-scatter.1

commit v7 on v6

--- a/solution.py
+++ b/solution.py
@@ -102,7 +102,13 @@
     yield copies
 
 
-def moe_sum_kernel(n_dp, n_t, widths, order, p_ref, o_ref, *scratch):
+def block_product(h_ref, w_ref, chunk, cols, rows):
+    start = pl.multiple_of(chunk * rows, 16)
+    product = jnp.dot(h_ref[pl.ds(start, rows), :], w_ref[:, cols], preferred_element_type=jnp.float32)
+    return product.astype(jnp.bfloat16).astype(jnp.float32)
+
+
+def moe_sum_kernel(n_dp, n_t, widths, order, h_ref, w_ref, o_ref, *scratch):
     recv_sems, send_sems = scratch[-2], scratch[-1]
     bufs = scratch[:-2]
     me_dp = lax.axis_index("dp")
@@ -128,11 +134,11 @@
         r1, s1, acc, r2, s2 = bufs[block * 5: block * 5 + 5]
         if block < 2:
             first = (n_dp, me_dp, (dp_dev(direction), direction), n_t)
-            own1 = lambda c, i, cols=cols: p_ref[c, i, :, cols].astype(jnp.float32)
+            own1 = lambda c, i, cols=cols: block_product(h_ref, w_ref, c * n_t + i, cols, o_ref.shape[0])
             second = (n_t, me_t, (t_dev(direction), direction))
         else:
             first = (n_t, me_t, (t_dev(direction), direction), n_dp)
-            own1 = lambda c, i, cols=cols: p_ref[i, c, :, cols].astype(jnp.float32)
+            own1 = lambda c, i, cols=cols: block_product(h_ref, w_ref, i * n_t + c, cols, o_ref.shape[0])
             second = (n_dp, me_dp, (dp_dev(direction), direction))
 
         def fin1(i, v, acc=acc):
@@ -270,8 +276,8 @@
     )(x)
 
 
-def moe_sum(partial, n_dp, n_t):
-    rows, model_width = partial.shape[2], partial.shape[3]
+def moe_sum(hidden, down, n_dp, n_t):
+    rows, model_width = hidden.shape[0] // (n_dp * n_t), down.shape[1]
     widths, order = split_plan(n_dp, n_t, rows, model_width, True)
     scratch = []
     for block in range(4):
@@ -292,13 +298,13 @@
     return pl.pallas_call(
         functools.partial(moe_sum_kernel, n_dp, n_t, tuple(widths), tuple(order)),
         out_shape=jax.ShapeDtypeStruct((rows, model_width), jnp.bfloat16),
-        in_specs=[pl.BlockSpec(memory_space=pltpu.VMEM)],
+        in_specs=[pl.BlockSpec(memory_space=pltpu.VMEM)] * 2,
         out_specs=pl.BlockSpec(memory_space=pltpu.VMEM),
         scratch_shapes=scratch,
         compiler_params=pltpu.CompilerParams(
             collective_id=0, has_side_effects=True, vmem_limit_bytes=60 * 1024 * 1024
         ),
-    )(partial)
+    )(hidden, down)
 
 
 def normalize(parts):
@@ -415,11 +421,12 @@
         row_piece, expand_matrices[0], (((1,), (1,)), ((), ())), preferred_element_type=jnp.float32
     )
     hidden = (jax.nn.silu(gate_part) * up_part).astype(jnp.bfloat16)
-    partial_out = jnp.dot(
-        hidden, contract_matrices[0], preferred_element_type=jnp.float32
-    ).astype(jnp.bfloat16)
+    inner = hidden.shape[1]
+    padded = -(-inner // 128) * 128
+    hidden = jnp.pad(hidden, ((0, 0), (0, padded - inner)))
+    down = jnp.pad(contract_matrices[0], ((0, padded - inner), (0, 0)))
     n_dp, n_t = lax.axis_size("dp"), lax.axis_size("tensor")
-    summed = moe_sum(partial_out.reshape(n_dp, n_t, -1, model_width), n_dp, n_t)
+    summed = moe_sum(hidden, down, n_dp, n_t)
     arrived_back = lax.all_to_all(summed, "expert", split_axis=0, concat_axis=0, tiled=True)
     return arrived_back.reshape(specialist_index, slot_count, model_width)
 

time: 340 us -> 321 us (0.944)
  matrix products: 38.9 us -> 19.7 us
  blocking collectives: 40.7 us -> 26 us
  starting transfers between devices: 0.01 us -> 6.6 us
  waiting for transfers between devices: 24.8 us -> 31.2 us
  local copies, waits for them, and re-layouts: 26.1 us -> 32.3 us
    all_to_all x1 -> x0, blocking collectives: 15.8 us -> none  [expert_pass(): lax.all_to_all(flat, 'expert', split_axis=0, concat_axis=0, tiled=True)]
    dot_general x1, matrix products: 19.6 us -> 3.96 us  [expert_pass(): lax.dot_general(row_piece, expand_matrices[0], (((1,), (1,)), ((), ())),...]
    all_to_all x0 -> x1, starting transfers between devices: none -> 6.6 us  [expert_pass(): lax.all_to_all(flat, 'expert', split_axis=0, concat_axis=0, tiled=True)]
    all_to_all x0 -> x1, waiting for transfers between devices: none -> 6.4 us  [expert_pass(): lax.all_to_all(flat, 'expert', split_axis=0, concat_axis=0, tiled=True)]
    pad x0 -> x2, local copies, waits for them, and re-layouts: none -> 4.1 us  [the longest x1 3.08 us: expert_pass(): down = jnp.pad(contract_matrices[0], ((0, padded - inner), (0, 0)))]
    unnamed x39, local copies, waits for them, and re-layouts: 2.28 us -> 6.24 us
  transfers between devices with their start and end apart: 1 -> 2, of which waited for: 1 -> 2; matrix products, arithmetic and copies ran while one was open for 0% -> 1% of each run, Pallas kernels for 0% -> 0%
where the time goes in v7:
time: 321 us
  Pallas kernels  186 us (58%)
  local copies, waits for them, and re-layouts  32.3 us (10%)
  waiting for transfers between devices  31.2 us (10%)
  blocking collectives  26 us (8%)
  matrix products  19.7 us (6%)
  between operations  14.5 us (5%)
  starting transfers between devices  6.6 us (2%)
  other arithmetic  4.31 us (1%)
    pallas_call x1, Pallas kernels, row_gather(): pl.pallas_call(functools.partial(row_gather_kernel, n_dp, n_t, tuple(widt...  97.5 us
    pallas_call x1, Pallas kernels, moe_sum(): pl.pallas_call(functools.partial(moe_sum_kernel, n_dp, n_t, tuple(widths)...  88.6 us
    all_to_all x1, blocking collectives, expert_pass(): lax.all_to_all(summed, 'expert', split_axis=0, concat_axis=0, tiled=True)  26 us
    reduce_scatter x1, waiting for transfers between devices, local(): lax.psum_scatter(jnp.dot(heads_out, attention_merge_matrix, preferred_ele...  24.8 us
    gather x1, local copies, waits for them, and re-layouts, attend(): page_keys = key_pages[table]  8.84 us
    dot_general x1, matrix products, expert_pass(): lax.dot_general(row_piece, gating_matrices[0], (((1,), (1,)), ((), ())),...  7.79 us
    gather x1, local copies, waits for them, and re-layouts, attend(): page_values = value_pages[table]  7.52 us
    all_to_all x1, starting transfers between devices, expert_pass(): lax.all_to_all(flat, 'expert', split_axis=0, concat_axis=0, tiled=True)  6.6 us
  transfers between devices with their start and end apart: 2, of which 2 were waited for; matrix products, arithmetic and copies ran while one was open for 1% of the time, Pallas kernels for 0%

profile of v7, /device:TPU:1, one launch (start us, length us, event | category | flops | bytes accessed | tf_op | source)
XLA Modules:
  0.0 320.7 jit_solution(14263764548234383952)
XLA Ops:
  6.6 0.9 slice.44
  7.4 0.7 compare_select_fusion
  8.1 0.1 copy.56
  8.2 0.1 reshape.307
  8.3 1.2 slice.49
  9.6 0.7 broadcast_compare_fusion.1
  10.2 8.8 %gather_fusion = bf16[136,128,128]{2,1,0:T(8,128)(2,1)} fusion(bf16[40,128,128]{2,1,0:T(8,128)(2,1)} %bitcast.146, s32[1024]{0:T(1024)S(1)} %pad_clamp_fusion), kind=kCustom, calls=%fused_computation | custom fusion | bytes 8913440 | tf_op jit(solution)/shard_map/gather | solution.py:334
  19.1 0.0 copy-start.11
  19.1 0.0 copy-start.14
  19.1 0.0 copy-start.13
  19.1 0.0 copy-start.3
  19.1 2.2 copy-done.2
  21.3 0.3 select_reduce_fusion
  21.7 0.0 copy-done.14
  21.7 0.2 select_reduce_fusion.2
  21.9 0.7 copy-done.8
  22.7 0.3 bitcast_reduce_fusion
  23.0 0.2 convolution_bitcast_fusion.2
  23.2 7.5 %gather_fusion.1 = bf16[136,128,128]{2,1,0:T(8,128)(2,1)} fusion(bf16[40,128,128]{2,1,0:T(8,128)(2,1)S(1)} %bitcast.147, s32[1024]{0:T(1024)S(1)} %pad_clamp_fusion), kind=kCustom, calls=%fused_computation.1 | custom fusion | bytes 8913440 | tf_op jit(solution)/shard_map/gather | solution.py:335
  30.8 0.0 copy-start.15
  30.8 0.0 slice-start.1
  30.8 2.2 copy-done.1
  33.0 1.8 fusion.10
  34.9 0.1 broadcast_compare_fusion
  35.0 0.1 fusion.54
  35.1 0.0 copy-start.5
  35.1 1.3 select_reduce_fusion.1
  36.4 0.3 bitcast_reduce_fusion.1
  36.7 0.0 copy-start.9
  36.8 0.0 copy-start.10
  36.8 0.0 copy-start.17
  36.8 0.0 copy-start.6
  36.8 0.8 fusion.12
  37.6 1.6 convolution_convert_fusion
  39.2 0.0 reduce-scatter.2.cloned.1.call-update
  39.2 0.1 copy.62
  39.3 0.1 eq.56
  39.4 0.1 fusion.48
  39.5 0.1 reduce_window_sum.11
  39.5 0.2 select_reduce_fusion.3
  39.7 0.1 reduce_sum.82
  39.8 0.1 copy.63
  40.6 0.1 select_reduce_fusion.4
  40.8 24.8 %reduce-scatter.2.cloned.1.call-done = bf16[16,4096]{1,0:T(8,128)(2,1)} async-done(((bf16[64,4096]{1,0:T(8,128)(2,1)}), bf16[16,4096]{1,0:T(8,128)(2,1)}) %reduce-scatter.2.cloned.1.call-update) | async-done | bytes 131088 | tf_op jit(solution)/shard_map/reduce_scatter | solution.py:481
  65.5 1.1 fusion.19
  66.6 1.2 convolution_convert_fusion.1
  67.8 1.0 copy.65
  68.8 6.6 %all-to-all-start = ((bf16[8,6,4096]{2,1,0:T(8,128)(2,1)}), bf16[8,6,4096]{2,1,0:T(8,128)(2,1)S(1)}, u32[]{:S(2)}, u32[]{:S(2)}) async-start(bf16[8,6,4096]{2,1,0:T(8,128)(2,1)} %copy.65), calls=%async_computation.1 | async-start | bytes 1048576 | tf_op jit(solution)/shard_map/all_to_all | solution.py:414
  75.4 3.1 pad.9.w_ref
  78.5 6.4 %all-to-all-done = bf16[8,6,4096]{2,1,0:T(8,128)(2,1)S(1)} async-done(((bf16[8,6,4096]{2,1,0:T(8,128)(2,1)}), bf16[8,6,4096]{2,1,0:T(8,128)(2,1)S(1)}, u32[]{:S(2)}, u32[]{:S(2)}) %all-to-all-start) | async-done | bytes 393248 | tf_op jit(solution)/shard_map/all_to_all | solution.py:414
  84.9 0.9 all_to_all.12.x_ref
  85.8 97.5 %shard_map.163 = bf16[1536,4096]{1,0:T(8,128)(2,1)} custom-call(bf16[48,4096]{1,0:T(8,128)(2,1)} %all_to_all.12.x_ref), custom_call_target="tpu_custom_call" | custom-call | tf_op jit(solution)/shard_map/pallas_call | solution.py:267
  183.3 0.0 copy-start.16
  183.3 7.8 %fusion.3 = f32[1536,224]{1,0:T(8,128)S(1)} fusion(bf16[1536,4096]{1,0:T(8,128)(2,1)} %shard_map.163, bf16[1,224,4096]{2,1,0:T(8,128)(2,1)S(1)} %copy-done), kind=kOutput, calls=%fused_computation.9 | convolution fusion | flops 2818572288 | bytes 15794176 | tf_op jit(solution)/shard_map/dot_general | solution.py:417
  191.1 0.4 copy-done.4
  191.5 0.5 copy-done.16
  192.0 4.0 %fusion.1 = bf16[1536,224]{1,0:T(8,128)(2,1)S(1)} fusion(bf16[1536,4096]{1,0:T(8,128)(2,1)S(1)} %copy-done.4, bf16[1,224,4096]{2,1,0:T(8,128)(2,1)S(1)} %copy-done.16, f32[1536,224]{1,0:T(8,128)S(1)} %fusion.3), kind=kOutput, calls=%fused_computation.7 | convolution fusion | flops 2820636672 | bytes 16482304 | tf_op jit(solution)/shard_map/dot_general | solution.py:420
  196.0 0.0 copy-start.12
  196.0 1.0 pad.8.h_ref
  197.0 88.6 %shard_map.164 = bf16[48,4096]{1,0:T(8,128)(2,1)} custom-call(bf16[1536,256]{1,0:T(8,128)(2,1)} %pad.8.h_ref, bf16[256,4096]{1,0:T(8,128)(2,1)} %pad.9.w_ref), custom_call_target="tpu_custom_call" | custom-call | tf_op jit(solution)/shard_map/pallas_call | solution.py:298
  285.6 1.1 all_to_all.13
  286.8 26.0 %all_to_all.17 = bf16[8,6,4096]{2,1,0:T(8,128)(2,1)S(1)} all-to-all(bf16[8,6,4096]{2,1,0:T(8,128)(2,1)S(1)} %all_to_all.13), channel_id=1, replica_groups=mesh['dp'=8,'expert'=8,'tensor'=4] {'expert'}, dimensions={0} | all-to-all | bytes 786432 | tf_op jit(solution)/shard_map/all_to_all | solution.py:430
  312.8 0.3 fusion.6
  313.2 0.7 fusion.22
  (44 shorter events, 0.3 us)
Async XLA Ops:
  6.5 176.8 %copy-start = (bf16[1,224,4096]{2,1,0:T(8,128)(2,1)S(1)}, bf16[1,224,4096]{2,1,0:T(8,128)(2,1)}, u32[]{:S(2)}) copy-start(bf16[1,224,4096]{2,1,0:T(8,128)(2,1)} %param.31) | copy-start | bytes 5505028
  6.5 59.0 %reduce-scatter.2.cloned.1.call-start = ((), (), s32[]{:S(2)}) async-start(), calls=%async_computation.3 | async-start | bytes 655360 | tf_op jit(solution)/shard_map/reduce_scatter | solution.py:481
  19.1 2.3 copy-start.2
  19.1 2.3 copy-start.11
  19.1 2.6 copy-start.14
  19.1 3.9 %copy-start.13 = (bf16[64,128]{1,0:T(8,128)(2,1)S(1)}, bf16[64,128]{1,0:T(8,128)(2,1)}, u32[]{:S(2)}) copy-start(bf16[64,128]{1,0:T(8,128)(2,1)} %param.20) | copy-start | bytes 49156
  19.1 4.1 %copy-start.3 = (bf16[40,1,128,128]{3,2,1,0:T(8,128)(2,1)S(1)}, bf16[40,1,128,128]{3,2,1,0:T(8,128)(2,1)}, u32[]{:S(2)}) copy-start(bf16[40,1,128,128]{3,2,1,0:T(8,128)(2,1)} %param.22) | copy-start | bytes 3932164
  21.7 1.0 copy-start.8
  30.7 2.3 copy-start.1
  30.8 4.1 %copy-start.15 = (s32[17]{0:T(128)S(1)}, s32[17]{0:T(128)}, u32[]{:S(2)}) copy-start(s32[17]{0:T(128)} %param.24) | copy-start | bytes 208
  30.8 4.3 %slice-start.1 = ((bf16[136,128,128]{2,1,0:T(8,128)(2,1)}), bf16[128,128,128]{2,1,0:T(8,128)(2,1)S(1)}, s32[]{:S(2)}) async-start(bf16[136,128,128]{2,1,0:T(8,128)(2,1)} %gather_fusion), calls=%async_computation.5 | async-start | bytes 8388608 | tf_op jit(solution)/shard_map/slice | solution.py:343
  33.0 3.7 %slice-start = ((bf16[136,128,128]{2,1,0:T(8,128)(2,1)}), bf16[128,128,128]{2,1,0:T(8,128)(2,1)S(1)}, s32[]{:S(2)}) async-start(bf16[136,128,128]{2,1,0:T(8,128)(2,1)} %gather_fusion.1), calls=%async_computation.4 | async-start | bytes 8388608 | tf_op jit(solution)/shard_map/slice | solution.py:361
  35.1 2.4 copy-start.5
  36.7 2.5 copy-start.9
  36.8 3.8 %copy-start.10 = (bf16[4096]{0:T(1024)(128)(2,1)S(1)}, bf16[4096]{0:T(1024)(128)(2,1)}, u32[]{:S(2)}) copy-start(bf16[4096]{0:T(1024)(128)(2,1)} %param.26) | copy-start | bytes 24580
  36.8 3.8 %copy-start.17 = (s32[8]{0:T(128)S(1)}, s32[8]{0:T(128)}, u32[]{:S(2)}) copy-start(s32[8]{0:T(128)} %param.29) | copy-start | bytes 100
  36.8 28.7 %copy-start.6 = (bf16[16,4096]{1,0:T(8,128)(2,1)S(1)}, bf16[16,4096]{1,0:T(8,128)(2,1)}, u32[]{:S(2)}) copy-start(bf16[16,4096]{1,0:T(8,128)(2,1)} %param.17) | copy-start | bytes 393220
  68.8 16.1 %all-to-all-start = ((bf16[8,6,4096]{2,1,0:T(8,128)(2,1)}), bf16[8,6,4096]{2,1,0:T(8,128)(2,1)S(1)}, u32[]{:S(2)}, u32[]{:S(2)}) async-start(bf16[8,6,4096]{2,1,0:T(8,128)(2,1)} %copy.65), calls=%async_computation.1 | async-start | bytes 1048576 | tf_op jit(solution)/shard_map/all_to_all | solution.py:414
  183.3 8.2 %copy-start.4 = (bf16[1536,4096]{1,0:T(8,128)(2,1)S(1)}, bf16[1536,4096]{1,0:T(8,128)(2,1)}, u32[]{:S(2)}) copy-start(bf16[1536,4096]{1,0:T(8,128)(2,1)} %shard_map.163) | copy-start | bytes 37748740
  183.3 8.7 %copy-start.16 = (bf16[1,224,4096]{2,1,0:T(8,128)(2,1)S(1)}, bf16[1,224,4096]{2,1,0:T(8,128)(2,1)}, u32[]{:S(2)}) copy-start(bf16[1,224,4096]{2,1,0:T(8,128)(2,1)} %param.32) | copy-start | bytes 5505028
  196.0 116.8 %copy-start.12 = (f32[16,2]{0,1:T(2,128)S(1)}, f32[16,2]{0,1:T(2,128)}, u32[]{:S(2)}) copy-start(f32[16,2]{0,1:T(2,128)} %param.28) | copy-start | bytes 388
  196.0 117.2 %copy-start.7 = (bf16[16,4096]{1,0:T(8,128)(2,1)S(1)}, bf16[16,4096]{1,0:T(8,128)(2,1)}, u32[]{:S(2)}) copy-start(bf16[16,4096]{1,0:T(8,128)(2,1)} %reduce-scatter.2.cloned.1.call-done) | copy-start | bytes 393220
Sparse Core Ops, SparseCore 0:
  39.4 26.1 reduce-scatter.1

commit v8 on v7

--- a/solution.py
+++ b/solution.py
@@ -273,6 +273,109 @@
         compiler_params=pltpu.CompilerParams(
             collective_id=1, has_side_effects=True, vmem_limit_bytes=60 * 1024 * 1024
         ),
+    )(x)
+
+
+def head_sum_kernel(n_t, x_ref, o_ref, recv0, send0, recv1, send1, recv_sems, send_sems):
+    me_dp = lax.axis_index("dp")
+    me_e = lax.axis_index("expert")
+    me_t = lax.axis_index("tensor")
+    rows = o_ref.shape[0]
+    width = o_ref.shape[1] // 2
+
+    def t_dev(d):
+        return (me_dp, me_e, lax.rem(me_t + n_t + d, n_t))
+
+    barrier = pltpu.get_barrier_semaphore()
+    for dev in (t_dev(1), t_dev(-1)):
+        pl.semaphore_signal(barrier, 1, device_id=dev, device_id_type=MESH_ID)
+    pl.semaphore_wait(barrier, 2)
+    streams = []
+    for block, (recv, send0_buf) in enumerate(((recv0, send0), (recv1, send1))):
+        cols = pl.ds(block * width, width)
+        direction = 1 if block == 0 else -1
+        own = lambda c, i, cols=cols: x_ref[pl.ds(pl.multiple_of(c * rows, 8), rows), cols].astype(jnp.float32)
+
+        def finish(i, v, cols=cols):
+            o_ref[:, cols] = v.astype(o_ref.dtype)
+
+        def stream(own=own, recv=recv, send0_buf=send0_buf, finish=finish, direction=direction, base=block):
+            copies = []
+            for copies in ring_phase(n_t, me_t, (t_dev(direction), direction), own, 1, recv, send0_buf,
+                                     send_sems, recv_sems, base * (n_t - 1), finish):
+                yield
+            for copy in copies:
+                copy.wait_send()
+
+        streams.append(stream())
+    run_in_order(streams, [0, 1] * n_t)
+
+
+def head_sum(x, n_t):
+    rows, model_width = x.shape[0] // n_t, x.shape[1]
+    width = model_width // 2
+    scratch = []
+    for _ in range(2):
+        scratch += [
+            pltpu.VMEM((n_t - 1, 1, rows, width), jnp.bfloat16),
+            pltpu.VMEM((1, rows, width), jnp.bfloat16),
+        ]
+    copies = 2 * (n_t - 1)
+    scratch += [pltpu.SemaphoreType.DMA((copies,)), pltpu.SemaphoreType.DMA((copies,))]
+    return pl.pallas_call(
+        functools.partial(head_sum_kernel, n_t),
+        out_shape=jax.ShapeDtypeStruct((rows, model_width), jnp.bfloat16),
+        in_specs=[pl.BlockSpec(memory_space=pltpu.VMEM)],
+        out_specs=pl.BlockSpec(memory_space=pltpu.VMEM),
+        scratch_shapes=scratch,
+        compiler_params=pltpu.CompilerParams(collective_id=2, has_side_effects=True),
+    )(x)
+
+
+def expert_exchange_kernel(n_e, x_ref, o_ref, recv, recv_sems, send_sems):
+    me_dp = lax.axis_index("dp")
+    me_e = lax.axis_index("expert")
+    me_t = lax.axis_index("tensor")
+    barrier = pltpu.get_barrier_semaphore()
+    for k in range(1, n_e):
+        pl.semaphore_signal(barrier, 1, device_id=(me_dp, lax.rem(me_e + k, n_e), me_t),
+                            device_id_type=MESH_ID)
+    pl.semaphore_wait(barrier, n_e - 1)
+    copies = []
+    for k in range(1, n_e):
+        target = lax.rem(me_e + k, n_e)
+        copy = pltpu.make_async_remote_copy(
+            src_ref=x_ref.at[target],
+            dst_ref=recv.at[me_e],
+            send_sem=send_sems.at[k - 1],
+            recv_sem=recv_sems.at[k - 1],
+            device_id=(me_dp, target, me_t),
+            device_id_type=MESH_ID,
+        )
+        copy.start()
+        copies.append(copy)
+    o_ref[me_e] = x_ref[me_e]
+    for k in range(1, n_e):
+        copies[k - 1].wait_recv()
+        source = lax.rem(me_e + n_e - k, n_e)
+        o_ref[source] = recv[source]
+    for copy in copies:
+        copy.wait_send()
+
+
+def expert_exchange(x, collective):
+    n_e = x.shape[0]
+    return pl.pallas_call(
+        functools.partial(expert_exchange_kernel, n_e),
+        out_shape=jax.ShapeDtypeStruct(x.shape, x.dtype),
+        in_specs=[pl.BlockSpec(memory_space=pltpu.VMEM)],
+        out_specs=pl.BlockSpec(memory_space=pltpu.VMEM),
+        scratch_shapes=[
+            pltpu.VMEM(x.shape, x.dtype),
+            pltpu.SemaphoreType.DMA((n_e - 1,)),
+            pltpu.SemaphoreType.DMA((n_e - 1,)),
+        ],
+        compiler_params=pltpu.CompilerParams(collective_id=collective, has_side_effects=True),
     )(x)
 
 
@@ -410,8 +513,8 @@
 def expert_pass(send, gating_matrices, expand_matrices, contract_matrices):
     specialist_index, slot_count, model_width = send.shape
     local_count = gating_matrices.shape[0]
-    flat = send.reshape(specialist_index * slot_count, model_width)
-    arrived = lax.all_to_all(flat, "expert", split_axis=0, concat_axis=0, tiled=True)
+    assert local_count == 1
+    arrived = expert_exchange(send, 3).reshape(specialist_index * slot_count, model_width)
     row_piece = row_gather(arrived, lax.axis_size("dp"), lax.axis_size("tensor"))
     assert local_count == 1
     gate_part = lax.dot_general(
@@ -427,8 +530,7 @@
     down = jnp.pad(contract_matrices[0], ((0, padded - inner), (0, 0)))
     n_dp, n_t = lax.axis_size("dp"), lax.axis_size("tensor")
     summed = moe_sum(hidden, down, n_dp, n_t)
-    arrived_back = lax.all_to_all(summed, "expert", split_axis=0, concat_axis=0, tiled=True)
-    return arrived_back.reshape(specialist_index, slot_count, model_width)
+    return expert_exchange(summed.reshape(specialist_index, slot_count, model_width), 4)
 
 
 def local(
@@ -478,13 +580,11 @@
         sequence_sheet_map,
         stored_position_counts,
     )
-    own_attn = lax.psum_scatter(
+    own_attn = head_sum(
         jnp.dot(heads_out, attention_merge_matrix, preferred_element_type=jnp.float32).astype(
             jnp.bfloat16
         ),
-        "tensor",
-        scatter_dimension=0,
-        tiled=True,
+        lax.axis_size("tensor"),
     ).astype(jnp.float32)
     stream = (skip_stream_entry.astype(jnp.float32) + own_attn).astype(jnp.bfloat16)
     wide = stream.astype(jnp.float32)

time: 321 us -> 312 us (0.972)
  Pallas kernels: 186 us -> 247 us
  waiting for transfers between devices: 31.2 us -> 0 us
  blocking collectives: 26 us -> 0 us
  between operations: 14.5 us -> 1.12 us
  starting transfers between devices: 6.6 us -> 0 us
  matrix products: 19.7 us -> 23.8 us
    pallas_call x0 -> x3, Pallas kernels: none -> 53.7 us  [the longest x2 40.6 us: expert_exchange(): pl.pallas_call(functools.partial(expert_exchange_kernel, n_e), out_shape=...]
    all_to_all x1 -> x0, blocking collectives: 26 us -> none  [expert_pass(): lax.all_to_all(summed, 'expert', split_axis=0, concat_axis=0, tiled=True)]
    reduce_scatter x1 -> x0, waiting for transfers between devices: 24.8 us -> none  [local(): lax.psum_scatter(jnp.dot(heads_out, attention_merge_matrix, preferred_ele...]
    pallas_call x1, Pallas kernels: 97.5 us -> 104 us  [row_gather(): pl.pallas_call(functools.partial(row_gather_kernel, n_dp, n_t, tuple(widt...]
    all_to_all x1 -> x0, starting transfers between devices: 6.6 us -> none  [expert_pass(): lax.all_to_all(flat, 'expert', split_axis=0, concat_axis=0, tiled=True)]
    all_to_all x1 -> x0, waiting for transfers between devices: 6.4 us -> none  [expert_pass(): lax.all_to_all(flat, 'expert', split_axis=0, concat_axis=0, tiled=True)]
    slice x2 -> x1, local copies, waits for them, and re-layouts: 0.01 us -> 4.77 us  [attend(): page_keys[:single_count]]
    unnamed x39 -> x37, local copies, waits for them, and re-layouts: 6.24 us -> 1.6 us
  transfers between devices with their start and end apart: 2 -> 0, of which waited for: 2 -> 0; matrix products, arithmetic and copies ran while one was open for 1% -> 0% of each run, Pallas kernels for 0% -> 0%
where the time goes in v8:
time: 312 us
  Pallas kernels  247 us (79%)
  local copies, waits for them, and re-layouts  34.9 us (11%)
  matrix products  23.8 us (8%)
  other arithmetic  4.46 us (1%)
    pallas_call x1, Pallas kernels, row_gather(): pl.pallas_call(functools.partial(row_gather_kernel, n_dp, n_t, tuple(widt...  104 us
    pallas_call x1, Pallas kernels, moe_sum(): pl.pallas_call(functools.partial(moe_sum_kernel, n_dp, n_t, tuple(widths)...  89.2 us
    pallas_call x2, Pallas kernels, expert_exchange(): pl.pallas_call(functools.partial(expert_exchange_kernel, n_e), out_shape=...  40.6 us
    pallas_call x1, Pallas kernels, head_sum(): pl.pallas_call(functools.partial(head_sum_kernel, n_t), out_shape=jax.Sha...  13.1 us
    gather x1, local copies, waits for them, and re-layouts, attend(): page_keys = key_pages[table]  8.94 us
    dot_general x1, matrix products, expert_pass(): lax.dot_general(row_piece, gating_matrices[0], (((1,), (1,)), ((), ())),...  7.96 us
    gather x1, local copies, waits for them, and re-layouts, attend(): page_values = value_pages[table]  7.52 us

profile of v8, /device:TPU:1, one launch (start us, length us, event | category | flops | bytes accessed | tf_op | source)
XLA Modules:
  0.0 311.6 jit_solution(9769640165178910693)
XLA Ops:
  0.0 0.0 copy-start
  0.0 0.8 compare_select_fusion
  0.8 0.1 copy.56
  0.9 0.1 reshape.307
  1.0 0.0 copy-start.14
  1.0 0.0 copy-start.10
  1.0 0.0 copy-start.13
  1.1 0.0 copy-start.12
  1.1 0.0 copy-start.1
  1.1 8.9 %gather_fusion = bf16[136,128,128]{2,1,0:T(8,128)(2,1)} fusion(bf16[40,128,128]{2,1,0:T(8,128)(2,1)} %bitcast.146, s32[1024]{0:T(1024)S(1)} %pad_clamp_fusion), kind=kCustom, calls=%fused_computation | custom fusion | bytes 8913440 | tf_op jit(solution)/shard_map/gather | solution.py:437
  10.0 0.0 copy-done.14
  10.0 0.6 slice.49
  10.6 0.7 broadcast_compare_fusion.1
  11.3 0.0 copy-done.10
  11.3 1.3 select_reduce_fusion
  12.6 0.0 copy-start.7
  12.6 0.0 copy-done.13
  12.6 0.2 select_reduce_fusion.2
  12.8 0.7 copy-done.7
  13.6 0.3 bitcast_reduce_fusion
  13.9 0.0 copy-done.12
  13.9 0.2 convolution_bitcast_fusion.2
  14.1 0.0 copy-done.1
  14.1 7.5 %gather_fusion.1 = bf16[136,128,128]{2,1,0:T(8,128)(2,1)} fusion(bf16[40,128,128]{2,1,0:T(8,128)(2,1)S(1)} %bitcast.147, s32[1024]{0:T(1024)S(1)} %pad_clamp_fusion), kind=kCustom, calls=%fused_computation.1 | custom fusion | bytes 8913440 | tf_op jit(solution)/shard_map/gather | solution.py:438
  21.6 1.6 fusion.10
  23.2 4.8 %slice.62 = bf16[128,128,128]{2,1,0:T(8,128)(2,1)} slice(bf16[136,128,128]{2,1,0:T(8,128)(2,1)} %gather_fusion), slice={[0:128], [0:128], [0:128]} | slice | bytes 8388608 | tf_op jit(solution)/shard_map/slice | solution.py:446
  28.0 0.1 broadcast_compare_fusion
  28.1 3.5 %select_reduce_fusion.1 = (f32[16,4]{1,0:T(8,128)S(1)}, f32[16,8,128,4]{2,3,1,0:T(4,128)S(1)}) fusion(pred[16,8,128]{2,1,0:T(8,128)(4,1)S(1)} %broadcast_compare_fusion, bf16[16,8,128,128]{3,2,1,0:T(8,128)(2,1)} %bitcast.145, bf16[16,4,128,1]{2,1,0,3:T(4,128)(2,1)S(1)} %reshape.337), kind=kOutput, calls=%fused_computation.47 | convolution fusion | flops 16973760 | bytes 4489472 | tf_op jit(solution)/shard_map/rkgh,rmkph->rkgmp/dot_general | solution.py:443
  31.6 0.1 fusion.54
  31.8 0.3 bitcast_reduce_fusion.1
  32.1 0.0 slice-start
  32.1 0.0 copy-start.3
  32.1 3.4 %slice-done = bf16[128,128,128]{2,1,0:T(8,128)(2,1)S(1)} async-done(((bf16[136,128,128]{2,1,0:T(8,128)(2,1)}), bf16[128,128,128]{2,1,0:T(8,128)(2,1)S(1)}, s32[]{:S(2)}) %slice-start) | async-done | bytes 4194328 | tf_op jit(solution)/shard_map/slice | solution.py:464
  35.6 0.8 fusion.12
  36.4 0.0 copy-done.3
  36.4 1.7 convolution_convert_fusion.x_ref
  38.0 13.1 %shard_map.163 = bf16[16,4096]{1,0:T(8,128)(2,1)} custom-call(bf16[64,4096]{1,0:T(8,128)(2,1)} %convolution_convert_fusion.x_ref), custom_call_target="tpu_custom_call" | custom-call | tf_op jit(solution)/shard_map/pallas_call | solution.py:325
  51.1 0.0 copy-done.6
  51.1 1.1 fusion.19
  52.2 0.1 copy.62
  52.3 0.1 eq.56
  52.4 0.1 fusion.48
  52.4 0.1 reduce_window_sum.11
  52.5 0.2 select_reduce_fusion.3
  52.7 0.1 reduce_sum.82
  52.7 0.1 copy.63
  53.5 0.1 select_reduce_fusion.4
  53.7 1.2 convolution_convert_fusion.1
  54.9 1.0 copy.65.x_ref
  55.9 16.0 %shard_map.164 = bf16[8,6,4096]{2,1,0:T(8,128)(2,1)} custom-call(bf16[8,6,4096]{2,1,0:T(8,128)(2,1)} %copy.65.x_ref), custom_call_target="tpu_custom_call" | custom-call | tf_op jit(solution)/shard_map/pallas_call | solution.py:368
  72.0 1.9 reshape.301.x_ref
  73.9 104.4 %shard_map.165 = bf16[1536,4096]{1,0:T(8,128)(2,1)} custom-call(bf16[48,4096]{1,0:T(8,128)(2,1)} %reshape.301.x_ref), custom_call_target="tpu_custom_call" | custom-call | tf_op jit(solution)/shard_map/pallas_call | solution.py:267
  178.4 0.0 copy-start.15
  178.4 8.0 %fusion.3 = f32[1536,224]{1,0:T(8,128)S(1)} fusion(bf16[1536,4096]{1,0:T(8,128)(2,1)} %shard_map.165, bf16[1,224,4096]{2,1,0:T(8,128)(2,1)S(1)} %copy-done), kind=kOutput, calls=%fused_computation.9 | convolution fusion | flops 2818572288 | bytes 15794176 | tf_op jit(solution)/shard_map/dot_general | solution.py:520
  186.3 0.2 copy-done.2
  186.5 0.5 copy-done.15
  187.0 4.0 %fusion.1 = bf16[1536,224]{1,0:T(8,128)(2,1)S(1)} fusion(bf16[1536,4096]{1,0:T(8,128)(2,1)S(1)} %copy-done.2, bf16[1,224,4096]{2,1,0:T(8,128)(2,1)S(1)} %copy-done.15, f32[1536,224]{1,0:T(8,128)S(1)} %fusion.3), kind=kOutput, calls=%fused_computation.7 | convolution fusion | flops 2820636672 | bytes 16482304 | tf_op jit(solution)/shard_map/dot_general | solution.py:523
  191.0 1.0 pad.8.h_ref
  192.0 1.7 pad.9.w_ref
  193.7 89.2 %shard_map.166 = bf16[48,4096]{1,0:T(8,128)(2,1)} custom-call(bf16[1536,256]{1,0:T(8,128)(2,1)} %pad.8.h_ref, bf16[256,4096]{1,0:T(8,128)(2,1)} %pad.9.w_ref), custom_call_target="tpu_custom_call" | custom-call | tf_op jit(solution)/shard_map/pallas_call | solution.py:401
  282.9 1.9 reshape.302.x_ref
  284.8 24.6 %shard_map.167 = bf16[8,6,4096]{2,1,0:T(8,128)(2,1)} custom-call(bf16[8,6,4096]{2,1,0:T(8,128)(2,1)} %reshape.302.x_ref), custom_call_target="tpu_custom_call" | custom-call | tf_op jit(solution)/shard_map/pallas_call | solution.py:368
  309.5 1.4 fusion.6
  310.9 0.7 fusion.22
  (38 shorter events, 0.3 us)
Async XLA Ops:
  0.0 178.3 %copy-start = (bf16[1,224,4096]{2,1,0:T(8,128)(2,1)S(1)}, bf16[1,224,4096]{2,1,0:T(8,128)(2,1)}, u32[]{:S(2)}) copy-start(bf16[1,224,4096]{2,1,0:T(8,128)(2,1)} %param.31) | copy-start | bytes 5505028
  1.0 9.0 %copy-start.14 = (s32[17]{0:T(128)S(1)}, s32[17]{0:T(128)}, u32[]{:S(2)}) copy-start(s32[17]{0:T(128)} %param.24) | copy-start | bytes 208
  1.0 10.2 %copy-start.10 = (bf16[64,512]{1,0:T(8,128)(2,1)S(1)}, bf16[64,512]{1,0:T(8,128)(2,1)}, u32[]{:S(2)}) copy-start(bf16[64,512]{1,0:T(8,128)(2,1)} %param.18) | copy-start | bytes 196612
  1.0 11.6 %copy-start.13 = (bf16[64,128]{1,0:T(8,128)(2,1)S(1)}, bf16[64,128]{1,0:T(8,128)(2,1)}, u32[]{:S(2)}) copy-start(bf16[64,128]{1,0:T(8,128)(2,1)} %param.19) | copy-start | bytes 49156
  1.1 12.8 %copy-start.12 = (bf16[64,128]{1,0:T(8,128)(2,1)S(1)}, bf16[64,128]{1,0:T(8,128)(2,1)}, u32[]{:S(2)}) copy-start(bf16[64,128]{1,0:T(8,128)(2,1)} %param.20) | copy-start | bytes 49156
  1.1 13.0 %copy-start.1 = (bf16[40,1,128,128]{3,2,1,0:T(8,128)(2,1)S(1)}, bf16[40,1,128,128]{3,2,1,0:T(8,128)(2,1)}, u32[]{:S(2)}) copy-start(bf16[40,1,128,128]{3,2,1,0:T(8,128)(2,1)} %param.22) | copy-start | bytes 3932164
  12.6 1.0 copy-start.7
  32.1 3.5 %slice-start = ((bf16[136,128,128]{2,1,0:T(8,128)(2,1)}), bf16[128,128,128]{2,1,0:T(8,128)(2,1)S(1)}, s32[]{:S(2)}) async-start(bf16[136,128,128]{2,1,0:T(8,128)(2,1)} %gather_fusion.1), calls=%async_computation | async-start | bytes 8388608 | tf_op jit(solution)/shard_map/slice | solution.py:464
  32.1 4.3 %copy-start.3 = (bf16[512,4096]{1,0:T(8,128)(2,1)S(1)}, bf16[512,4096]{1,0:T(8,128)(2,1)}, u32[]{:S(2)}) copy-start(bf16[512,4096]{1,0:T(8,128)(2,1)} %param.25) | copy-start | bytes 12582916
  35.5 15.5 %copy-start.6 = (bf16[16,4096]{1,0:T(8,128)(2,1)S(1)}, bf16[16,4096]{1,0:T(8,128)(2,1)}, u32[]{:S(2)}) copy-start(bf16[16,4096]{1,0:T(8,128)(2,1)} %param.17) | copy-start | bytes 393220
  35.5 16.6 %copy-start.8 = (s32[16,2]{0,1:T(2,128)S(1)}, s32[16,2]{0,1:T(2,128)}, u32[]{:S(2)}) copy-start(s32[16,2]{0,1:T(2,128)} %param.27) | copy-start | bytes 388
  35.5 18.0 %copy-start.16 = (s32[8]{0:T(128)S(1)}, s32[8]{0:T(128)}, u32[]{:S(2)}) copy-start(s32[8]{0:T(128)} %param.29) | copy-start | bytes 100
  35.6 18.1 %copy-start.9 = (bf16[4096]{0:T(1024)(128)(2,1)S(1)}, bf16[4096]{0:T(1024)(128)(2,1)}, u32[]{:S(2)}) copy-start(bf16[4096]{0:T(1024)(128)(2,1)} %param.26) | copy-start | bytes 24580
  178.3 8.2 %copy-start.2 = (bf16[1536,4096]{1,0:T(8,128)(2,1)S(1)}, bf16[1536,4096]{1,0:T(8,128)(2,1)}, u32[]{:S(2)}) copy-start(bf16[1536,4096]{1,0:T(8,128)(2,1)} %shard_map.165) | copy-start | bytes 37748740
  178.4 8.7 %copy-start.15 = (bf16[1,224,4096]{2,1,0:T(8,128)(2,1)S(1)}, bf16[1,224,4096]{2,1,0:T(8,128)(2,1)}, u32[]{:S(2)}) copy-start(bf16[1,224,4096]{2,1,0:T(8,128)(2,1)} %param.32) | copy-start | bytes 5505028
  187.0 5.0 %copy-start.5 = (bf16[1,224,4096]{2,1,0:T(8,128)(2,1)S(1)}, bf16[1,224,4096]{2,1,0:T(8,128)(2,1)}, u32[]{:S(2)}) copy-start(bf16[1,224,4096]{2,1,0:T(8,128)(2,1)} %param.33) | copy-start | bytes 5505028
  192.0 117.4 %copy-start.11 = (f32[16,2]{0,1:T(2,128)S(1)}, f32[16,2]{0,1:T(2,128)}, u32[]{:S(2)}) copy-start(f32[16,2]{0,1:T(2,128)} %param.28) | copy-start | bytes 388
  192.0 118.8 %copy-start.4 = (bf16[16,4096]{1,0:T(8,128)(2,1)S(1)}, bf16[16,4096]{1,0:T(8,128)(2,1)}, u32[]{:S(2)}) copy-start(bf16[16,4096]{1,0:T(8,128)(2,1)} %shard_map.163) | copy-start | bytes 393220

commit v9 on v8

--- a/solution.py
+++ b/solution.py
@@ -379,6 +379,152 @@
     )(x)
 
 
+def gather_feed_phase(n, me, step_to, chunk, send_sems, recv_sems, first_sem, process, own_too):
+    copies = []
+    for s in range(n - 1):
+        c = lax.rem(me + n * 2 - step_to[1] * s, n)
+        if s > 0:
+            copies[-1].wait_recv()
+        copy = pltpu.make_async_remote_copy(
+            src_ref=chunk(c),
+            dst_ref=chunk(c),
+            send_sem=send_sems.at[first_sem + s],
+            recv_sem=recv_sems.at[first_sem + s],
+            device_id=step_to[0],
+            device_id_type=MESH_ID,
+        )
+        copy.start()
+        copies.append(copy)
+        if s > 0 or own_too:
+            process(c)
+        yield copies
+    copies[-1].wait_recv()
+    process(lax.rem(me + n * 2 - step_to[1] * (n - 1), n))
+    yield copies
+
+
+def expert_front_kernel(n_dp, n_t, widths, order, x_ref, wg_ref, wu_ref, o_ref, *scratch):
+    recv_sems, send_sems = scratch[-2], scratch[-1]
+    gate_acc, up_acc = scratch[-4], scratch[-3]
+    bufs = scratch[:-4]
+    me_dp = lax.axis_index("dp")
+    me_t = lax.axis_index("tensor")
+    me_e = lax.axis_index("expert")
+    rows = x_ref.shape[0]
+
+    def dp_dev(d):
+        return (lax.rem(me_dp + n_dp + d, n_dp), me_e, me_t)
+
+    def t_dev(d):
+        return (me_dp, me_e, lax.rem(me_t + n_t + d, n_t))
+
+    gate_acc[...] = jnp.zeros_like(gate_acc)
+    up_acc[...] = jnp.zeros_like(up_acc)
+    for block in range(4):
+        cols = pl.ds(sum(widths[:block]), widths[block])
+        if block < 2:
+            bufs[block][me_t, me_dp] = x_ref[:, cols]
+        else:
+            bufs[block][me_dp, me_t] = x_ref[:, cols]
+
+    barrier = pltpu.get_barrier_semaphore()
+    for dev in (dp_dev(1), dp_dev(-1), t_dev(1), t_dev(-1)):
+        pl.semaphore_signal(barrier, 1, device_id=dev, device_id_type=MESH_ID)
+    pl.semaphore_wait(barrier, 4)
+
+    def feed(piece, row_chunk, cols):
+        start = pl.multiple_of(row_chunk * rows, 16)
+        v = piece[...]
+        dims = (((1,), (1,)), ((), ()))
+        gate_acc[pl.ds(start, rows), :] += lax.dot_general(
+            v, wg_ref[:, cols], dims, preferred_element_type=jnp.float32)
+        up_acc[pl.ds(start, rows), :] += lax.dot_general(
+            v, wu_ref[:, cols], dims, preferred_element_type=jnp.float32)
+
+    streams = []
+    sem_at = 0
+    for block in range(4):
+        direction = 1 if block % 2 == 0 else -1
+        g = bufs[block]
+        cols = pl.ds(sum(widths[:block]), widths[block])
+        if block < 2:
+            def p1(c, g=g, cols=cols):
+                feed(g.at[me_t, c], c * n_t + me_t, cols)
+
+            def p2(c, g=g, cols=cols):
+                def body(d, carry):
+                    feed(g.at[c, d], d * n_t + c, cols)
+                    return carry
+                lax.fori_loop(0, n_dp, body, 0)
+            first = (n_dp, me_dp, (dp_dev(direction), direction), lambda c, g=g: g.at[me_t, c], p1)
+            second = (n_t, me_t, (t_dev(direction), direction), lambda c, g=g: g.at[c], p2)
+        else:
+            def p1(c, g=g, cols=cols):
+                feed(g.at[me_dp, c], me_dp * n_t + c, cols)
+
+            def p2(c, g=g, cols=cols):
+                def body(t, carry):
+                    feed(g.at[c, t], c * n_t + t, cols)
+                    return carry
+                lax.fori_loop(0, n_t, body, 0)
+            first = (n_t, me_t, (t_dev(direction), direction), lambda c, g=g: g.at[me_dp, c], p1)
+            second = (n_dp, me_dp, (dp_dev(direction), direction), lambda c, g=g: g.at[c], p2)
+
+        def stream(first=first, second=second, base=sem_at):
+            n1, me1, to1, chunk1, proc1 = first
+            copies = []
+            for copies in gather_feed_phase(n1, me1, to1, chunk1, send_sems, recv_sems, base, proc1, True):
+                yield
+            done1 = copies
+            n2, me2, to2, chunk2, proc2 = second
+            for copies in gather_feed_phase(n2, me2, to2, chunk2, send_sems, recv_sems, base + n1 - 1,
+                                            proc2, False):
+                yield
+            for copy in done1 + copies:
+                copy.wait_send()
+
+        streams.append(stream())
+        sem_at += n_dp + n_t - 2
+
+    run_in_order(streams, order)
+
+    tile = 128
+
+    def finish(i, carry):
+        at = pl.ds(pl.multiple_of(i * tile, tile), tile)
+        gate = gate_acc[at, :]
+        o_ref[at, :] = (gate / (1.0 + jnp.exp(-gate)) * up_acc[at, :]).astype(o_ref.dtype)
+        return carry
+
+    lax.fori_loop(0, o_ref.shape[0] // tile, finish, 0)
+
+
+def expert_front(x, gate_w, up_w, n_dp, n_t):
+    rows, model_width = x.shape
+    inner = gate_w.shape[0]
+    widths, order = split_plan(n_dp, n_t, rows, model_width, False)
+    scratch = [
+        pltpu.VMEM((n_t, n_dp, rows, widths[0]), jnp.bfloat16),
+        pltpu.VMEM((n_t, n_dp, rows, widths[1]), jnp.bfloat16),
+        pltpu.VMEM((n_dp, n_t, rows, widths[2]), jnp.bfloat16),
+        pltpu.VMEM((n_dp, n_t, rows, widths[3]), jnp.bfloat16),
+        pltpu.VMEM((n_dp * n_t * rows, inner), jnp.float32),
+        pltpu.VMEM((n_dp * n_t * rows, inner), jnp.float32),
+    ]
+    copies = 4 * (n_dp + n_t - 2)
+    scratch += [pltpu.SemaphoreType.DMA((copies,)), pltpu.SemaphoreType.DMA((copies,))]
+    return pl.pallas_call(
+        functools.partial(expert_front_kernel, n_dp, n_t, tuple(widths), tuple(order)),
+        out_shape=jax.ShapeDtypeStruct((n_dp * n_t * rows, inner), jnp.bfloat16),
+        in_specs=[pl.BlockSpec(memory_space=pltpu.VMEM)] * 3,
+        out_specs=pl.BlockSpec(memory_space=pltpu.VMEM),
+        scratch_shapes=scratch,
+        compiler_params=pltpu.CompilerParams(
+            collective_id=1, has_side_effects=True, vmem_limit_bytes=60 * 1024 * 1024
+        ),
+    )(x, gate_w, up_w)
+
+
 def moe_sum(hidden, down, n_dp, n_t):
     rows, model_width = hidden.shape[0] // (n_dp * n_t), down.shape[1]
     widths, order = split_plan(n_dp, n_t, rows, model_width, True)
@@ -515,19 +661,17 @@
     local_count = gating_matrices.shape[0]
     assert local_count == 1
     arrived = expert_exchange(send, 3).reshape(specialist_index * slot_count, model_width)
-    row_piece = row_gather(arrived, lax.axis_size("dp"), lax.axis_size("tensor"))
-    assert local_count == 1
-    gate_part = lax.dot_general(
-        row_piece, gating_matrices[0], (((1,), (1,)), ((), ())), preferred_element_type=jnp.float32
-    )
-    up_part = lax.dot_general(
-        row_piece, expand_matrices[0], (((1,), (1,)), ((), ())), preferred_element_type=jnp.float32
-    )
-    hidden = (jax.nn.silu(gate_part) * up_part).astype(jnp.bfloat16)
-    inner = hidden.shape[1]
+    inner = gating_matrices.shape[1]
     padded = -(-inner // 128) * 128
-    hidden = jnp.pad(hidden, ((0, 0), (0, padded - inner)))
-    down = jnp.pad(contract_matrices[0], ((0, padded - inner), (0, 0)))
+    widen = ((0, padded - inner), (0, 0))
+    hidden = expert_front(
+        arrived,
+        jnp.pad(gating_matrices[0], widen),
+        jnp.pad(expand_matrices[0], widen),
+        lax.axis_size("dp"),
+        lax.axis_size("tensor"),
+    )
+    down = jnp.pad(contract_matrices[0], widen)
     n_dp, n_t = lax.axis_size("dp"), lax.axis_size("tensor")
     summed = moe_sum(hidden, down, n_dp, n_t)
     return expert_exchange(summed.reshape(specialist_index, slot_count, model_width), 4)

time: 312 us -> 310 us (level)
  matrix products: 23.8 us -> 12.3 us
  Pallas kernels: 247 us -> 257 us
    dot_general x2 -> x0, matrix products: 11.9 us -> none  [the longest x1 7.96 us: expert_pass(): lax.dot_general(row_piece, gating_matrices[0], (((1,), (1,)), ((), ())),...]
    pallas_call x2, Pallas kernels: 40.6 us -> 46.5 us  [expert_exchange(): pl.pallas_call(functools.partial(expert_exchange_kernel, n_e), out_shape=...]
where the time goes in v9:
time: 310 us
  Pallas kernels  257 us (83%)
  local copies, waits for them, and re-layouts  34.4 us (11%)
  matrix products  12.3 us (4%)
  other arithmetic  4.42 us (1%)
    pallas_call x1, Pallas kernels, expert_front(): pl.pallas_call(functools.partial(expert_front_kernel, n_dp, n_t, tuple(wi...  107 us
    pallas_call x1, Pallas kernels, moe_sum(): pl.pallas_call(functools.partial(moe_sum_kernel, n_dp, n_t, tuple(widths)...  90.4 us
    pallas_call x2, Pallas kernels, expert_exchange(): pl.pallas_call(functools.partial(expert_exchange_kernel, n_e), out_shape=...  46.5 us
    pallas_call x1, Pallas kernels, head_sum(): pl.pallas_call(functools.partial(head_sum_kernel, n_t), out_shape=jax.Sha...  13.1 us
    gather x1, local copies, waits for them, and re-layouts, attend(): page_values = value_pages[table]  7.69 us
    gather x1, local copies, waits for them, and re-layouts, attend(): page_keys = key_pages[table]  7.51 us

profile of v9, /device:TPU:1, one launch (start us, length us, event | category | flops | bytes accessed | tf_op | source)
XLA Modules:
  0.0 309.6 jit_solution(431359832169260883)
XLA Ops:
  0.0 0.0 copy-start
  0.0 0.8 compare_select_fusion
  0.8 0.1 copy.47
  0.9 0.1 reshape.307
  1.0 0.3 copy-done
  1.3 0.0 copy-start.1
  1.4 7.5 %gather_fusion = bf16[136,128,128]{2,1,0:T(8,128)(2,1)} fusion(bf16[40,128,128]{2,1,0:T(8,128)(2,1)S(1)} %bitcast.138, s32[1024]{0:T(1024)S(1)} %pad_clamp_fusion), kind=kCustom, calls=%fused_computation | custom fusion | bytes 8913440 | tf_op jit(solution)/shard_map/gather | solution.py:583
  8.9 0.0 copy-done.14
  8.9 0.6 slice.49
  9.5 0.7 broadcast_compare_fusion.1
  10.1 0.0 copy-done.10
  10.1 1.3 select_reduce_fusion
  11.5 0.0 copy-done.13
  11.5 0.2 select_reduce_fusion.2
  11.7 0.3 bitcast_reduce_fusion
  12.0 0.0 copy-done.12
  12.0 0.8 convolution_bitcast_fusion.2
  12.9 0.0 copy-done.1
  12.9 7.7 %gather_fusion.1 = bf16[136,128,128]{2,1,0:T(8,128)(2,1)} fusion(bf16[40,128,128]{2,1,0:T(8,128)(2,1)S(1)} %bitcast.141, s32[1024]{0:T(1024)S(1)} %pad_clamp_fusion), kind=kCustom, calls=%fused_computation.1 | custom fusion | bytes 8913440 | tf_op jit(solution)/shard_map/gather | solution.py:584
  20.6 1.3 fusion.6
  21.9 4.8 %slice.62 = bf16[128,128,128]{2,1,0:T(8,128)(2,1)} slice(bf16[136,128,128]{2,1,0:T(8,128)(2,1)} %gather_fusion), slice={[0:128], [0:128], [0:128]} | slice | bytes 8388608 | tf_op jit(solution)/shard_map/slice | solution.py:592
  26.7 0.1 broadcast_compare_fusion
  26.8 3.5 %select_reduce_fusion.1 = (f32[16,4]{1,0:T(8,128)S(1)}, f32[16,8,128,4]{2,3,1,0:T(4,128)S(1)}) fusion(pred[16,8,128]{2,1,0:T(8,128)(4,1)S(1)} %broadcast_compare_fusion, bf16[16,8,128,128]{3,2,1,0:T(8,128)(2,1)} %bitcast.140, bf16[16,4,128,1]{2,1,0,3:T(4,128)(2,1)S(1)} %reshape.337), kind=kOutput, calls=%fused_computation.42 | convolution fusion | flops 16973760 | bytes 4489472 | tf_op jit(solution)/shard_map/rkgh,rmkph->rkgmp/dot_general | solution.py:589
  30.3 0.1 fusion.50
  30.4 0.3 bitcast_reduce_fusion.1
  30.8 0.0 slice-start
  30.8 0.0 copy-start.2
  30.8 2.2 slice-done
  33.0 0.8 fusion.8
  33.8 0.5 copy-done.2
  34.2 1.7 convolution_convert_fusion.x_ref
  35.9 13.1 %shard_map.163 = bf16[16,4096]{1,0:T(8,128)(2,1)} custom-call(bf16[64,4096]{1,0:T(8,128)(2,1)} %convolution_convert_fusion.x_ref), custom_call_target="tpu_custom_call" | custom-call | tf_op jit(solution)/shard_map/pallas_call | solution.py:325
  49.0 0.0 copy-done.7
  49.0 1.1 fusion.15
  50.1 0.0 copy-done.8
  50.1 0.1 copy.53
  50.2 0.1 eq.56
  50.3 0.1 fusion.44
  50.4 0.1 reduce_window_sum.11
  50.4 0.2 select_reduce_fusion.3
  50.6 0.1 reduce_sum.82
  50.7 0.1 copy.54
  51.4 0.0 copy-done.15
  51.5 0.1 select_reduce_fusion.4
  51.6 0.0 copy-done.9
  51.6 1.2 convolution_convert_fusion.1
  52.8 1.0 copy.56.x_ref
  53.9 16.0 %shard_map.164 = bf16[8,6,4096]{2,1,0:T(8,128)(2,1)} custom-call(bf16[8,6,4096]{2,1,0:T(8,128)(2,1)} %copy.56.x_ref), custom_call_target="tpu_custom_call" | custom-call | tf_op jit(solution)/shard_map/pallas_call | solution.py:368
  69.9 1.9 reshape.301.x_ref
  71.8 0.0 copy-done.4
  71.8 1.6 pad.10.wg_ref
  73.4 0.7 copy-done.5
  74.1 1.5 pad.11.wu_ref
  75.6 107.4 %shard_map.165.h_ref = bf16[1536,256]{1,0:T(8,128)(2,1)} custom-call(bf16[48,4096]{1,0:T(8,128)(2,1)} %reshape.301.x_ref, bf16[256,4096]{1,0:T(8,128)(2,1)} %pad.10.wg_ref, bf16[256,4096]{1,0:T(8,128)(2,1)} %pad.11.wu_ref), custom_call_target="tpu_custom_call" | custom-call | tf_op jit(solution)/shard_map/pallas_call | solution.py:516
  183.0 0.0 copy-done.6
  183.0 0.0 copy-start.11
  183.0 0.0 copy-start.3
  183.0 1.6 pad.12.w_ref
  184.6 90.4 %shard_map.166 = bf16[48,4096]{1,0:T(8,128)(2,1)} custom-call(bf16[1536,256]{1,0:T(8,128)(2,1)} %shard_map.165.h_ref, bf16[256,4096]{1,0:T(8,128)(2,1)} %pad.12.w_ref), custom_call_target="tpu_custom_call" | custom-call | tf_op jit(solution)/shard_map/pallas_call | solution.py:547
  275.0 1.9 reshape.302.x_ref
  276.9 30.5 %shard_map.167 = bf16[8,6,4096]{2,1,0:T(8,128)(2,1)} custom-call(bf16[8,6,4096]{2,1,0:T(8,128)(2,1)} %reshape.302.x_ref), custom_call_target="tpu_custom_call" | custom-call | tf_op jit(solution)/shard_map/pallas_call | solution.py:368
  307.5 0.0 copy-done.11
  307.5 1.4 fusion.2
  308.9 0.7 fusion.18
  (35 shorter events, 0.2 us)
Async XLA Ops:
  0.0 1.3 copy-start
  1.3 7.5 %copy-start.14 = (s32[17]{0:T(128)S(1)}, s32[17]{0:T(128)}, u32[]{:S(2)}) copy-start(s32[17]{0:T(128)} %param.24) | copy-start | bytes 208
  1.3 8.8 %copy-start.10 = (bf16[64,512]{1,0:T(8,128)(2,1)S(1)}, bf16[64,512]{1,0:T(8,128)(2,1)}, u32[]{:S(2)}) copy-start(bf16[64,512]{1,0:T(8,128)(2,1)} %param.18) | copy-start | bytes 196612
  1.3 10.1 %copy-start.13 = (bf16[64,128]{1,0:T(8,128)(2,1)S(1)}, bf16[64,128]{1,0:T(8,128)(2,1)}, u32[]{:S(2)}) copy-start(bf16[64,128]{1,0:T(8,128)(2,1)} %param.19) | copy-start | bytes 49156
  1.3 10.7 %copy-start.12 = (bf16[64,128]{1,0:T(8,128)(2,1)S(1)}, bf16[64,128]{1,0:T(8,128)(2,1)}, u32[]{:S(2)}) copy-start(bf16[64,128]{1,0:T(8,128)(2,1)} %param.20) | copy-start | bytes 49156
  1.3 11.5 %copy-start.1 = (bf16[40,1,128,128]{3,2,1,0:T(8,128)(2,1)S(1)}, bf16[40,1,128,128]{3,2,1,0:T(8,128)(2,1)}, u32[]{:S(2)}) copy-start(bf16[40,1,128,128]{3,2,1,0:T(8,128)(2,1)} %param.22) | copy-start | bytes 3932164
  30.8 2.2 slice-start
  30.8 3.5 %copy-start.2 = (bf16[512,4096]{1,0:T(8,128)(2,1)S(1)}, bf16[512,4096]{1,0:T(8,128)(2,1)}, u32[]{:S(2)}) copy-start(bf16[512,4096]{1,0:T(8,128)(2,1)} %param.25) | copy-start | bytes 12582916
  33.0 16.1 %copy-start.7 = (bf16[16,4096]{1,0:T(8,128)(2,1)S(1)}, bf16[16,4096]{1,0:T(8,128)(2,1)}, u32[]{:S(2)}) copy-start(bf16[16,4096]{1,0:T(8,128)(2,1)} %param.17) | copy-start | bytes 393220
  33.0 17.1 %copy-start.8 = (s32[16,2]{0,1:T(2,128)S(1)}, s32[16,2]{0,1:T(2,128)}, u32[]{:S(2)}) copy-start(s32[16,2]{0,1:T(2,128)} %param.27) | copy-start | bytes 388
  33.0 18.5 %copy-start.15 = (s32[8]{0:T(128)S(1)}, s32[8]{0:T(128)}, u32[]{:S(2)}) copy-start(s32[8]{0:T(128)} %param.29) | copy-start | bytes 100
  33.0 18.6 %copy-start.9 = (bf16[4096]{0:T(1024)(128)(2,1)S(1)}, bf16[4096]{0:T(1024)(128)(2,1)}, u32[]{:S(2)}) copy-start(bf16[4096]{0:T(1024)(128)(2,1)} %param.26) | copy-start | bytes 24580
  34.2 37.6 %copy-start.4 = (bf16[1,224,4096]{2,1,0:T(8,128)(2,1)S(1)}, bf16[1,224,4096]{2,1,0:T(8,128)(2,1)}, u32[]{:S(2)}) copy-start(bf16[1,224,4096]{2,1,0:T(8,128)(2,1)} %param.31) | copy-start | bytes 5505028
  71.8 2.3 copy-start.5
  74.0 108.9 %copy-start.6 = (bf16[1,224,4096]{2,1,0:T(8,128)(2,1)S(1)}, bf16[1,224,4096]{2,1,0:T(8,128)(2,1)}, u32[]{:S(2)}) copy-start(bf16[1,224,4096]{2,1,0:T(8,128)(2,1)} %param.33) | copy-start | bytes 5505028
  183.0 124.5 %copy-start.11 = (f32[16,2]{0,1:T(2,128)S(1)}, f32[16,2]{0,1:T(2,128)}, u32[]{:S(2)}) copy-start(f32[16,2]{0,1:T(2,128)} %param.28) | copy-start | bytes 388
  183.0 125.9 %copy-start.3 = (bf16[16,4096]{1,0:T(8,128)(2,1)S(1)}, bf16[16,4096]{1,0:T(8,128)(2,1)}, u32[]{:S(2)}) copy-start(bf16[16,4096]{1,0:T(8,128)(2,1)} %shard_map.163) | copy-start | bytes 393220

commit v10 on v9

--- a/solution.py
+++ b/solution.py
@@ -435,11 +435,8 @@
     def feed(piece, row_chunk, cols):
         start = pl.multiple_of(row_chunk * rows, 16)
         v = piece[...]
-        dims = (((1,), (1,)), ((), ()))
-        gate_acc[pl.ds(start, rows), :] += lax.dot_general(
-            v, wg_ref[:, cols], dims, preferred_element_type=jnp.float32)
-        up_acc[pl.ds(start, rows), :] += lax.dot_general(
-            v, wu_ref[:, cols], dims, preferred_element_type=jnp.float32)
+        gate_acc[pl.ds(start, rows), :] += jnp.dot(v, wg_ref[cols, :], preferred_element_type=jnp.float32)
+        up_acc[pl.ds(start, rows), :] += jnp.dot(v, wu_ref[cols, :], preferred_element_type=jnp.float32)
 
     streams = []
     sem_at = 0
@@ -501,7 +498,7 @@
 
 def expert_front(x, gate_w, up_w, n_dp, n_t):
     rows, model_width = x.shape
-    inner = gate_w.shape[0]
+    inner = gate_w.shape[1]
     widths, order = split_plan(n_dp, n_t, rows, model_width, False)
     scratch = [
         pltpu.VMEM((n_t, n_dp, rows, widths[0]), jnp.bfloat16),
@@ -666,8 +663,8 @@
     widen = ((0, padded - inner), (0, 0))
     hidden = expert_front(
         arrived,
-        jnp.pad(gating_matrices[0], widen),
-        jnp.pad(expand_matrices[0], widen),
+        jnp.pad(gating_matrices[0], widen).T,
+        jnp.pad(expand_matrices[0], widen).T,
         lax.axis_size("dp"),
         lax.axis_size("tensor"),
     )

time: 310 us -> 312 us (level)
  local copies, waits for them, and re-layouts: 34.4 us -> 41.9 us
  Pallas kernels: 257 us -> 251 us
    unnamed x35 -> x33, local copies, waits for them, and re-layouts: 1.66 us -> 8.17 us
    pallas_call x1, Pallas kernels: 107 us -> 102 us  [expert_front(): pl.pallas_call(functools.partial(expert_front_kernel, n_dp, n_t, tuple(wi...]
    transpose x0 -> x1, local copies, waits for them, and re-layouts: none -> 4.19 us  [expert_pass(): jnp.pad(expand_matrices[0], widen)]
where the time goes in v10:
time: 312 us; the launch traced here: 310 us
  Pallas kernels  251 us (80%)
  local copies, waits for them, and re-layouts  41.9 us (13%)
  matrix products  12.3 us (4%)
  other arithmetic  4.42 us (1%)
    pallas_call x1, Pallas kernels, expert_front(): pl.pallas_call(functools.partial(expert_front_kernel, n_dp, n_t, tuple(wi...  102 us
    pallas_call x1, Pallas kernels, moe_sum(): pl.pallas_call(functools.partial(moe_sum_kernel, n_dp, n_t, tuple(widths)...  89.8 us
    pallas_call x2, Pallas kernels, expert_exchange(): pl.pallas_call(functools.partial(expert_exchange_kernel, n_e), out_shape=...  45.8 us
    pallas_call x1, Pallas kernels, head_sum(): pl.pallas_call(functools.partial(head_sum_kernel, n_t), out_shape=jax.Sha...  13.1 us
    unnamed x33, local copies, waits for them, and re-layouts  8.17 us
    gather x1, local copies, waits for them, and re-layouts, attend(): page_keys = key_pages[table]  7.51 us
    gather x1, local copies, waits for them, and re-layouts, attend(): page_values = value_pages[table]  7.51 us

profile of v10, /device:TPU:1, one launch (start us, length us, event | category | flops | bytes accessed | tf_op | source)
XLA Modules:
  0.0 310.3 jit_solution(10179313089267997776)
XLA Ops:
  0.0 0.0 copy-start
  0.0 0.8 compare_select_fusion
  0.8 0.1 copy.53
  0.9 0.1 reshape.307
  1.0 0.3 copy-done
  1.3 0.0 copy-start.1
  1.4 7.5 %gather_fusion = bf16[136,128,128]{2,1,0:T(8,128)(2,1)} fusion(bf16[40,128,128]{2,1,0:T(8,128)(2,1)S(1)} %bitcast.142, s32[1024]{0:T(1024)S(1)} %pad_clamp_fusion), kind=kCustom, calls=%fused_computation | custom fusion | bytes 8913440 | tf_op jit(solution)/shard_map/gather | solution.py:580
  8.9 0.0 copy-done.12
  8.9 0.6 slice.49
  9.5 0.7 broadcast_compare_fusion.1
  10.1 0.0 copy-done.8
  10.1 1.3 select_reduce_fusion
  11.5 0.0 copy-done.11
  11.5 0.2 select_reduce_fusion.2
  11.7 0.3 bitcast_reduce_fusion
  12.0 0.0 copy-done.10
  12.0 0.8 convolution_bitcast_fusion.2
  12.9 0.0 copy-done.1
  12.9 7.5 %gather_fusion.1 = bf16[136,128,128]{2,1,0:T(8,128)(2,1)} fusion(bf16[40,128,128]{2,1,0:T(8,128)(2,1)S(1)} %bitcast.145, s32[1024]{0:T(1024)S(1)} %pad_clamp_fusion), kind=kCustom, calls=%fused_computation.1 | custom fusion | bytes 8913440 | tf_op jit(solution)/shard_map/gather | solution.py:581
  20.4 1.3 fusion.6
  21.7 4.8 %slice.62 = bf16[128,128,128]{2,1,0:T(8,128)(2,1)} slice(bf16[136,128,128]{2,1,0:T(8,128)(2,1)} %gather_fusion), slice={[0:128], [0:128], [0:128]} | slice | bytes 8388608 | tf_op jit(solution)/shard_map/slice | solution.py:589
  26.5 0.1 broadcast_compare_fusion
  26.6 3.5 %select_reduce_fusion.1 = (f32[16,4]{1,0:T(8,128)S(1)}, f32[16,8,128,4]{2,3,1,0:T(4,128)S(1)}) fusion(pred[16,8,128]{2,1,0:T(8,128)(4,1)S(1)} %broadcast_compare_fusion, bf16[16,8,128,128]{3,2,1,0:T(8,128)(2,1)} %bitcast.144, bf16[16,4,128,1]{2,1,0,3:T(4,128)(2,1)S(1)} %reshape.337), kind=kOutput, calls=%fused_computation.44 | convolution fusion | flops 16973760 | bytes 4489472 | tf_op jit(solution)/shard_map/rkgh,rmkph->rkgmp/dot_general | solution.py:586
  30.1 0.1 fusion.50
  30.3 0.3 bitcast_reduce_fusion.1
  30.6 0.0 slice-start
  30.6 0.0 copy-start.2
  30.6 2.2 slice-done
  32.8 0.8 fusion.8
  33.6 0.5 copy-done.2
  34.1 1.7 convolution_convert_fusion.x_ref
  35.7 13.1 %shard_map.163 = bf16[16,4096]{1,0:T(8,128)(2,1)} custom-call(bf16[64,4096]{1,0:T(8,128)(2,1)} %convolution_convert_fusion.x_ref), custom_call_target="tpu_custom_call" | custom-call | tf_op jit(solution)/shard_map/pallas_call | solution.py:325
  48.8 0.0 copy-done.5
  48.8 1.1 fusion.15
  49.9 0.0 copy-done.6
  49.9 0.1 copy.59
  50.0 0.1 eq.56
  50.0 0.1 fusion.44
  50.1 0.1 reduce_window_sum.11
  50.2 0.2 select_reduce_fusion.3
  50.4 0.1 reduce_sum.82
  50.4 0.1 copy.60
  51.2 0.0 copy-done.13
  51.2 0.1 select_reduce_fusion.4
  51.4 0.0 copy-done.7
  51.4 1.2 convolution_convert_fusion.1
  52.6 1.0 copy.62.x_ref
  53.6 16.0 %shard_map.164 = bf16[8,6,4096]{2,1,0:T(8,128)(2,1)} custom-call(bf16[8,6,4096]{2,1,0:T(8,128)(2,1)} %copy.62.x_ref), custom_call_target="tpu_custom_call" | custom-call | tf_op jit(solution)/shard_map/pallas_call | solution.py:368
  69.7 1.9 reshape.301.x_ref
  71.6 3.2 %copy.63 = bf16[1,224,4096]{1,2,0:T(8,128)(2,1)S(1)} copy(bf16[1,224,4096]{2,1,0:T(8,128)(2,1)} %param.31) | data formatting | bytes 3670016 | tf_op args[14]
  74.8 4.0 %copy.64 = bf16[1,224,4096]{1,2,0:T(8,128)(2,1)} copy(bf16[1,224,4096]{2,1,0:T(8,128)(2,1)} %param.32) | data formatting | bytes 3670016 | tf_op args[15]
  78.8 4.2 %pad_bitcast_fusion = (bf16[4096,256]{1,0:T(8,128)(2,1)}, bf16[4096,256]{1,0:T(8,128)(2,1)}) fusion(bf16[224,4096]{0,1:T(8,128)(2,1)} %bitcast.147, bf16[224,4096]{0,1:T(8,128)(2,1)S(1)} %bitcast.146), kind=kLoop, calls=%fused_computation.6 | loop fusion | bytes 7864320 | tf_op jit(solution)/shard_map/transpose | solution.py:667
  83.0 102.0 %shard_map.165.h_ref = bf16[1536,256]{1,0:T(8,128)(2,1)} custom-call(bf16[48,4096]{1,0:T(8,128)(2,1)} %reshape.301.x_ref, bf16[4096,256]{1,0:T(8,128)(2,1)} %get-tuple-element.14.wg_ref, bf16[4096,256]{1,0:T(8,128)(2,1)} %get-tuple-element.13.wu_ref), custom_call_target="tpu_custom_call" | custom-call | tf_op jit(solution)/shard_map/pallas_call | solution.py:513
  185.0 0.0 copy-done.4
  185.0 0.0 copy-start.9
  185.0 0.0 copy-start.3
  185.0 1.6 pad.12.w_ref
  186.6 89.8 %shard_map.166 = bf16[48,4096]{1,0:T(8,128)(2,1)} custom-call(bf16[1536,256]{1,0:T(8,128)(2,1)} %shard_map.165.h_ref, bf16[256,4096]{1,0:T(8,128)(2,1)} %pad.12.w_ref), custom_call_target="tpu_custom_call" | custom-call | tf_op jit(solution)/shard_map/pallas_call | solution.py:544
  276.4 1.9 reshape.302.x_ref
  278.4 29.8 %shard_map.167 = bf16[8,6,4096]{2,1,0:T(8,128)(2,1)} custom-call(bf16[8,6,4096]{2,1,0:T(8,128)(2,1)} %reshape.302.x_ref), custom_call_target="tpu_custom_call" | custom-call | tf_op jit(solution)/shard_map/pallas_call | solution.py:368
  308.2 0.0 copy-done.9
  308.2 1.4 fusion.2
  309.6 0.0 copy-done.3
  309.6 0.7 fusion.18
  (32 shorter events, 0.2 us)
Async XLA Ops:
  0.0 1.3 copy-start
  1.3 7.5 %copy-start.12 = (s32[17]{0:T(128)S(1)}, s32[17]{0:T(128)}, u32[]{:S(2)}) copy-start(s32[17]{0:T(128)} %param.24) | copy-start | bytes 208
  1.3 8.8 %copy-start.8 = (bf16[64,512]{1,0:T(8,128)(2,1)S(1)}, bf16[64,512]{1,0:T(8,128)(2,1)}, u32[]{:S(2)}) copy-start(bf16[64,512]{1,0:T(8,128)(2,1)} %param.18) | copy-start | bytes 196612
  1.3 10.1 %copy-start.11 = (bf16[64,128]{1,0:T(8,128)(2,1)S(1)}, bf16[64,128]{1,0:T(8,128)(2,1)}, u32[]{:S(2)}) copy-start(bf16[64,128]{1,0:T(8,128)(2,1)} %param.19) | copy-start | bytes 49156
  1.3 10.7 %copy-start.10 = (bf16[64,128]{1,0:T(8,128)(2,1)S(1)}, bf16[64,128]{1,0:T(8,128)(2,1)}, u32[]{:S(2)}) copy-start(bf16[64,128]{1,0:T(8,128)(2,1)} %param.20) | copy-start | bytes 49156
  1.3 11.5 %copy-start.1 = (bf16[40,1,128,128]{3,2,1,0:T(8,128)(2,1)S(1)}, bf16[40,1,128,128]{3,2,1,0:T(8,128)(2,1)}, u32[]{:S(2)}) copy-start(bf16[40,1,128,128]{3,2,1,0:T(8,128)(2,1)} %param.22) | copy-start | bytes 3932164
  30.6 2.2 slice-start
  30.6 3.5 %copy-start.2 = (bf16[512,4096]{1,0:T(8,128)(2,1)S(1)}, bf16[512,4096]{1,0:T(8,128)(2,1)}, u32[]{:S(2)}) copy-start(bf16[512,4096]{1,0:T(8,128)(2,1)} %param.25) | copy-start | bytes 12582916
  32.8 16.0 %copy-start.5 = (bf16[16,4096]{1,0:T(8,128)(2,1)S(1)}, bf16[16,4096]{1,0:T(8,128)(2,1)}, u32[]{:S(2)}) copy-start(bf16[16,4096]{1,0:T(8,128)(2,1)} %param.17) | copy-start | bytes 393220
  32.8 17.1 %copy-start.6 = (s32[16,2]{0,1:T(2,128)S(1)}, s32[16,2]{0,1:T(2,128)}, u32[]{:S(2)}) copy-start(s32[16,2]{0,1:T(2,128)} %param.27) | copy-start | bytes 388
  32.8 18.4 %copy-start.13 = (s32[8]{0:T(128)S(1)}, s32[8]{0:T(128)}, u32[]{:S(2)}) copy-start(s32[8]{0:T(128)} %param.29) | copy-start | bytes 100
  32.8 18.6 %copy-start.7 = (bf16[4096]{0:T(1024)(128)(2,1)S(1)}, bf16[4096]{0:T(1024)(128)(2,1)}, u32[]{:S(2)}) copy-start(bf16[4096]{0:T(1024)(128)(2,1)} %param.26) | copy-start | bytes 24580
  83.0 102.0 %copy-start.4 = (bf16[1,224,4096]{2,1,0:T(8,128)(2,1)S(1)}, bf16[1,224,4096]{2,1,0:T(8,128)(2,1)}, u32[]{:S(2)}) copy-start(bf16[1,224,4096]{2,1,0:T(8,128)(2,1)} %param.33) | copy-start | bytes 5505028
  185.0 123.2 %copy-start.9 = (f32[16,2]{0,1:T(2,128)S(1)}, f32[16,2]{0,1:T(2,128)}, u32[]{:S(2)}) copy-start(f32[16,2]{0,1:T(2,128)} %param.28) | copy-start | bytes 388
  185.0 124.6 %copy-start.3 = (bf16[16,4096]{1,0:T(8,128)(2,1)S(1)}, bf16[16,4096]{1,0:T(8,128)(2,1)}, u32[]{:S(2)}) copy-start(bf16[16,4096]{1,0:T(8,128)(2,1)} %shard_map.163) | copy-start | bytes 393220

commit v11 on v10

--- a/solution.py
+++ b/solution.py
@@ -577,8 +577,13 @@
     page_width = key_pages.shape[2]
     context = page_count * page_width
     inverse_root = 1.0 / math.sqrt(head_width)
-    page_keys = key_pages[table]
-    page_values = value_pages[table]
+    pick = (table[..., None] == jnp.arange(key_pages.shape[0], dtype=table.dtype)).astype(key_pages.dtype)
+    page_keys = jnp.einsum(
+        "rmp,pkab->rmkab", pick, key_pages, preferred_element_type=jnp.float32
+    ).astype(key_pages.dtype)
+    page_values = jnp.einsum(
+        "rmp,pkab->rmkab", pick, value_pages, preferred_element_type=jnp.float32
+    ).astype(value_pages.dtype)
     grouped = question_vectors.reshape(rows_all, kv_heads, group_size, head_width)
     positions = jnp.arange(context, dtype=jnp.int32)
     single_q = grouped[:single_count]

time: 312 us -> 308 us (0.987)
  local copies, waits for them, and re-layouts: 41.9 us -> 29.1 us
  matrix products: 12.3 us -> 20.5 us
    gather x2 -> x0, local copies, waits for them, and re-layouts: 15 us -> none  [the longest x1 7.51 us: attend(): page_keys = key_pages[table]]
    slice x3 -> x0, local copies, waits for them, and re-layouts: 6.93 us -> none  [the longest x1 4.77 us: attend(): page_keys[:single_count]]
    dot_general x0 -> x2, matrix products: none -> 4.09 us  [the longest x1 2.72 us: attend(): jnp.einsum('rmp,pkab->rmkab', pick, key_pages, preferred_element_type=jnp...]
    unnamed x33 -> x36, local copies, waits for them, and re-layouts: 8.17 us -> 12.2 us
    dot_general x1, matrix products: 0.78 us -> 4.29 us  [attend(): jnp.einsum('rkgmp,rmkph->rkgh', weight_cache.reshape(single_count, kv_hea...]
    dot_general x0 -> x1, local copies, waits for them, and re-layouts: none -> 3.42 us  [attend(): jnp.einsum('rkgh,rmkph->rkgmp', single_q, page_keys[:single_count], prefe...]
where the time goes in v11:
time: 308 us; the launch traced here: 307 us
  Pallas kernels  252 us (82%)
  local copies, waits for them, and re-layouts  29.1 us (9%)
  matrix products  20.5 us (7%)
  other arithmetic  4.31 us (1%)
    pallas_call x1, Pallas kernels, expert_front(): pl.pallas_call(functools.partial(expert_front_kernel, n_dp, n_t, tuple(wi...  102 us
    pallas_call x1, Pallas kernels, moe_sum(): pl.pallas_call(functools.partial(moe_sum_kernel, n_dp, n_t, tuple(widths)...  90.7 us
    pallas_call x2, Pallas kernels, expert_exchange(): pl.pallas_call(functools.partial(expert_exchange_kernel, n_e), out_shape=...  46.5 us
    pallas_call x1, Pallas kernels, head_sum(): pl.pallas_call(functools.partial(head_sum_kernel, n_t), out_shape=jax.Sha...  13.1 us
    unnamed x36, local copies, waits for them, and re-layouts  12.2 us
    dot_general x1, matrix products, attend(): jnp.einsum('rkgh,rmkph->rkgmp', single_q, page_keys[:single_count], prefe...  6.49 us

profile of v11, /device:TPU:1, one launch (start us, length us, event | category | flops | bytes accessed | tf_op | source)
XLA Modules:
  0.0 307.1 jit_solution(8658348053198609347)
XLA Ops:
  0.0 0.8 copy.72
  0.8 2.7 convolution_convert_fusion.3
  3.5 0.0 copy-start
  3.5 2.1 copy-done
  5.6 0.0 copy-done.13
  5.6 0.6 slice.53
  6.2 0.7 broadcast_compare_fusion.1
  6.9 0.0 copy-done.9
  6.9 0.4 select_reduce_fusion
  7.2 0.0 copy-start.5
  7.3 0.0 copy-done.12
  7.3 0.2 select_reduce_fusion.2
  7.5 0.3 bitcast_reduce_fusion
  7.8 0.3 fusion.25
  8.1 0.5 copy.80
  8.6 0.0 copy-done.5
  8.6 0.0 copy-start.11
  8.7 1.4 convolution_convert_fusion.2
  10.0 2.0 copy-done.1
  12.1 0.4 convolution_bitcast_fusion.2
  12.5 0.0 copy-done.11
  12.5 0.2 fusion.12
  12.8 6.5 %fusion.55 = f32[16,8,128,4]{1,3,2,0:T(4,128)} fusion(bf16[17,8,128,128]{3,1,2,0:T(8,128)(2,1)} %copy-done, bf16[16,4,128,1]{2,1,0,3:T(4,128)(2,1)S(1)} %reshape.320), kind=kOutput, calls=%fused_computation.83 | convolution fusion | flops 16777216 | bytes 4734976 | tf_op jit(solution)/shard_map/rkgh,rmkph->rkgmp/dot_general | solution.py:591
  19.3 3.4 %copy.74 = f32[16,8,128,4]{2,1,3,0:T(8,128)S(1)} copy(f32[16,8,128,4]{1,3,2,0:T(4,128)} %fusion.55) | data formatting | bytes 524288 | tf_op jit(solution)/shard_map/rkgh,rmkph->rkgmp/dot_general | solution.py:591
  22.7 0.1 broadcast_compare_fusion
  22.8 0.2 select_reduce_fusion.1
  23.0 0.1 fusion.63
  23.2 0.3 bitcast_reduce_fusion.1
  23.5 0.2 fusion.31
  23.7 1.3 copy.76
  25.0 0.0 copy-start.2
  25.0 4.3 %fusion.19 = bf16[16,4,128]{2,1,0:T(4,128)(2,1)S(1)} fusion(bf16[16,4,8,128]{2,1,3,0:T(4,128)(2,1)S(1)} %copy.76, bf16[17,8,128,128]{3,1,2,0:T(8,128)(2,1)} %copy-done.1, f32[16,128]{1,0:T(8,128)S(1)} %slice_convert_fusion, f32[16,4]{1,0:T(8,128)S(1)} %get-tuple-element.5), kind=kOutput, calls=%fused_computation.26 | convolution fusion | flops 16801792 | bytes 4350208 | tf_op jit(solution)/shard_map/rkgmp,rmkph->rkgh/dot_general | solution.py:609
  29.4 0.0 copy-start.6
  29.4 0.0 copy-start.7
  29.4 0.0 copy-start.14
  29.4 0.0 copy-start.8
  29.4 1.7 convolution_convert_fusion.x_ref
  31.1 13.1 %shard_map.163 = bf16[16,4096]{1,0:T(8,128)(2,1)} custom-call(bf16[64,4096]{1,0:T(8,128)(2,1)} %convolution_convert_fusion.x_ref), custom_call_target="tpu_custom_call" | custom-call | tf_op jit(solution)/shard_map/pallas_call | solution.py:325
  44.1 1.1 fusion.26
  45.2 0.1 copy.83
  45.3 0.1 eq.72
  45.4 0.1 fusion.57
  45.5 0.1 reduce_window_sum.11
  45.5 0.2 select_reduce_fusion.3
  45.7 0.1 reduce_sum.82
  45.8 0.1 copy.84
  46.5 0.0 copy-done.14
  46.6 0.1 select_reduce_fusion.4
  46.7 1.2 convolution_convert_fusion.1
  47.9 1.0 copy.86.x_ref
  49.0 16.0 %shard_map.164 = bf16[8,6,4096]{2,1,0:T(8,128)(2,1)} custom-call(bf16[8,6,4096]{2,1,0:T(8,128)(2,1)} %copy.86.x_ref), custom_call_target="tpu_custom_call" | custom-call | tf_op jit(solution)/shard_map/pallas_call | solution.py:368
  65.0 1.9 reshape.316.x_ref
  67.0 3.2 %copy.87 = bf16[1,224,4096]{1,2,0:T(8,128)(2,1)S(1)} copy(bf16[1,224,4096]{2,1,0:T(8,128)(2,1)} %param.31) | data formatting | bytes 3670016 | tf_op args[14]
  70.2 4.0 %copy.88 = bf16[1,224,4096]{1,2,0:T(8,128)(2,1)} copy(bf16[1,224,4096]{2,1,0:T(8,128)(2,1)} %param.32) | data formatting | bytes 3670016 | tf_op args[15]
  74.2 4.2 %pad_bitcast_fusion = (bf16[4096,256]{1,0:T(8,128)(2,1)}, bf16[4096,256]{1,0:T(8,128)(2,1)}) fusion(bf16[224,4096]{0,1:T(8,128)(2,1)} %bitcast.143, bf16[224,4096]{0,1:T(8,128)(2,1)S(1)} %bitcast.142), kind=kLoop, calls=%fused_computation.8 | loop fusion | bytes 7864320 | tf_op jit(solution)/shard_map/transpose | solution.py:672
  78.4 101.9 %shard_map.165.h_ref = bf16[1536,256]{1,0:T(8,128)(2,1)} custom-call(bf16[48,4096]{1,0:T(8,128)(2,1)} %reshape.316.x_ref, bf16[4096,256]{1,0:T(8,128)(2,1)} %get-tuple-element.12.wg_ref, bf16[4096,256]{1,0:T(8,128)(2,1)} %get-tuple-element.11.wu_ref), custom_call_target="tpu_custom_call" | custom-call | tf_op jit(solution)/shard_map/pallas_call | solution.py:513
  180.2 0.0 copy-done.4
  180.2 1.6 pad.12.w_ref
  181.8 90.7 %shard_map.166 = bf16[48,4096]{1,0:T(8,128)(2,1)} custom-call(bf16[1536,256]{1,0:T(8,128)(2,1)} %shard_map.165.h_ref, bf16[256,4096]{1,0:T(8,128)(2,1)} %pad.12.w_ref), custom_call_target="tpu_custom_call" | custom-call | tf_op jit(solution)/shard_map/pallas_call | solution.py:544
  272.5 0.0 copy-start.3
  272.5 2.0 reshape.317.x_ref
  274.4 30.5 %shard_map.167 = bf16[8,6,4096]{2,1,0:T(8,128)(2,1)} custom-call(bf16[8,6,4096]{2,1,0:T(8,128)(2,1)} %reshape.317.x_ref), custom_call_target="tpu_custom_call" | custom-call | tf_op jit(solution)/shard_map/pallas_call | solution.py:368
  305.0 1.4 fusion.8
  306.4 0.7 fusion.29
  (35 shorter events, 0.3 us)
Async XLA Ops:
  0.8 4.8 %copy-start.13 = (s32[17]{0:T(128)S(1)}, s32[17]{0:T(128)}, u32[]{:S(2)}) copy-start(s32[17]{0:T(128)} %param.24) | copy-start | bytes 208
  0.8 6.1 %copy-start.9 = (bf16[64,512]{1,0:T(8,128)(2,1)S(1)}, bf16[64,512]{1,0:T(8,128)(2,1)}, u32[]{:S(2)}) copy-start(bf16[64,512]{1,0:T(8,128)(2,1)} %param.18) | copy-start | bytes 196612
  0.8 6.5 %copy-start.12 = (bf16[64,128]{1,0:T(8,128)(2,1)S(1)}, bf16[64,128]{1,0:T(8,128)(2,1)}, u32[]{:S(2)}) copy-start(bf16[64,128]{1,0:T(8,128)(2,1)} %param.19) | copy-start | bytes 49156
  3.5 2.1 copy-start
  7.2 1.4 copy-start.5
  8.6 3.9 %copy-start.11 = (bf16[64,128]{1,0:T(8,128)(2,1)S(1)}, bf16[64,128]{1,0:T(8,128)(2,1)}, u32[]{:S(2)}) copy-start(bf16[64,128]{1,0:T(8,128)(2,1)} %param.20) | copy-start | bytes 49156
  10.0 2.0 copy-start.1
  25.0 4.3 %copy-start.2 = (bf16[512,4096]{1,0:T(8,128)(2,1)S(1)}, bf16[512,4096]{1,0:T(8,128)(2,1)}, u32[]{:S(2)}) copy-start(bf16[512,4096]{1,0:T(8,128)(2,1)} %param.25) | copy-start | bytes 12582916
  29.4 14.8 %copy-start.6 = (bf16[16,4096]{1,0:T(8,128)(2,1)S(1)}, bf16[16,4096]{1,0:T(8,128)(2,1)}, u32[]{:S(2)}) copy-start(bf16[16,4096]{1,0:T(8,128)(2,1)} %param.17) | copy-start | bytes 393220
  29.4 15.8 %copy-start.7 = (s32[16,2]{0,1:T(2,128)S(1)}, s32[16,2]{0,1:T(2,128)}, u32[]{:S(2)}) copy-start(s32[16,2]{0,1:T(2,128)} %param.27) | copy-start | bytes 388
  29.4 17.2 %copy-start.14 = (s32[8]{0:T(128)S(1)}, s32[8]{0:T(128)}, u32[]{:S(2)}) copy-start(s32[8]{0:T(128)} %param.29) | copy-start | bytes 100
  29.4 17.3 %copy-start.8 = (bf16[4096]{0:T(1024)(128)(2,1)S(1)}, bf16[4096]{0:T(1024)(128)(2,1)}, u32[]{:S(2)}) copy-start(bf16[4096]{0:T(1024)(128)(2,1)} %param.26) | copy-start | bytes 24580
  78.4 101.9 %copy-start.4 = (bf16[1,224,4096]{2,1,0:T(8,128)(2,1)S(1)}, bf16[1,224,4096]{2,1,0:T(8,128)(2,1)}, u32[]{:S(2)}) copy-start(bf16[1,224,4096]{2,1,0:T(8,128)(2,1)} %param.33) | copy-start | bytes 5505028
  181.8 123.1 %copy-start.10 = (f32[16,2]{0,1:T(2,128)S(1)}, f32[16,2]{0,1:T(2,128)}, u32[]{:S(2)}) copy-start(f32[16,2]{0,1:T(2,128)} %param.28) | copy-start | bytes 388
  272.5 33.9 %copy-start.3 = (bf16[16,4096]{1,0:T(8,128)(2,1)S(1)}, bf16[16,4096]{1,0:T(8,128)(2,1)}, u32[]{:S(2)}) copy-start(bf16[16,4096]{1,0:T(8,128)(2,1)} %shard_map.163) | copy-start | bytes 393220

commit v12 on v11

--- a/solution.py
+++ b/solution.py
@@ -435,8 +435,11 @@
     def feed(piece, row_chunk, cols):
         start = pl.multiple_of(row_chunk * rows, 16)
         v = piece[...]
-        gate_acc[pl.ds(start, rows), :] += jnp.dot(v, wg_ref[cols, :], preferred_element_type=jnp.float32)
-        up_acc[pl.ds(start, rows), :] += jnp.dot(v, wu_ref[cols, :], preferred_element_type=jnp.float32)
+        dims = (((1,), (1,)), ((), ()))
+        gate_acc[pl.ds(start, rows), :] += lax.dot_general(
+            v, wg_ref[:, cols], dims, preferred_element_type=jnp.float32)
+        up_acc[pl.ds(start, rows), :] += lax.dot_general(
+            v, wu_ref[:, cols], dims, preferred_element_type=jnp.float32)
 
     streams = []
     sem_at = 0
@@ -498,7 +501,7 @@
 
 def expert_front(x, gate_w, up_w, n_dp, n_t):
     rows, model_width = x.shape
-    inner = gate_w.shape[1]
+    inner = gate_w.shape[0]
     widths, order = split_plan(n_dp, n_t, rows, model_width, False)
     scratch = [
         pltpu.VMEM((n_t, n_dp, rows, widths[0]), jnp.bfloat16),
@@ -663,17 +666,14 @@
     local_count = gating_matrices.shape[0]
     assert local_count == 1
     arrived = expert_exchange(send, 3).reshape(specialist_index * slot_count, model_width)
-    inner = gating_matrices.shape[1]
-    padded = -(-inner // 128) * 128
-    widen = ((0, padded - inner), (0, 0))
     hidden = expert_front(
         arrived,
-        jnp.pad(gating_matrices[0], widen).T,
-        jnp.pad(expand_matrices[0], widen).T,
+        gating_matrices[0],
+        expand_matrices[0],
         lax.axis_size("dp"),
         lax.axis_size("tensor"),
     )
-    down = jnp.pad(contract_matrices[0], widen)
+    down = contract_matrices[0]
     n_dp, n_t = lax.axis_size("dp"), lax.axis_size("tensor")
     summed = moe_sum(hidden, down, n_dp, n_t)
     return expert_exchange(summed.reshape(specialist_index, slot_count, model_width), 4)

time: 308 us -> 299 us (0.971)
  local copies, waits for them, and re-layouts: 29.1 us -> 16.1 us
  Pallas kernels: 252 us -> 256 us
    unnamed x36 -> x32, local copies, waits for them, and re-layouts: 12.2 us -> 5.07 us
    pallas_call x1, Pallas kernels: 102 us -> 107 us  [expert_front(): pl.pallas_call(functools.partial(expert_front_kernel, n_dp, n_t, tuple(wi...]
    transpose x1 -> x0, local copies, waits for them, and re-layouts: 4.19 us -> none  [expert_pass(): jnp.pad(expand_matrices[0], widen)]
where the time goes in v12:
time: 299 us; the launch traced here: 298 us
  Pallas kernels  256 us (86%)
  matrix products  20.5 us (7%)
  local copies, waits for them, and re-layouts  16.1 us (5%)
  other arithmetic  4.31 us (1%)
    pallas_call x1, Pallas kernels, expert_front(): pl.pallas_call(functools.partial(expert_front_kernel, n_dp, n_t, tuple(wi...  107 us
    pallas_call x1, Pallas kernels, moe_sum(): pl.pallas_call(functools.partial(moe_sum_kernel, n_dp, n_t, tuple(widths)...  91.4 us
    pallas_call x2, Pallas kernels, expert_exchange(): pl.pallas_call(functools.partial(expert_exchange_kernel, n_e), out_shape=...  44.6 us
    pallas_call x1, Pallas kernels, head_sum(): pl.pallas_call(functools.partial(head_sum_kernel, n_t), out_shape=jax.Sha...  13.1 us
    dot_general x1, matrix products, attend(): jnp.einsum('rkgh,rmkph->rkgmp', single_q, page_keys[:single_count], prefe...  6.49 us

profile of v12, /device:TPU:1, one launch (start us, length us, event | category | flops | bytes accessed | tf_op | source)
XLA Modules:
  0.0 298.2 jit_solution(15343856612834238081)
XLA Ops:
  0.0 0.0 copy-start.12
  0.0 0.8 copy.66
  0.8 2.8 convolution_convert_fusion.3
  3.6 0.0 copy-start
  3.6 2.1 copy-done
  5.7 0.0 copy-done.12
  5.7 0.6 slice.53
  6.3 0.7 broadcast_compare_fusion.1
  7.0 0.0 copy-done.8
  7.0 0.4 select_reduce_fusion
  7.4 0.0 copy-done.11
  7.4 0.2 select_reduce_fusion.2
  7.6 0.3 bitcast_reduce_fusion
  7.9 0.3 fusion.25
  8.2 0.0 copy-start.10
  8.2 0.5 copy.74
  8.7 0.0 copy-done.4
  8.7 1.4 convolution_convert_fusion.2
  10.1 0.0 copy-start.1
  10.1 2.0 copy-done.1
  12.2 0.4 convolution_bitcast_fusion.2
  12.6 0.0 copy-done.10
  12.6 0.2 fusion.12
  12.9 6.5 %fusion.55 = f32[16,8,128,4]{1,3,2,0:T(4,128)} fusion(bf16[17,8,128,128]{3,1,2,0:T(8,128)(2,1)} %copy-done, bf16[16,4,128,1]{2,1,0,3:T(4,128)(2,1)S(1)} %reshape.320), kind=kOutput, calls=%fused_computation.81 | convolution fusion | flops 16777216 | bytes 4734976 | tf_op jit(solution)/shard_map/rkgh,rmkph->rkgmp/dot_general | solution.py:594
  19.4 3.4 %copy.68 = f32[16,8,128,4]{2,1,3,0:T(8,128)S(1)} copy(f32[16,8,128,4]{1,3,2,0:T(4,128)} %fusion.55) | data formatting | bytes 524288 | tf_op jit(solution)/shard_map/rkgh,rmkph->rkgmp/dot_general | solution.py:594
  22.8 0.1 broadcast_compare_fusion
  22.9 0.2 select_reduce_fusion.1
  23.1 0.1 fusion.63
  23.3 0.3 bitcast_reduce_fusion.1
  23.6 0.2 fusion.31
  23.8 1.3 copy.70
  25.1 0.0 copy-start.2
  25.1 4.3 %fusion.19 = bf16[16,4,128]{2,1,0:T(4,128)(2,1)S(1)} fusion(bf16[16,4,8,128]{2,1,3,0:T(4,128)(2,1)S(1)} %copy.70, bf16[17,8,128,128]{3,1,2,0:T(8,128)(2,1)} %copy-done.1, f32[16,128]{1,0:T(8,128)S(1)} %slice_convert_fusion, f32[16,4]{1,0:T(8,128)S(1)} %get-tuple-element.5), kind=kOutput, calls=%fused_computation.24 | convolution fusion | flops 16801792 | bytes 4350208 | tf_op jit(solution)/shard_map/rkgmp,rmkph->rkgh/dot_general | solution.py:612
  29.4 0.0 copy-start.6
  29.4 0.0 copy-start.13
  29.4 0.0 copy-start.7
  29.5 0.0 copy-done.2
  29.5 1.7 convolution_convert_fusion.x_ref
  31.1 13.1 %shard_map.163 = bf16[16,4096]{1,0:T(8,128)(2,1)} custom-call(bf16[64,4096]{1,0:T(8,128)(2,1)} %convolution_convert_fusion.x_ref), custom_call_target="tpu_custom_call" | custom-call | tf_op jit(solution)/shard_map/pallas_call | solution.py:325
  44.2 0.0 copy-done.5
  44.2 1.1 fusion.26
  45.3 0.0 copy-done.6
  45.3 0.1 copy.77
  45.4 0.1 eq.72
  45.5 0.1 fusion.57
  45.5 0.1 reduce_window_sum.11
  45.6 0.2 select_reduce_fusion.3
  45.8 0.1 reduce_sum.82
  45.9 0.1 copy.78
  46.6 0.0 copy-done.13
  46.7 0.1 select_reduce_fusion.4
  46.8 0.0 copy-done.7
  46.8 1.2 convolution_convert_fusion.1
  48.0 1.0 copy.80.x_ref
  49.1 16.0 %shard_map.164 = bf16[8,6,4096]{2,1,0:T(8,128)(2,1)} custom-call(bf16[8,6,4096]{2,1,0:T(8,128)(2,1)} %copy.80.x_ref), custom_call_target="tpu_custom_call" | custom-call | tf_op jit(solution)/shard_map/pallas_call | solution.py:368
  65.1 1.9 reshape.316.x_ref
  67.0 107.2 %shard_map.165.h_ref = bf16[1536,224]{1,0:T(8,128)(2,1)} custom-call(bf16[48,4096]{1,0:T(8,128)(2,1)} %reshape.316.x_ref, bf16[224,4096]{1,0:T(8,128)(2,1)} %bitcast.138, bf16[224,4096]{1,0:T(8,128)(2,1)} %bitcast.139), custom_call_target="tpu_custom_call" | custom-call | tf_op jit(solution)/shard_map/pallas_call | solution.py:516
  174.2 91.4 %shard_map.166 = bf16[48,4096]{1,0:T(8,128)(2,1)} custom-call(bf16[1536,224]{1,0:T(8,128)(2,1)} %shard_map.165.h_ref, bf16[224,4096]{1,0:T(8,128)(2,1)} %bitcast.140), custom_call_target="tpu_custom_call" | custom-call | tf_op jit(solution)/shard_map/pallas_call | solution.py:547
  265.6 1.9 reshape.317.x_ref
  267.5 28.5 %shard_map.167 = bf16[8,6,4096]{2,1,0:T(8,128)(2,1)} custom-call(bf16[8,6,4096]{2,1,0:T(8,128)(2,1)} %reshape.317.x_ref), custom_call_target="tpu_custom_call" | custom-call | tf_op jit(solution)/shard_map/pallas_call | solution.py:368
  296.1 0.0 copy-done.9
  296.1 1.4 fusion.8
  297.5 0.0 copy-done.3
  297.5 0.7 fusion.29
  (29 shorter events, 0.2 us)
Async XLA Ops:
  0.0 5.7 %copy-start.12 = (s32[17]{0:T(128)S(1)}, s32[17]{0:T(128)}, u32[]{:S(2)}) copy-start(s32[17]{0:T(128)} %param.24) | copy-start | bytes 208
  0.0 7.0 %copy-start.8 = (bf16[64,512]{1,0:T(8,128)(2,1)S(1)}, bf16[64,512]{1,0:T(8,128)(2,1)}, u32[]{:S(2)}) copy-start(bf16[64,512]{1,0:T(8,128)(2,1)} %param.18) | copy-start | bytes 196612
  0.0 7.4 %copy-start.11 = (bf16[64,128]{1,0:T(8,128)(2,1)S(1)}, bf16[64,128]{1,0:T(8,128)(2,1)}, u32[]{:S(2)}) copy-start(bf16[64,128]{1,0:T(8,128)(2,1)} %param.19) | copy-start | bytes 49156
  0.8 7.9 %copy-start.4 = (bf16[40,1,128,128]{3,2,1,0:T(8,128)(2,1)S(1)}, bf16[40,1,128,128]{3,2,1,0:T(8,128)(2,1)}, u32[]{:S(2)}) copy-start(bf16[40,1,128,128]{3,2,1,0:T(8,128)(2,1)} %param.22) | copy-start | bytes 3932164
  3.6 2.1 copy-start
  8.2 4.4 %copy-start.10 = (bf16[64,128]{1,0:T(8,128)(2,1)S(1)}, bf16[64,128]{1,0:T(8,128)(2,1)}, u32[]{:S(2)}) copy-start(bf16[64,128]{1,0:T(8,128)(2,1)} %param.20) | copy-start | bytes 49156
  10.1 2.0 copy-start.1
  25.1 4.4 %copy-start.2 = (bf16[512,4096]{1,0:T(8,128)(2,1)S(1)}, bf16[512,4096]{1,0:T(8,128)(2,1)}, u32[]{:S(2)}) copy-start(bf16[512,4096]{1,0:T(8,128)(2,1)} %param.25) | copy-start | bytes 12582916
  29.4 14.8 %copy-start.5 = (bf16[16,4096]{1,0:T(8,128)(2,1)S(1)}, bf16[16,4096]{1,0:T(8,128)(2,1)}, u32[]{:S(2)}) copy-start(bf16[16,4096]{1,0:T(8,128)(2,1)} %param.17) | copy-start | bytes 393220
  29.4 15.9 %copy-start.6 = (s32[16,2]{0,1:T(2,128)S(1)}, s32[16,2]{0,1:T(2,128)}, u32[]{:S(2)}) copy-start(s32[16,2]{0,1:T(2,128)} %param.27) | copy-start | bytes 388
  29.4 17.2 %copy-start.13 = (s32[8]{0:T(128)S(1)}, s32[8]{0:T(128)}, u32[]{:S(2)}) copy-start(s32[8]{0:T(128)} %param.29) | copy-start | bytes 100
  29.4 17.3 %copy-start.7 = (bf16[4096]{0:T(1024)(128)(2,1)S(1)}, bf16[4096]{0:T(1024)(128)(2,1)}, u32[]{:S(2)}) copy-start(bf16[4096]{0:T(1024)(128)(2,1)} %param.26) | copy-start | bytes 24580
  67.0 229.1 %copy-start.9 = (f32[16,2]{0,1:T(2,128)S(1)}, f32[16,2]{0,1:T(2,128)}, u32[]{:S(2)}) copy-start(f32[16,2]{0,1:T(2,128)} %param.28) | copy-start | bytes 388
  67.0 230.5 %copy-start.3 = (bf16[16,4096]{1,0:T(8,128)(2,1)S(1)}, bf16[16,4096]{1,0:T(8,128)(2,1)}, u32[]{:S(2)}) copy-start(bf16[16,4096]{1,0:T(8,128)(2,1)} %shard_map.163) | copy-start | bytes 393220

commit v13 on v12

--- a/solution.py
+++ b/solution.py
@@ -44,7 +44,7 @@
     return [(link1, size1)] * (n1 - 1) + [None] + [(link2, size2)] * (n2 - 1) + [None]
 
 
-def split_plan(n_dp, n_t, rows, model_width, reduce):
+def split_plan(n_dp, n_t, rows, model_width, reduce, per_step=0.3):
     best = None
     for first_dp in range(128, model_width // 2, 128):
         widths = [first_dp, first_dp, model_width // 2 - first_dp, model_width // 2 - first_dp]
@@ -58,7 +58,7 @@
             else:
                 big1, big2 = (n_dp * unit, unit) if reduce else (unit, n_t * unit)
                 events.append(ring_events(n_t, n_dp, "y" + sign, "z" + sign, big1, big2))
-        order, finish = plan_order(events)
+        order, finish = plan_order(events, per_step=per_step)
         if best is None or finish < best[0]:
             best = (finish, widths, order)
     return best[1], best[2]
@@ -502,7 +502,7 @@
 def expert_front(x, gate_w, up_w, n_dp, n_t):
     rows, model_width = x.shape
     inner = gate_w.shape[0]
-    widths, order = split_plan(n_dp, n_t, rows, model_width, False)
+    widths, order = split_plan(n_dp, n_t, rows, model_width, False, per_step=1.0)
     scratch = [
         pltpu.VMEM((n_t, n_dp, rows, widths[0]), jnp.bfloat16),
         pltpu.VMEM((n_t, n_dp, rows, widths[1]), jnp.bfloat16),

time: 299 us -> 295 us (0.987)
  Pallas kernels: 256 us -> 252 us
    pallas_call x1, Pallas kernels: 107 us -> 104 us  [expert_front(): pl.pallas_call(functools.partial(expert_front_kernel, n_dp, n_t, tuple(wi...]
where the time goes in v13:
time: 295 us
  Pallas kernels  252 us (85%)
  matrix products  20.5 us (7%)
  local copies, waits for them, and re-layouts  16.1 us (5%)
  other arithmetic  4.31 us (1%)
    pallas_call x1, Pallas kernels, expert_front(): pl.pallas_call(functools.partial(expert_front_kernel, n_dp, n_t, tuple(wi...  104 us
    pallas_call x1, Pallas kernels, moe_sum(): pl.pallas_call(functools.partial(moe_sum_kernel, n_dp, n_t, tuple(widths)...  93.1 us
    pallas_call x2, Pallas kernels, expert_exchange(): pl.pallas_call(functools.partial(expert_exchange_kernel, n_e), out_shape=...  42.6 us
    pallas_call x1, Pallas kernels, head_sum(): pl.pallas_call(functools.partial(head_sum_kernel, n_t), out_shape=jax.Sha...  13.1 us
    dot_general x1, matrix products, attend(): jnp.einsum('rkgh,rmkph->rkgmp', single_q, page_keys[:single_count], prefe...  6.49 us

profile of v13, /device:TPU:1, one launch (start us, length us, event | category | flops | bytes accessed | tf_op | source)
XLA Modules:
  0.0 294.5 jit_solution(7454504902618669104)
XLA Ops:
  0.0 0.0 copy-start.12
  0.0 0.8 copy.66
  0.8 2.8 convolution_convert_fusion.3
  3.6 0.0 copy-start
  3.6 2.1 copy-done
  5.7 0.0 copy-done.12
  5.7 0.6 slice.53
  6.3 0.7 broadcast_compare_fusion.1
  7.0 0.0 copy-done.8
  7.0 0.4 select_reduce_fusion
  7.4 0.0 copy-done.11
  7.4 0.2 select_reduce_fusion.2
  7.6 0.3 bitcast_reduce_fusion
  7.9 0.3 fusion.25
  8.2 0.0 copy-start.10
  8.2 0.5 copy.74
  8.7 0.0 copy-done.4
  8.7 1.4 convolution_convert_fusion.2
  10.1 0.0 copy-start.1
  10.1 2.0 copy-done.1
  12.2 0.4 convolution_bitcast_fusion.2
  12.6 0.0 copy-done.10
  12.6 0.2 fusion.12
  12.9 6.5 %fusion.55 = f32[16,8,128,4]{1,3,2,0:T(4,128)} fusion(bf16[17,8,128,128]{3,1,2,0:T(8,128)(2,1)} %copy-done, bf16[16,4,128,1]{2,1,0,3:T(4,128)(2,1)S(1)} %reshape.320), kind=kOutput, calls=%fused_computation.81 | convolution fusion | flops 16777216 | bytes 4734976 | tf_op jit(solution)/shard_map/rkgh,rmkph->rkgmp/dot_general | solution.py:594
  19.4 3.4 %copy.68 = f32[16,8,128,4]{2,1,3,0:T(8,128)S(1)} copy(f32[16,8,128,4]{1,3,2,0:T(4,128)} %fusion.55) | data formatting | bytes 524288 | tf_op jit(solution)/shard_map/rkgh,rmkph->rkgmp/dot_general | solution.py:594
  22.8 0.1 broadcast_compare_fusion
  22.9 0.2 select_reduce_fusion.1
  23.1 0.1 fusion.63
  23.3 0.3 bitcast_reduce_fusion.1
  23.6 0.2 fusion.31
  23.8 1.3 copy.70
  25.1 0.0 copy-start.2
  25.1 4.3 %fusion.19 = bf16[16,4,128]{2,1,0:T(4,128)(2,1)S(1)} fusion(bf16[16,4,8,128]{2,1,3,0:T(4,128)(2,1)S(1)} %copy.70, bf16[17,8,128,128]{3,1,2,0:T(8,128)(2,1)} %copy-done.1, f32[16,128]{1,0:T(8,128)S(1)} %slice_convert_fusion, f32[16,4]{1,0:T(8,128)S(1)} %get-tuple-element.5), kind=kOutput, calls=%fused_computation.24 | convolution fusion | flops 16801792 | bytes 4350208 | tf_op jit(solution)/shard_map/rkgmp,rmkph->rkgh/dot_general | solution.py:612
  29.4 0.0 copy-start.6
  29.4 0.0 copy-start.13
  29.4 0.0 copy-start.7
  29.5 0.0 copy-done.2
  29.5 1.7 convolution_convert_fusion.x_ref
  31.1 13.1 %shard_map.163 = bf16[16,4096]{1,0:T(8,128)(2,1)} custom-call(bf16[64,4096]{1,0:T(8,128)(2,1)} %convolution_convert_fusion.x_ref), custom_call_target="tpu_custom_call" | custom-call | tf_op jit(solution)/shard_map/pallas_call | solution.py:325
  44.2 0.0 copy-done.5
  44.2 1.1 fusion.26
  45.3 0.0 copy-done.6
  45.3 0.1 copy.77
  45.4 0.1 eq.72
  45.5 0.1 fusion.57
  45.5 0.1 reduce_window_sum.11
  45.6 0.2 select_reduce_fusion.3
  45.8 0.1 reduce_sum.82
  45.9 0.1 copy.78
  46.6 0.0 copy-done.13
  46.7 0.1 select_reduce_fusion.4
  46.8 0.0 copy-done.7
  46.8 1.2 convolution_convert_fusion.1
  48.0 1.0 copy.80.x_ref
  49.1 16.0 %shard_map.164 = bf16[8,6,4096]{2,1,0:T(8,128)(2,1)} custom-call(bf16[8,6,4096]{2,1,0:T(8,128)(2,1)} %copy.80.x_ref), custom_call_target="tpu_custom_call" | custom-call | tf_op jit(solution)/shard_map/pallas_call | solution.py:368
  65.1 1.9 reshape.316.x_ref
  67.0 103.8 %shard_map.165.h_ref = bf16[1536,224]{1,0:T(8,128)(2,1)} custom-call(bf16[48,4096]{1,0:T(8,128)(2,1)} %reshape.316.x_ref, bf16[224,4096]{1,0:T(8,128)(2,1)} %bitcast.138, bf16[224,4096]{1,0:T(8,128)(2,1)} %bitcast.139), custom_call_target="tpu_custom_call" | custom-call | tf_op jit(solution)/shard_map/pallas_call | solution.py:516
  170.8 93.1 %shard_map.166 = bf16[48,4096]{1,0:T(8,128)(2,1)} custom-call(bf16[1536,224]{1,0:T(8,128)(2,1)} %shard_map.165.h_ref, bf16[224,4096]{1,0:T(8,128)(2,1)} %bitcast.140), custom_call_target="tpu_custom_call" | custom-call | tf_op jit(solution)/shard_map/pallas_call | solution.py:547
  263.9 1.9 reshape.317.x_ref
  265.8 26.6 %shard_map.167 = bf16[8,6,4096]{2,1,0:T(8,128)(2,1)} custom-call(bf16[8,6,4096]{2,1,0:T(8,128)(2,1)} %reshape.317.x_ref), custom_call_target="tpu_custom_call" | custom-call | tf_op jit(solution)/shard_map/pallas_call | solution.py:368
  292.4 0.0 copy-done.9
  292.4 1.4 fusion.8
  293.8 0.0 copy-done.3
  293.8 0.7 fusion.29
  (29 shorter events, 0.2 us)
Async XLA Ops:
  0.0 5.7 %copy-start.12 = (s32[17]{0:T(128)S(1)}, s32[17]{0:T(128)}, u32[]{:S(2)}) copy-start(s32[17]{0:T(128)} %param.24) | copy-start | bytes 208
  0.0 7.0 %copy-start.8 = (bf16[64,512]{1,0:T(8,128)(2,1)S(1)}, bf16[64,512]{1,0:T(8,128)(2,1)}, u32[]{:S(2)}) copy-start(bf16[64,512]{1,0:T(8,128)(2,1)} %param.18) | copy-start | bytes 196612
  0.0 7.4 %copy-start.11 = (bf16[64,128]{1,0:T(8,128)(2,1)S(1)}, bf16[64,128]{1,0:T(8,128)(2,1)}, u32[]{:S(2)}) copy-start(bf16[64,128]{1,0:T(8,128)(2,1)} %param.19) | copy-start | bytes 49156
  0.8 7.9 %copy-start.4 = (bf16[40,1,128,128]{3,2,1,0:T(8,128)(2,1)S(1)}, bf16[40,1,128,128]{3,2,1,0:T(8,128)(2,1)}, u32[]{:S(2)}) copy-start(bf16[40,1,128,128]{3,2,1,0:T(8,128)(2,1)} %param.22) | copy-start | bytes 3932164
  3.6 2.1 copy-start
  8.2 4.4 %copy-start.10 = (bf16[64,128]{1,0:T(8,128)(2,1)S(1)}, bf16[64,128]{1,0:T(8,128)(2,1)}, u32[]{:S(2)}) copy-start(bf16[64,128]{1,0:T(8,128)(2,1)} %param.20) | copy-start | bytes 49156
  10.1 2.0 copy-start.1
  25.1 4.4 %copy-start.2 = (bf16[512,4096]{1,0:T(8,128)(2,1)S(1)}, bf16[512,4096]{1,0:T(8,128)(2,1)}, u32[]{:S(2)}) copy-start(bf16[512,4096]{1,0:T(8,128)(2,1)} %param.25) | copy-start | bytes 12582916
  29.4 14.8 %copy-start.5 = (bf16[16,4096]{1,0:T(8,128)(2,1)S(1)}, bf16[16,4096]{1,0:T(8,128)(2,1)}, u32[]{:S(2)}) copy-start(bf16[16,4096]{1,0:T(8,128)(2,1)} %param.17) | copy-start | bytes 393220
  29.4 15.9 %copy-start.6 = (s32[16,2]{0,1:T(2,128)S(1)}, s32[16,2]{0,1:T(2,128)}, u32[]{:S(2)}) copy-start(s32[16,2]{0,1:T(2,128)} %param.27) | copy-start | bytes 388
  29.4 17.2 %copy-start.13 = (s32[8]{0:T(128)S(1)}, s32[8]{0:T(128)}, u32[]{:S(2)}) copy-start(s32[8]{0:T(128)} %param.29) | copy-start | bytes 100
  29.4 17.3 %copy-start.7 = (bf16[4096]{0:T(1024)(128)(2,1)S(1)}, bf16[4096]{0:T(1024)(128)(2,1)}, u32[]{:S(2)}) copy-start(bf16[4096]{0:T(1024)(128)(2,1)} %param.26) | copy-start | bytes 24580
  67.0 225.4 %copy-start.9 = (f32[16,2]{0,1:T(2,128)S(1)}, f32[16,2]{0,1:T(2,128)}, u32[]{:S(2)}) copy-start(f32[16,2]{0,1:T(2,128)} %param.28) | copy-start | bytes 388
  67.0 226.8 %copy-start.3 = (bf16[16,4096]{1,0:T(8,128)(2,1)S(1)}, bf16[16,4096]{1,0:T(8,128)(2,1)}, u32[]{:S(2)}) copy-start(bf16[16,4096]{1,0:T(8,128)(2,1)} %shard_map.163) | copy-start | bytes 393220

commit v14 on v13

--- a/solution.py
+++ b/solution.py
@@ -527,7 +527,7 @@
 
 def moe_sum(hidden, down, n_dp, n_t):
     rows, model_width = hidden.shape[0] // (n_dp * n_t), down.shape[1]
-    widths, order = split_plan(n_dp, n_t, rows, model_width, True)
+    widths, order = split_plan(n_dp, n_t, rows, model_width, True, per_step=1.0)
     scratch = []
     for block in range(4):
         width = widths[block]

time: 295 us -> 295 us (level)
  no operation moved by 1% of the time
where the time goes in v14:
time: 295 us; the launch traced here: 294 us
  Pallas kernels  252 us (85%)
  matrix products  20.5 us (7%)
  local copies, waits for them, and re-layouts  16.1 us (5%)
  other arithmetic  4.31 us (1%)
    pallas_call x1, Pallas kernels, expert_front(): pl.pallas_call(functools.partial(expert_front_kernel, n_dp, n_t, tuple(wi...  104 us
    pallas_call x1, Pallas kernels, moe_sum(): pl.pallas_call(functools.partial(moe_sum_kernel, n_dp, n_t, tuple(widths)...  92.8 us
    pallas_call x2, Pallas kernels, expert_exchange(): pl.pallas_call(functools.partial(expert_exchange_kernel, n_e), out_shape=...  42.3 us
    pallas_call x1, Pallas kernels, head_sum(): pl.pallas_call(functools.partial(head_sum_kernel, n_t), out_shape=jax.Sha...  13.1 us
    dot_general x1, matrix products, attend(): jnp.einsum('rkgh,rmkph->rkgmp', single_q, page_keys[:single_count], prefe...  6.49 us

profile of v14, /device:TPU:1, one launch (start us, length us, event | category | flops | bytes accessed | tf_op | source)
XLA Modules:
  0.0 294.0 jit_solution(6833748425614016855)
XLA Ops:
  0.0 0.0 copy-start.12
  0.0 0.8 copy.66
  0.8 2.8 convolution_convert_fusion.3
  3.6 0.0 copy-start
  3.6 2.1 copy-done
  5.7 0.0 copy-done.12
  5.7 0.6 slice.53
  6.3 0.7 broadcast_compare_fusion.1
  7.0 0.0 copy-done.8
  7.0 0.4 select_reduce_fusion
  7.4 0.0 copy-done.11
  7.4 0.2 select_reduce_fusion.2
  7.6 0.3 bitcast_reduce_fusion
  7.9 0.3 fusion.25
  8.2 0.0 copy-start.10
  8.2 0.5 copy.74
  8.7 0.0 copy-done.4
  8.7 1.4 convolution_convert_fusion.2
  10.1 0.0 copy-start.1
  10.1 2.0 copy-done.1
  12.2 0.4 convolution_bitcast_fusion.2
  12.6 0.0 copy-done.10
  12.6 0.2 fusion.12
  12.9 6.5 %fusion.55 = f32[16,8,128,4]{1,3,2,0:T(4,128)} fusion(bf16[17,8,128,128]{3,1,2,0:T(8,128)(2,1)} %copy-done, bf16[16,4,128,1]{2,1,0,3:T(4,128)(2,1)S(1)} %reshape.320), kind=kOutput, calls=%fused_computation.81 | convolution fusion | flops 16777216 | bytes 4734976 | tf_op jit(solution)/shard_map/rkgh,rmkph->rkgmp/dot_general | solution.py:594
  19.4 3.4 %copy.68 = f32[16,8,128,4]{2,1,3,0:T(8,128)S(1)} copy(f32[16,8,128,4]{1,3,2,0:T(4,128)} %fusion.55) | data formatting | bytes 524288 | tf_op jit(solution)/shard_map/rkgh,rmkph->rkgmp/dot_general | solution.py:594
  22.8 0.1 broadcast_compare_fusion
  22.9 0.2 select_reduce_fusion.1
  23.1 0.1 fusion.63
  23.3 0.3 bitcast_reduce_fusion.1
  23.6 0.2 fusion.31
  23.8 1.3 copy.70
  25.1 0.0 copy-start.2
  25.1 4.3 %fusion.19 = bf16[16,4,128]{2,1,0:T(4,128)(2,1)S(1)} fusion(bf16[16,4,8,128]{2,1,3,0:T(4,128)(2,1)S(1)} %copy.70, bf16[17,8,128,128]{3,1,2,0:T(8,128)(2,1)} %copy-done.1, f32[16,128]{1,0:T(8,128)S(1)} %slice_convert_fusion, f32[16,4]{1,0:T(8,128)S(1)} %get-tuple-element.5), kind=kOutput, calls=%fused_computation.24 | convolution fusion | flops 16801792 | bytes 4350208 | tf_op jit(solution)/shard_map/rkgmp,rmkph->rkgh/dot_general | solution.py:612
  29.4 0.0 copy-start.6
  29.4 0.0 copy-start.13
  29.4 0.0 copy-start.7
  29.5 0.0 copy-done.2
  29.5 1.7 convolution_convert_fusion.x_ref
  31.1 13.1 %shard_map.163 = bf16[16,4096]{1,0:T(8,128)(2,1)} custom-call(bf16[64,4096]{1,0:T(8,128)(2,1)} %convolution_convert_fusion.x_ref), custom_call_target="tpu_custom_call" | custom-call | tf_op jit(solution)/shard_map/pallas_call | solution.py:325
  44.2 0.0 copy-done.5
  44.2 1.1 fusion.26
  45.3 0.0 copy-done.6
  45.3 0.1 copy.77
  45.4 0.1 eq.72
  45.5 0.1 fusion.57
  45.5 0.1 reduce_window_sum.11
  45.6 0.2 select_reduce_fusion.3
  45.8 0.1 reduce_sum.82
  45.9 0.1 copy.78
  46.6 0.0 copy-done.13
  46.7 0.1 select_reduce_fusion.4
  46.8 0.0 copy-done.7
  46.8 1.2 convolution_convert_fusion.1
  48.0 1.0 copy.80.x_ref
  49.1 16.0 %shard_map.164 = bf16[8,6,4096]{2,1,0:T(8,128)(2,1)} custom-call(bf16[8,6,4096]{2,1,0:T(8,128)(2,1)} %copy.80.x_ref), custom_call_target="tpu_custom_call" | custom-call | tf_op jit(solution)/shard_map/pallas_call | solution.py:368
  65.1 1.9 reshape.316.x_ref
  67.0 103.8 %shard_map.165.h_ref = bf16[1536,224]{1,0:T(8,128)(2,1)} custom-call(bf16[48,4096]{1,0:T(8,128)(2,1)} %reshape.316.x_ref, bf16[224,4096]{1,0:T(8,128)(2,1)} %bitcast.138, bf16[224,4096]{1,0:T(8,128)(2,1)} %bitcast.139), custom_call_target="tpu_custom_call" | custom-call | tf_op jit(solution)/shard_map/pallas_call | solution.py:516
  170.8 92.8 %shard_map.166 = bf16[48,4096]{1,0:T(8,128)(2,1)} custom-call(bf16[1536,224]{1,0:T(8,128)(2,1)} %shard_map.165.h_ref, bf16[224,4096]{1,0:T(8,128)(2,1)} %bitcast.140), custom_call_target="tpu_custom_call" | custom-call | tf_op jit(solution)/shard_map/pallas_call | solution.py:547
  263.6 1.9 reshape.317.x_ref
  265.6 26.3 %shard_map.167 = bf16[8,6,4096]{2,1,0:T(8,128)(2,1)} custom-call(bf16[8,6,4096]{2,1,0:T(8,128)(2,1)} %reshape.317.x_ref), custom_call_target="tpu_custom_call" | custom-call | tf_op jit(solution)/shard_map/pallas_call | solution.py:368
  291.9 0.0 copy-done.9
  291.9 1.4 fusion.8
  293.3 0.0 copy-done.3
  293.3 0.7 fusion.29
  (29 shorter events, 0.2 us)
Async XLA Ops:
  0.0 5.7 %copy-start.12 = (s32[17]{0:T(128)S(1)}, s32[17]{0:T(128)}, u32[]{:S(2)}) copy-start(s32[17]{0:T(128)} %param.24) | copy-start | bytes 208
  0.0 7.0 %copy-start.8 = (bf16[64,512]{1,0:T(8,128)(2,1)S(1)}, bf16[64,512]{1,0:T(8,128)(2,1)}, u32[]{:S(2)}) copy-start(bf16[64,512]{1,0:T(8,128)(2,1)} %param.18) | copy-start | bytes 196612
  0.0 7.4 %copy-start.11 = (bf16[64,128]{1,0:T(8,128)(2,1)S(1)}, bf16[64,128]{1,0:T(8,128)(2,1)}, u32[]{:S(2)}) copy-start(bf16[64,128]{1,0:T(8,128)(2,1)} %param.19) | copy-start | bytes 49156
  0.8 7.9 %copy-start.4 = (bf16[40,1,128,128]{3,2,1,0:T(8,128)(2,1)S(1)}, bf16[40,1,128,128]{3,2,1,0:T(8,128)(2,1)}, u32[]{:S(2)}) copy-start(bf16[40,1,128,128]{3,2,1,0:T(8,128)(2,1)} %param.22) | copy-start | bytes 3932164
  3.6 2.1 copy-start
  8.2 4.4 %copy-start.10 = (bf16[64,128]{1,0:T(8,128)(2,1)S(1)}, bf16[64,128]{1,0:T(8,128)(2,1)}, u32[]{:S(2)}) copy-start(bf16[64,128]{1,0:T(8,128)(2,1)} %param.20) | copy-start | bytes 49156
  10.1 2.0 copy-start.1
  25.1 4.4 %copy-start.2 = (bf16[512,4096]{1,0:T(8,128)(2,1)S(1)}, bf16[512,4096]{1,0:T(8,128)(2,1)}, u32[]{:S(2)}) copy-start(bf16[512,4096]{1,0:T(8,128)(2,1)} %param.25) | copy-start | bytes 12582916
  29.4 14.8 %copy-start.5 = (bf16[16,4096]{1,0:T(8,128)(2,1)S(1)}, bf16[16,4096]{1,0:T(8,128)(2,1)}, u32[]{:S(2)}) copy-start(bf16[16,4096]{1,0:T(8,128)(2,1)} %param.17) | copy-start | bytes 393220
  29.4 15.9 %copy-start.6 = (s32[16,2]{0,1:T(2,128)S(1)}, s32[16,2]{0,1:T(2,128)}, u32[]{:S(2)}) copy-start(s32[16,2]{0,1:T(2,128)} %param.27) | copy-start | bytes 388
  29.4 17.2 %copy-start.13 = (s32[8]{0:T(128)S(1)}, s32[8]{0:T(128)}, u32[]{:S(2)}) copy-start(s32[8]{0:T(128)} %param.29) | copy-start | bytes 100
  29.4 17.3 %copy-start.7 = (bf16[4096]{0:T(1024)(128)(2,1)S(1)}, bf16[4096]{0:T(1024)(128)(2,1)}, u32[]{:S(2)}) copy-start(bf16[4096]{0:T(1024)(128)(2,1)} %param.26) | copy-start | bytes 24580
  67.0 224.9 %copy-start.9 = (f32[16,2]{0,1:T(2,128)S(1)}, f32[16,2]{0,1:T(2,128)}, u32[]{:S(2)}) copy-start(f32[16,2]{0,1:T(2,128)} %param.28) | copy-start | bytes 388
  67.0 226.3 %copy-start.3 = (bf16[16,4096]{1,0:T(8,128)(2,1)S(1)}, bf16[16,4096]{1,0:T(8,128)(2,1)}, u32[]{:S(2)}) copy-start(bf16[16,4096]{1,0:T(8,128)(2,1)} %shard_map.163) | copy-start | bytes 393220
